TPU v7x, 512 devices: a whole 4x8x8 slice. The times are simulated.
512 devices in a mesh: row: 16 (over x, z_lo), col: 32 (over y, z_hi, core).
Axes of the slice: x: 4, y: 8, z: 8 (z_hi: 2, z_lo: 4; z = z_hi * 4 + z_lo), core: 2. Of those that a mesh axis runs over, the one named last changes fastest.
Arguments:
- covariance: float32 [16384, 16384], P('row', 'col'), may hold values from -7 to 14, as said below
- wind_mask: int32 [2, 16384], replicated, may hold values 0 or 1
- wind_speed: float32 [2, 16384], replicated, may hold values from 0.02 to 0.3
- obs_cells: int32 [256, 128], replicated, may hold values from 0 to 16383
- obs_scale: float32 [256], replicated, may hold values from 0.05 to 0.2
- gain: bfloat16 [16384, 256], P('row'), may hold values from -0.375 to 0.375
Outputs:
- updated: float32 [16384, 16384], P('row', 'col')
Inputs may be any that keep to these rules, and one draw needn't show every extreme that they name: A covariance window.
All inputs are finite; a program needn't handle non-finite values.
Results may differ from a plain program's by a relative error of at most 0.0003.
Values sent between devices are 32-bit elements; how exact they have to be, the bound alone decides.
No kernel may reach another device: no remote copies, remote signals or barrier semaphores. Data moves between devices by JAX's collectives and lax.ppermute only.
A program may use at most 64 MiB of HBM per device.

v0:
```python
import jax
import jax.numpy as jnp
from jax import lax
from jax.experimental import pallas as pl
from jax.experimental.pallas import tpu as pltpu
from jax.sharding import PartitionSpec as P


MAPX = 256


diffusion = 0.05
HIGH = lax.Precision.HIGHEST


def coefficients(wind_mask, wind_speed):
    cell_total = wind_speed.shape[1]
    cells = jnp.arange(cell_total, dtype=jnp.int32)
    map_column = cells % MAPX
    map_row = cells // MAPX
    last_row = cell_total // MAPX - 1
    speed_x = wind_speed[0]
    speed_y = wind_speed[1]
    sign_x = wind_mask[0].astype(jnp.float32)
    sign_y = wind_mask[1].astype(jnp.float32)
    middle = 1.0 - speed_x - speed_y - 4.0 * diffusion
    western = jnp.where(map_column > 0, speed_x * sign_x + diffusion, 0.0)
    eastern = jnp.where(map_column < MAPX - 1, speed_x * (1.0 - sign_x) + diffusion, 0.0)
    northern = jnp.where(map_row > 0, speed_y * sign_y + diffusion, 0.0)
    southern = jnp.where(map_row < last_row, speed_y * (1.0 - sign_y) + diffusion, 0.0)
    return jnp.stack([middle, western, eastern, northern, southern])


def after(value, *earlier):
    return lax.optimization_barrier((value,) + earlier)[0]


def along(array, start, size, dim):
    return lax.slice_in_dim(array, start, start + size, axis=dim)


def transposed(select, weights):
    length = select.shape[1] - 2 * MAPX

    def term(k, offset):
        return along(weights, offset, length, 1)[k] * along(select, offset, length, 1)

    result = term(0, MAPX) + term(1, MAPX + 1) + term(2, MAPX - 1)
    return result + term(3, 2 * MAPX) + term(4, 0)


def step_cols(before, here, behind, weights):
    width = here.shape[1]
    result = weights[0] * here + weights[1] * pltpu.roll(here, 1, 1)
    result = result + weights[2] * pltpu.roll(here, width - 1, 1)
    return result + weights[3] * before + weights[4] * behind


def cols_kernel(core_ref, here_ref, near_ref, far_ref, weights_ref, out_ref):
    first = core_ref[0] == 0
    near, far = near_ref[...], far_ref[...]
    west = jnp.where(first, far, near)
    east = jnp.where(first, near, far)
    here = here_ref[...]
    maps = [piece[:, MAPX * k : MAPX * (k + 1)] for piece in (west, here, east) for k in range(2)]

    def weights(m):
        return [weights_ref[k : k + 1, MAPX * m : MAPX * (m + 1)] for k in range(5)]

    once = [step_cols(maps[m], maps[m + 1], maps[m + 2], weights(m)) for m in range(4)]
    for m in range(2):
        out_ref[:, MAPX * m : MAPX * (m + 1)] = step_cols(
            once[m], once[m + 1], once[m + 2], weights(m + 1)
        )


def move_cols(core, here, here_at, near, near_at, far, weights, rows):
    cols = here.shape[1]
    tile = min(rows, 32)
    steps = rows // tile
    return pl.pallas_call(
        cols_kernel,
        out_shape=jax.ShapeDtypeStruct((rows, cols), jnp.float32),
        grid_spec=pltpu.PrefetchScalarGridSpec(
            num_scalar_prefetch=1,
            grid=(steps,),
            in_specs=[
                pl.BlockSpec((tile, cols), lambda s, c: (here_at * steps + s, 0)),
                pl.BlockSpec((tile, cols), lambda s, c: (near_at * steps + s, 0)),
                pl.BlockSpec((tile, cols), lambda s, c: (s, 0)),
                pl.BlockSpec(weights.shape, lambda s, c: (0, 0)),
            ],
            out_specs=pl.BlockSpec((tile, cols), lambda s, c: (s, 0)),
        ),
        cost_estimate=pl.CostEstimate(
            flops=27 * rows * cols, bytes_accessed=16 * rows * cols, transcendentals=0
        ),
        name="move_cols",
    )(core, here, near, far, weights)


def step_rows(before, here, behind, weights):
    height = here.shape[0]
    result = weights[:, 0:1] * here + weights[:, 1:2] * pltpu.roll(here, 1, 0)
    result = result + weights[:, 2:3] * pltpu.roll(here, height - 1, 0)
    if before is not None:
        result = result + weights[:, 3:4] * before
    return result + weights[:, 4:5] * behind


def rows_kernel(*refs):
    maps, update_ref, weights_ref, out_ref, once_ref = refs[:7], *refs[7:]
    for m in range(6):
        once_ref[MAPX * m : MAPX * (m + 1)] = step_rows(
            maps[m - 1][...] if m > 0 else None,
            maps[m][...],
            maps[m + 1][...],
            weights_ref[MAPX * m : MAPX * (m + 1)],
        )
    for m in range(1, 5):
        out_ref[MAPX * (m - 1) : MAPX * m] = (
            step_rows(
                once_ref[MAPX * (m - 1) : MAPX * m],
                once_ref[MAPX * m : MAPX * (m + 1)],
                once_ref[MAPX * (m + 1) : MAPX * (m + 2)],
                weights_ref[MAPX * m : MAPX * (m + 1)],
            )
            - update_ref[MAPX * (m - 1) : MAPX * m]
        )


def move_rows(maps, update, weights):
    rows, cols = update.shape
    tile = 128
    one = pl.BlockSpec((MAPX, tile), lambda s: (0, s))
    whole = pl.BlockSpec((rows, tile), lambda s: (0, s))
    return pl.pallas_call(
        rows_kernel,
        out_shape=jax.ShapeDtypeStruct((rows, cols), jnp.float32),
        grid=(cols // tile,),
        in_specs=[one] * 7 + [whole, pl.BlockSpec(weights.shape, lambda s: (0, 0))],
        out_specs=whole,
        scratch_shapes=[pltpu.VMEM((rows + 2 * MAPX, tile), jnp.float32)],
        cost_estimate=pl.CostEstimate(
            flops=24 * rows * cols, bytes_accessed=16 * rows * cols, transcendentals=0
        ),
        name="move_rows",
    )(*maps, update, weights)


def last_kernel(result_ref, halo_ref, weights_ref, before_ref, out_ref):
    factor = weights_ref[:, 3:4] * before_ref[:, 3:4]
    out_ref[...] = result_ref[...] + factor * halo_ref[...]


def add_last(result, halo, weights):
    cols = result.shape[1]
    tile = 128
    steps = MAPX // tile
    block = pl.BlockSpec((tile, cols), lambda s: (s, 0))
    return pl.pallas_call(
        last_kernel,
        out_shape=jax.ShapeDtypeStruct(result.shape, result.dtype),
        grid=(steps,),
        in_specs=[
            block,
            block,
            pl.BlockSpec((tile, weights.shape[1]), lambda s: (steps + s, 0)),
            pl.BlockSpec((tile, weights.shape[1]), lambda s: (s, 0)),
        ],
        out_specs=block,
        input_output_aliases={0: 0},
        cost_estimate=pl.CostEstimate(
            flops=2 * MAPX * cols, bytes_accessed=12 * MAPX * cols, transcendentals=0
        ),
        name="add_last",
    )(result, halo, weights, weights)


def local(covariance, wind_mask, wind_speed, obs_cells, obs_scale, gain):
    rows, cols = covariance.shape
    reach = 2 * MAPX
    row_parts = lax.axis_size("row")
    col_parts = lax.axis_size("col")
    row_at = lax.axis_index("row")
    col_at = lax.axis_index("col")
    down = [(i, i + 1) for i in range(row_parts - 1)]
    up = [(i + 1, i) for i in range(row_parts - 1)]
    near_swap = [(j, j ^ 1) for j in range(col_parts)]
    far_swap = [(j, (j - 1 ^ 1) + 1) for j in range(1, col_parts - 1)]
    core = (col_at % 2).reshape(1)

    def group(n):
        return along(covariance, MAPX * n, MAPX, 0)

    far = {n: lax.ppermute(group(n), "col", far_swap) for n in (0, 3)}
    near = lax.ppermute(covariance, "col", near_swap)

    table = coefficients(wind_mask, wind_speed)
    table = jnp.pad(table, ((0, 0), (reach, reach)))
    row_weights = lax.dynamic_slice_in_dim(table, row_at * rows, rows + 2 * reach, 1)
    col_weights = lax.dynamic_slice_in_dim(table, col_at * cols + MAPX, cols + 2 * MAPX, 1)
    down_weights = along(row_weights, MAPX, rows + 2 * MAPX, 1).T

    pieces = row_parts
    obs_count, foot = obs_cells.shape
    each = obs_count // pieces
    order = jnp.arange(pieces, dtype=jnp.int32) ^ row_at
    cells = obs_cells.reshape(pieces, each, foot)[order].reshape(obs_count, foot)
    scale = obs_scale.reshape(pieces, each)[order].reshape(obs_count)
    window = rows + 2 * reach
    lane = 128
    place = cells - (row_at * rows - reach)
    block_hit = (place[:, None, :] >> 7) == jnp.arange(window // lane, dtype=jnp.int32)[None, :, None]
    lane_hit = (place[:, :, None] & (lane - 1)) == jnp.arange(lane, dtype=jnp.int32)[None, None, :]
    counts = jnp.einsum(
        "obm,oml->obl",
        block_hit.astype(jnp.bfloat16),
        lane_hit.astype(jnp.bfloat16),
        preferred_element_type=jnp.float32,
    ).reshape(obs_count, window)
    select = transposed(counts * scale[:, None], row_weights)
    select = transposed(select, along(row_weights, MAPX, rows + 2 * MAPX, 1))
    part = jnp.dot(select, covariance, precision=HIGH, preferred_element_type=jnp.float32)

    def move_group(n, *earlier):
        return move_cols(core, covariance, n, near, n, after(far[n], *earlier), col_weights, MAPX)

    def across(bit):
        return [(i, i ^ bit) for i in range(row_parts)]

    bits = [8, 4, 2, 1]
    assert row_parts == 16

    moved, halo = {}, {}
    moved[0] = move_group(0, part)
    halo[0] = lax.ppermute(moved[0], "row", up)
    far[1] = lax.ppermute(after(group(1), moved[0]), "col", far_swap)

    total = after(part, moved[0])
    for bit in bits:
        half = total.shape[0] // 2
        total = total[:half] + lax.ppermute(total[half:], "row", across(bit))

    moved[3] = move_group(3, total)
    halo[3] = lax.ppermute(moved[3], "row", down)
    far[2] = lax.ppermute(after(group(2), moved[3]), "col", far_swap)

    total = after(total, moved[3])
    piece_far = lax.ppermute(total, "col", far_swap)
    piece_near = lax.ppermute(total, "col", near_swap)
    observed = move_cols(core, total, 0, piece_near, 0, piece_far, col_weights, each)
    for bit in bits[:1:-1]:
        observed = jnp.concatenate([observed, lax.ppermute(observed, "row", across(bit))])

    moved[1] = move_group(1, observed)
    halo[1] = lax.ppermute(moved[1], "row", up)

    observed = after(observed, moved[1])
    for bit in bits[1::-1]:
        observed = jnp.concatenate([observed, lax.ppermute(observed, "row", across(bit))])
    index = jnp.arange(obs_count, dtype=jnp.int32)
    reorder = (index[:, None] ^ (row_at * each)) == index[None, :]
    ordered_gain = jnp.dot(gain, reorder.astype(gain.dtype), preferred_element_type=jnp.float32)
    update = jnp.dot(ordered_gain, observed, precision=HIGH, preferred_element_type=jnp.float32)

    moved[2] = move_group(2, update)
    halo[2] = lax.ppermute(moved[2], "row", down)

    maps = [halo[3], moved[0], moved[1], moved[2], moved[3], halo[0], halo[1]]
    result = move_rows(maps, update, down_weights)
    return add_last(result, halo[2], down_weights)


def solution(mesh):
    placed = (P("row", "col"), P(), P(), P(), P(), P("row", None))
    return jax.shard_map(
        local, mesh=mesh, in_specs=placed, out_specs=P("row", "col"), check_vma=False
    )
```

profile of v0, /device:TPU:93, one launch (start us, length us, event | category | flops | bytes accessed | tf_op | source)
XLA Modules:
  0.0 253.7 jit_solution(15596812613037070784)
XLA Ops:
  5.4 9.6 %collective-permute-start.2 = (f32[256,512]{1,0:T(8,128)}, f32[256,512]{1,0:T(8,128)}, u32[]{:S(2)}, u32[]{:S(2)}) collective-permute-start(f32[256,512]{1,0:T(8,128)} %get-tuple-element.35), channel_id=1, source_target_pairs={{1,2},{2,1},{3,4},{4,3},{5,6},{6,5},{7,8},{8,7},{9,10},{10,9},{11,... | collective-permute-start | bytes 1572872 | tf_op jit(solution)/shard_map/ppermute | solution.py:196
  16.1 5.3 %copy.54 = f32[5,16384]{0,1:T(8,128)} copy(f32[5,16384]{1,0:T(8,128)S(1)} %stack.2) | data formatting | bytes 655360 | tf_op jit(solution)/shard_map/stack | solution.py:31
  22.7 4.8 %fusion.17 = (f32[1536]{0:T(1024)S(1)}, f32[1536]{0:T(1024)S(1)}, f32[1536]{0:T(1024)S(1)}, f32[1536]{0:T(1024)S(1)}, f32[1536]{0:T(1024)S(1)}) fusion(s32[]{:T(128)S(6)} %add.147, f32[5,16384]{0,1:T(8,128)} %copy.54, s32[]{:T(128)S(6)} %add.148, s32[]{:T(128)S(6)} %add.149, s32[]{:T(128)S(6)} %add.150, s32[]{:T(128)S(6)} %add.151, s32[]{:T(128)S(6)} %add.152, ...), kind=kLoop, calls=%fused_computation.40 | loop fusion | bytes 358436 | tf_op jit(solution)/shard_map/slice | solution.py:46
  27.6 10.3 %fusion = f32[256,16,128]{2,1,0:T(8,128)S(1)} fusion(s32[256,128]{1,0:T(8,128)S(1)} %bitcast.17, s32[256,128]{1,0:T(8,128)S(1)} %bitcast.16), kind=kOutput, calls=%fused_computation.3 | convolution fusion | flops 138936320 | bytes 2359296 | tf_op jit(solution)/shard_map/obm,oml->obl/dot_general | solution.py:216
  41.9 3.7 %fusion.33 = (f32[1024]{0:T(1024)S(1)}, f32[1024]{0:T(1024)S(1)}, f32[1024]{0:T(1024)S(1)}, f32[1024]{0:T(1024)S(1)}, f32[1024]{0:T(1024)S(1)}) fusion(s32[]{:T(128)S(6)} %add.146, f32[5,16384]{0,1:T(8,128)} %copy.54, s32[]{:T(128)S(6)} %add.148, s32[]{:T(128)S(6)} %add.156, s32[]{:T(128)S(6)} %add.150, s32[]{:T(128)S(6)} %add.158, s32[]{:T(128)S(6)} %add.152, ...), kind=kLoop, calls=%fused_computation.56 | loop fusion | bytes 348196 | tf_op jit(solution)/shard_map/slice | solution.py:46
  48.0 5.9 %move_cols.5.refs_1_ = f32[256,512]{1,0:T(8,128)} custom-call(s32[1]{0:T(128)} %bitcast.core_ref, f32[1024,512]{1,0:T(8,128)} %here_ref.7, f32[1024,512]{1,0:T(8,128)} %collective-permute-done.near_ref, f32[256,512]{1,0:T(8,128)} %collective-permute-done.2.far_ref, f32[5,1024]{1,0:T(8,128)} %copy.55.weights_ref), custom_call_target="tpu_custom_call" | custom-call | flops 3538944 | bytes 2097152 | tf_op jit(solution)/shard_map/move_cols/pallas_call | solution.py:81
  56.5 8.4 %collective-permute-done.3 = f32[128,512]{1,0:T(8,128)S(1)} collective-permute-done((f32[128,512]{1,0:T(8,128)S(1)}, f32[128,512]{1,0:T(8,128)S(1)}, u32[]{:S(2)}, u32[]{:S(2)}) %collective-permute-start.3) | collective-permute-done | bytes 262176 | tf_op jit(solution)/shard_map/ppermute | solution.py:243
  70.8 4.1 %collective-permute-start.5 = (f32[32,512]{1,0:T(8,128)S(1)}, f32[32,512]{1,0:T(8,128)S(1)}, u32[]{:S(2)}, u32[]{:S(2)}) collective-permute-start(f32[32,512]{1,0:T(8,128)S(1)} %slice.191), channel_id=1, source_target_pairs={{0,64},{32,96},{64,0},{96,32},{128,192},{160,224},{192,128},{224,1... | collective-permute-start | bytes 196616 | tf_op jit(solution)/shard_map/ppermute | solution.py:243
  74.9 5.3 %collective-permute-start.1 = (f32[256,512]{1,0:T(8,128)S(1)}, f32[256,512]{1,0:T(8,128)S(1)}, u32[]{:S(2)}, u32[]{:S(2)}) collective-permute-start(f32[256,512]{1,0:T(8,128)S(1)} %copy-done.7), channel_id=1, source_target_pairs={{1,2},{2,1},{3,4},{4,3},{5,6},{6,5},{7,8},{8,7},{9,10},{10,9},{11,... | collective-permute-start | bytes 1572872 | tf_op jit(solution)/shard_map/ppermute | solution.py:196
  82.5 4.4 %collective-permute-start.8 = (f32[256,512]{1,0:T(8,128)S(1)}, f32[256,512]{1,0:T(8,128)S(1)}, u32[]{:S(2)}, u32[]{:S(2)}) collective-permute-start(f32[256,512]{1,0:T(8,128)S(1)} %get-tuple-element.17), channel_id=1, source_target_pairs={{1,2},{2,1},{3,4},{4,3},{5,6},{6,5},{7,8},{8,7},{9,10},{10,9},{11,... | collective-permute-start | bytes 1572872 | tf_op jit(solution)/shard_map/ppermute | solution.py:238
  87.0 36.4 %collective-permute-done.6 = f32[16,512]{1,0:T(8,128)S(1)} collective-permute-done((f32[16,512]{1,0:T(8,128)S(1)}, f32[16,512]{1,0:T(8,128)S(1)}, u32[]{:S(2)}, u32[]{:S(2)}) %collective-permute-start.6) | collective-permute-done | bytes 32800 | tf_op jit(solution)/shard_map/ppermute | solution.py:243
  124.2 5.9 %move_cols.6.refs_4_ = f32[256,512]{1,0:T(8,128)} custom-call(s32[1]{0:T(128)} %bitcast.core_ref, f32[1024,512]{1,0:T(8,128)} %here_ref.7, f32[1024,512]{1,0:T(8,128)} %collective-permute-done.near_ref, f32[256,512]{1,0:T(8,128)} %copy-done.9, f32[5,1024]{1,0:T(8,128)} %copy.55.weights_ref), custom_call_target="tpu_custom_call" | custom-call | flops 3538944 | bytes 2097152 | tf_op jit(solution)/shard_map/move_cols/pallas_call | solution.py:81
  135.2 4.1 %collective-permute-done.10.far_ref = f32[16,512]{1,0:T(8,128)S(1)} collective-permute-done((f32[16,512]{1,0:T(8,128)S(1)}, f32[16,512]{1,0:T(8,128)S(1)}, u32[]{:S(2)}, u32[]{:S(2)}) %collective-permute-start.10) | collective-permute-done | bytes 32800 | tf_op jit(solution)/shard_map/ppermute | solution.py:250
  149.7 4.1 %collective-permute-done.12 = f32[32,512]{1,0:T(8,128)S(1)} collective-permute-done((f32[32,512]{1,0:T(8,128)S(1)}, f32[32,512]{1,0:T(8,128)S(1)}, u32[]{:S(2)}, u32[]{:S(2)}) %collective-permute-start.12) | collective-permute-done | bytes 65568 | tf_op jit(solution)/shard_map/ppermute | solution.py:254
  155.3 5.9 %move_cols.8.refs_2_ = f32[256,512]{1,0:T(8,128)} custom-call(s32[1]{0:T(128)} %bitcast.core_ref, f32[1024,512]{1,0:T(8,128)} %here_ref.7, f32[1024,512]{1,0:T(8,128)} %collective-permute-done.near_ref, f32[256,512]{1,0:T(8,128)} %copy-done.8, f32[5,1024]{1,0:T(8,128)} %copy.55.weights_ref), custom_call_target="tpu_custom_call" | custom-call | flops 3538944 | bytes 2097152 | tf_op jit(solution)/shard_map/move_cols/pallas_call | solution.py:81
  161.2 3.2 %collective-permute-start.14 = (f32[64,512]{1,0:T(8,128)S(1)}, f32[64,512]{1,0:T(8,128)S(1)}, u32[]{:S(2)}, u32[]{:S(2)}) collective-permute-start(f32[64,512]{1,0:T(8,128)S(1)} %pad_maximum_fusion.1), channel_id=1, source_target_pairs={{0,128},{32,160},{64,192},{96,224},{128,0},{160,32},{192,64},{224,... | collective-permute-start | bytes 393224 | tf_op jit(solution)/shard_map/ppermute | solution.py:261
  164.5 8.2 %collective-permute-start.13 = (f32[256,512]{1,0:T(8,128)}, f32[256,512]{1,0:T(8,128)}, u32[]{:S(2)}, u32[]{:S(2)}) collective-permute-start(f32[256,512]{1,0:T(8,128)} %get-tuple-element.20), channel_id=1, source_target_pairs={{1,2},{2,1},{3,4},{4,3},{5,6},{6,5},{7,8},{8,7},{9,10},{10,9},{11,... | collective-permute-start | bytes 1572872 | tf_op jit(solution)/shard_map/ppermute | solution.py:247
  175.1 3.8 %collective-permute-start.16 = (f32[256,512]{1,0:T(8,128)S(1)}, f32[256,512]{1,0:T(8,128)S(1)}, u32[]{:S(2)}, u32[]{:S(2)}) collective-permute-start(f32[256,512]{1,0:T(8,128)S(1)} %copy-done.2), channel_id=1, source_target_pairs={{32,0},{64,32},{96,64},{128,96},{160,128},{192,160},{224,192},{256... | collective-permute-start | bytes 1572872 | tf_op jit(solution)/shard_map/ppermute | solution.py:237
  180.8 3.4 %collective-permute-start.17 = (f32[256,512]{1,0:T(8,128)S(1)}, f32[256,512]{1,0:T(8,128)}, u32[]{:S(2)}, u32[]{:S(2)}) collective-permute-start(f32[256,512]{1,0:T(8,128)S(1)} %copy-done.4), channel_id=1, source_target_pairs={{32,0},{64,32},{96,64},{128,96},{160,128},{192,160},{224,192},{256... | collective-permute-start | bytes 1572872 | tf_op jit(solution)/shard_map/ppermute | solution.py:257
  187.4 14.8 %collective-permute-done.13.far_ref = f32[256,512]{1,0:T(8,128)} collective-permute-done((f32[256,512]{1,0:T(8,128)}, f32[256,512]{1,0:T(8,128)}, u32[]{:S(2)}, u32[]{:S(2)}) %collective-permute-start.13) | collective-permute-done | bytes 524320 | tf_op jit(solution)/shard_map/ppermute | solution.py:247
  202.1 5.9 %move_cols.9.refs_3_ = f32[256,512]{1,0:T(8,128)} custom-call(s32[1]{0:T(128)} %bitcast.core_ref, f32[1024,512]{1,0:T(8,128)} %here_ref.7, f32[1024,512]{1,0:T(8,128)} %collective-permute-done.near_ref, f32[256,512]{1,0:T(8,128)} %collective-permute-done.13.far_ref, f32[5,1024]{1,0:T(8,128)} %copy.55.weights_ref), custom_call_target="tpu_custom_call" | custom-call | flops 3538944 | bytes 2097152 | tf_op jit(solution)/shard_map/move_cols/pallas_call | solution.py:81
  208.0 14.9 %collective-permute-start.18 = (f32[256,512]{1,0:T(8,128)}, f32[256,512]{1,0:T(8,128)}, u32[]{:S(2)}, u32[]{:S(2)}) collective-permute-start(f32[256,512]{1,0:T(8,128)} %move_cols.9.refs_3_), channel_id=1, source_target_pairs={{0,32},{32,64},{64,96},{96,128},{128,160},{160,192},{192,224},{224... | collective-permute-start | bytes 1572872 | tf_op jit(solution)/shard_map/ppermute | solution.py:268
  225.3 15.3 %collective-permute-done.17.refs_6_ = f32[256,512]{1,0:T(8,128)} collective-permute-done((f32[256,512]{1,0:T(8,128)S(1)}, f32[256,512]{1,0:T(8,128)}, u32[]{:S(2)}, u32[]{:S(2)}) %collective-permute-start.17) | collective-permute-done | bytes 524320 | tf_op jit(solution)/shard_map/ppermute | solution.py:257
  240.6 11.1 %move_rows.1.result_ref = f32[1024,512]{1,0:T(8,128)} custom-call(f32[256,512]{1,0:T(8,128)} %copy-done.6, f32[256,512]{1,0:T(8,128)} %move_cols.5.refs_1_, f32[256,512]{1,0:T(8,128)} %move_cols.8.refs_2_, f32[256,512]{1,0:T(8,128)} %move_cols.9.refs_3_, f32[256,512]{1,0:T(8,128)} %move_cols.6.refs_4_, f32[256,512]{1,0:T(8,128)} %copy-done.5, ...), custom_call_target="tpu_custom_call" | custom-call | flops 12582912 | bytes 8388608 | tf_op jit(solution)/shard_map/move_rows/pallas_call | solution.py:137
  (89 shorter events, 54.3 us)
Async XLA Ops:
  0.0 174.7 %copy-start = (bf16[1024,256]{1,0:T(8,128)(2,1)S(1)}, bf16[1024,256]{1,0:T(8,128)(2,1)}, u32[]{:S(2)}) copy-start(bf16[1024,256]{1,0:T(8,128)(2,1)} %param.11) | copy-start | bytes 1572868
  0.0 48.0 %collective-permute-start = (f32[1024,512]{1,0:T(8,128)}, f32[1024,512]{1,0:T(8,128)}, u32[]{:S(2)}, u32[]{:S(2)}) collective-permute-start(f32[1024,512]{1,0:T(8,128)} %here_ref.7), channel_id=1, source_target_pairs={{0,1},{1,0},{2,3},{3,2},{4,5},{5,4},{6,7},{7,6},{8,9},{9,8},{10,11... | collective-permute-start | bytes 6291464 | tf_op jit(solution)/shard_map/ppermute | solution.py:197
  5.4 42.6 %collective-permute-start.2 = (f32[256,512]{1,0:T(8,128)}, f32[256,512]{1,0:T(8,128)}, u32[]{:S(2)}, u32[]{:S(2)}) collective-permute-start(f32[256,512]{1,0:T(8,128)} %get-tuple-element.35), channel_id=1, source_target_pairs={{1,2},{2,1},{3,4},{4,3},{5,6},{6,5},{7,8},{8,7},{9,10},{10,9},{11,... | collective-permute-start | bytes 1572872 | tf_op jit(solution)/shard_map/ppermute | solution.py:196
  53.9 21.0 %copy-start.7 = (f32[256,512]{1,0:T(8,128)S(1)}, f32[256,512]{1,0:T(8,128)}, u32[]{:S(2)}) copy-start(f32[256,512]{1,0:T(8,128)} %get-tuple-element.36) | copy-start | bytes 1572868
  54.0 11.0 %collective-permute-start.3 = (f32[128,512]{1,0:T(8,128)S(1)}, f32[128,512]{1,0:T(8,128)S(1)}, u32[]{:S(2)}, u32[]{:S(2)}) collective-permute-start(f32[128,512]{1,0:T(8,128)S(1)} %slice.164), channel_id=1, source_target_pairs={{0,256},{32,288},{64,320},{96,352},{128,384},{160,416},{192,448},{... | collective-permute-start | bytes 786440 | tf_op jit(solution)/shard_map/ppermute | solution.py:243
  65.0 5.7 %collective-permute-start.4 = (f32[64,512]{1,0:T(8,128)S(1)}, f32[64,512]{1,0:T(8,128)S(1)}, u32[]{:S(2)}, u32[]{:S(2)}) collective-permute-start(f32[64,512]{1,0:T(8,128)S(1)} %slice.189), channel_id=1, source_target_pairs={{0,128},{32,160},{64,192},{96,224},{128,0},{160,32},{192,64},{224,... | collective-permute-start | bytes 393224 | tf_op jit(solution)/shard_map/ppermute | solution.py:243
  70.8 9.5 %collective-permute-start.5 = (f32[32,512]{1,0:T(8,128)S(1)}, f32[32,512]{1,0:T(8,128)S(1)}, u32[]{:S(2)}, u32[]{:S(2)}) collective-permute-start(f32[32,512]{1,0:T(8,128)S(1)} %slice.191), channel_id=1, source_target_pairs={{0,64},{32,96},{64,0},{96,32},{128,192},{160,224},{192,128},{224,1... | collective-permute-start | bytes 196616 | tf_op jit(solution)/shard_map/ppermute | solution.py:243
  74.9 48.5 %collective-permute-start.1 = (f32[256,512]{1,0:T(8,128)S(1)}, f32[256,512]{1,0:T(8,128)S(1)}, u32[]{:S(2)}, u32[]{:S(2)}) collective-permute-start(f32[256,512]{1,0:T(8,128)S(1)} %copy-done.7), channel_id=1, source_target_pairs={{1,2},{2,1},{3,4},{4,3},{5,6},{6,5},{7,8},{8,7},{9,10},{10,9},{11,... | collective-permute-start | bytes 1572872 | tf_op jit(solution)/shard_map/ppermute | solution.py:196
  80.3 43.1 %collective-permute-start.6 = (f32[16,512]{1,0:T(8,128)S(1)}, f32[16,512]{1,0:T(8,128)S(1)}, u32[]{:S(2)}, u32[]{:S(2)}) collective-permute-start(f32[16,512]{1,0:T(8,128)S(1)} %slice.193), channel_id=1, source_target_pairs={{0,32},{32,0},{64,96},{96,64},{128,160},{160,128},{192,224},{224,1... | collective-permute-start | bytes 98312 | tf_op jit(solution)/shard_map/ppermute | solution.py:243
  82.5 72.0 %collective-permute-start.8 = (f32[256,512]{1,0:T(8,128)S(1)}, f32[256,512]{1,0:T(8,128)S(1)}, u32[]{:S(2)}, u32[]{:S(2)}) collective-permute-start(f32[256,512]{1,0:T(8,128)S(1)} %get-tuple-element.17), channel_id=1, source_target_pairs={{1,2},{2,1},{3,4},{4,3},{5,6},{6,5},{7,8},{8,7},{9,10},{10,9},{11,... | collective-permute-start | bytes 1572872 | tf_op jit(solution)/shard_map/ppermute | solution.py:238
  123.4 16.0 %copy-start.10 = (f32[16,512]{1,0:T(8,128)}, f32[16,512]{1,0:T(8,128)S(1)}, u32[]{:S(2)}) copy-start(f32[16,512]{1,0:T(8,128)S(1)} %slice_add_fusion.3.here_ref) | copy-start | bytes 98308
  130.1 9.2 %collective-permute-start.10 = (f32[16,512]{1,0:T(8,128)S(1)}, f32[16,512]{1,0:T(8,128)S(1)}, u32[]{:S(2)}, u32[]{:S(2)}) collective-permute-start(f32[16,512]{1,0:T(8,128)S(1)} %slice_add_fusion.3.here_ref), channel_id=1, source_target_pairs={{1,2},{2,1},{3,4},{4,3},{5,6},{6,5},{7,8},{8,7},{9,10},{10,9},{11,... | collective-permute-start | bytes 98312 | tf_op jit(solution)/shard_map/ppermute | solution.py:250
  133.3 6.1 %collective-permute-start.9 = (f32[16,512]{1,0:T(8,128)S(1)}, f32[16,512]{1,0:T(8,128)S(1)}, u32[]{:S(2)}, u32[]{:S(2)}) collective-permute-start(f32[16,512]{1,0:T(8,128)S(1)} %slice_add_fusion.3.here_ref), channel_id=1, source_target_pairs={{0,1},{1,0},{2,3},{3,2},{4,5},{5,4},{6,7},{7,6},{8,9},{9,8},{10,11... | collective-permute-start | bytes 98312 | tf_op jit(solution)/shard_map/ppermute | solution.py:251
  142.1 4.9 %collective-permute-start.11 = (f32[16,512]{1,0:T(8,128)}, f32[16,512]{1,0:T(8,128)S(1)}, u32[]{:S(2)}, u32[]{:S(2)}) collective-permute-start(f32[16,512]{1,0:T(8,128)} %move_cols.7), channel_id=1, source_target_pairs={{0,32},{32,0},{64,96},{96,64},{128,160},{160,128},{192,224},{224,1... | collective-permute-start | bytes 98312 | tf_op jit(solution)/shard_map/ppermute | solution.py:254
  147.7 6.0 %collective-permute-start.12 = (f32[32,512]{1,0:T(8,128)S(1)}, f32[32,512]{1,0:T(8,128)S(1)}, u32[]{:S(2)}, u32[]{:S(2)}) collective-permute-start(f32[32,512]{1,0:T(8,128)S(1)} %pad_maximum_fusion.2), channel_id=1, source_target_pairs={{0,64},{32,96},{64,0},{96,32},{128,192},{160,224},{192,128},{224,1... | collective-permute-start | bytes 196616 | tf_op jit(solution)/shard_map/ppermute | solution.py:254
  161.2 17.7 %copy-start.3 = (f32[256,512]{1,0:T(8,128)S(1)}, f32[256,512]{1,0:T(8,128)}, u32[]{:S(2)}) copy-start(f32[256,512]{1,0:T(8,128)} %move_cols.6.refs_4_) | copy-start | bytes 1572868
  161.2 19.6 %copy-start.4 = (f32[256,512]{1,0:T(8,128)S(1)}, f32[256,512]{1,0:T(8,128)}, u32[]{:S(2)}) copy-start(f32[256,512]{1,0:T(8,128)} %move_cols.8.refs_2_) | copy-start | bytes 1572868
  161.2 11.5 %collective-permute-start.14 = (f32[64,512]{1,0:T(8,128)S(1)}, f32[64,512]{1,0:T(8,128)S(1)}, u32[]{:S(2)}, u32[]{:S(2)}) collective-permute-start(f32[64,512]{1,0:T(8,128)S(1)} %pad_maximum_fusion.1), channel_id=1, source_target_pairs={{0,128},{32,160},{64,192},{96,224},{128,0},{160,32},{192,64},{224,... | collective-permute-start | bytes 393224 | tf_op jit(solution)/shard_map/ppermute | solution.py:261
  164.5 37.7 %collective-permute-start.13 = (f32[256,512]{1,0:T(8,128)}, f32[256,512]{1,0:T(8,128)}, u32[]{:S(2)}, u32[]{:S(2)}) collective-permute-start(f32[256,512]{1,0:T(8,128)} %get-tuple-element.20), channel_id=1, source_target_pairs={{1,2},{2,1},{3,4},{4,3},{5,6},{6,5},{7,8},{8,7},{9,10},{10,9},{11,... | collective-permute-start | bytes 1572872 | tf_op jit(solution)/shard_map/ppermute | solution.py:247
  172.7 11.5 %collective-permute-start.15 = (f32[128,512]{1,0:T(8,128)S(1)}, f32[128,512]{1,0:T(8,128)S(1)}, u32[]{:S(2)}, u32[]{:S(2)}) collective-permute-start(f32[128,512]{1,0:T(8,128)S(1)} %pad_maximum_fusion), channel_id=1, source_target_pairs={{0,256},{32,288},{64,320},{96,352},{128,384},{160,416},{192,448},{... | collective-permute-start | bytes 786440 | tf_op jit(solution)/shard_map/ppermute | solution.py:261
  175.1 50.2 %collective-permute-start.16 = (f32[256,512]{1,0:T(8,128)S(1)}, f32[256,512]{1,0:T(8,128)S(1)}, u32[]{:S(2)}, u32[]{:S(2)}) collective-permute-start(f32[256,512]{1,0:T(8,128)S(1)} %copy-done.2), channel_id=1, source_target_pairs={{32,0},{64,32},{96,64},{128,96},{160,128},{192,160},{224,192},{256... | collective-permute-start | bytes 1572872 | tf_op jit(solution)/shard_map/ppermute | solution.py:237
  178.9 46.4 %collective-permute-start.7 = (f32[256,512]{1,0:T(8,128)S(1)}, f32[256,512]{1,0:T(8,128)S(1)}, u32[]{:S(2)}, u32[]{:S(2)}) collective-permute-start(f32[256,512]{1,0:T(8,128)S(1)} %copy-done.3), channel_id=1, source_target_pairs={{0,32},{32,64},{64,96},{96,128},{128,160},{160,192},{192,224},{224... | collective-permute-start | bytes 1572872 | tf_op jit(solution)/shard_map/ppermute | solution.py:246
  180.8 59.8 %collective-permute-start.17 = (f32[256,512]{1,0:T(8,128)S(1)}, f32[256,512]{1,0:T(8,128)}, u32[]{:S(2)}, u32[]{:S(2)}) collective-permute-start(f32[256,512]{1,0:T(8,128)S(1)} %copy-done.4), channel_id=1, source_target_pairs={{32,0},{64,32},{96,64},{128,96},{160,128},{192,160},{224,192},{256... | collective-permute-start | bytes 1572872 | tf_op jit(solution)/shard_map/ppermute | solution.py:257
  208.0 43.6 %collective-permute-start.18 = (f32[256,512]{1,0:T(8,128)}, f32[256,512]{1,0:T(8,128)}, u32[]{:S(2)}, u32[]{:S(2)}) collective-permute-start(f32[256,512]{1,0:T(8,128)} %move_cols.9.refs_3_), channel_id=1, source_target_pairs={{0,32},{32,64},{64,96},{96,128},{128,160},{160,192},{192,224},{224... | collective-permute-start | bytes 1572872 | tf_op jit(solution)/shard_map/ppermute | solution.py:268
  (12 other events, 92.0 us)
where the time goes:
time: 256 us; the launch traced here: 254 us
  waiting for transfers between devices  87.9 us (34%)
  starting transfers between devices  81.1 us (32%)
  Pallas kernels  38.3 us (15%)
  local copies, waits for them, and re-layouts  25.7 us (10%)
  matrix products  16.3 us (6%)
  other arithmetic  3.94 us (2%)
    ppermute x4, waiting for transfers between devices, local(): total = total[:half] + lax.ppermute(total[half:], 'row', across(bit))  47.4 us
    pallas_call x5, Pallas kernels, move_cols(): pl.pallas_call(cols_kernel, out_shape=jax.ShapeDtypeStruct((rows, cols),...  25.2 us
    ppermute x1, waiting for transfers between devices, local(): halo[1] = lax.ppermute(moved[1], 'row', up)  15.3 us
    ppermute x2, starting transfers between devices, local(): far = {n: lax.ppermute(group(n), 'col', far_swap) for n in (0, 3)}  14.9 us
    ppermute x1, starting transfers between devices, local(): halo[2] = lax.ppermute(moved[2], 'row', down)  14.9 us
    ppermute x1, waiting for transfers between devices, local(): far[2] = lax.ppermute(after(group(2), moved[3]), 'col', far_swap)  14.8 us
    ppermute x4, starting transfers between devices, local(): total = total[:half] + lax.ppermute(total[half:], 'row', across(bit))  12.1 us
    pallas_call x1, Pallas kernels, move_rows(): pl.pallas_call(rows_kernel, out_shape=jax.ShapeDtypeStruct((rows, cols),...  11.1 us
  transfers between devices with their start and end apart: 19, of which 8 were waited for; matrix products, arithmetic and copies ran while one was open for 17% of the time, Pallas kernels for 10%

commit v1 on v0

v1 whole, which is shorter than its diff:
```python
import jax
import jax.numpy as jnp
from jax import lax
from jax.experimental import pallas as pl
from jax.experimental.pallas import tpu as pltpu
from jax.sharding import PartitionSpec as P


MAPX = 256
LANE = 128


diffusion = 0.05
HIGH = lax.Precision.HIGHEST
SMALL = pltpu.CompilerParams(vmem_limit_bytes=16 << 20)


def after(value, *earlier):
    return lax.optimization_barrier((value,) + earlier)[0]


def along(array, start, size, dim):
    return lax.slice_in_dim(array, start, start + size, axis=dim)


def weights_kernel(map_total, ahead, at_ref, mask_ref, speed_ref, rows_ref, cols_ref, down_ref):
    for ref, number in ((rows_ref, 0), (cols_ref, 1)):
        for m in range(ref.shape[1] // MAPX):
            map_row = at_ref[number] + m - ahead[number]
            inside = (map_row >= 0) & (map_row < map_total)
            cells = pl.ds(pl.multiple_of(jnp.clip(map_row, 0, map_total - 1) * MAPX, MAPX), MAPX)
            speed = speed_ref[:, cells]
            sign = mask_ref[:, cells].astype(jnp.float32)
            column = lax.broadcasted_iota(jnp.int32, (1, MAPX), 1)
            speed_x, speed_y = speed[0:1], speed[1:2]
            sign_x, sign_y = sign[0:1], sign[1:2]
            middle = 1.0 - speed_x - speed_y - 4.0 * diffusion
            western = jnp.where(column > 0, speed_x * sign_x + diffusion, 0.0)
            eastern = jnp.where(column < MAPX - 1, speed_x * (1.0 - sign_x) + diffusion, 0.0)
            northern = jnp.where(map_row > 0, speed_y * sign_y + diffusion, 0.0)
            southern = jnp.where(map_row < map_total - 1, speed_y * (1.0 - sign_y) + diffusion, 0.0)
            zero = jnp.zeros_like(middle)
            table = jnp.concatenate(
                [middle, western, eastern, northern, southern, zero, zero, zero], axis=0
            )
            table = jnp.where(inside, table, 0.0)
            ref[:, MAPX * m : MAPX * (m + 1)] = table
            if number == 0 and 0 < m < ref.shape[1] // MAPX - 1:
                down_ref[MAPX * (m - 1) : MAPX * m, :] = table.T


def local_weights(at, wind_mask, wind_speed, rows, cols):
    map_total = wind_speed.shape[1] // MAPX

    def kernel(*refs):
        weights_kernel(map_total, (2, 1), *refs)

    return pl.pallas_call(
        kernel,
        out_shape=(
            jax.ShapeDtypeStruct((8, rows + 4 * MAPX), jnp.float32),
            jax.ShapeDtypeStruct((8, cols + 2 * MAPX), jnp.float32),
            jax.ShapeDtypeStruct((rows + 2 * MAPX, 8), jnp.float32),
        ),
        grid_spec=pltpu.PrefetchScalarGridSpec(
            num_scalar_prefetch=1,
            grid=(1,),
            in_specs=[pl.BlockSpec(wind_mask.shape, lambda s, a: (0, 0))] * 2,
            out_specs=(
                pl.BlockSpec((8, rows + 4 * MAPX), lambda s, a: (0, 0)),
                pl.BlockSpec((8, cols + 2 * MAPX), lambda s, a: (0, 0)),
                pl.BlockSpec((rows + 2 * MAPX, 8), lambda s, a: (0, 0)),
            ),
        ),
        compiler_params=SMALL,
        cost_estimate=pl.CostEstimate(flops=1 << 16, bytes_accessed=1 << 20, transcendentals=0),
        name="local_weights",
    )(at, wind_mask, wind_speed)


def select_kernel(rows, at_ref, cells_ref, scale_ref, weights_ref, out_ref, counts_ref):
    each = cells_ref.shape[0]
    window = weights_ref.shape[1]
    blocks = window // LANE
    place = cells_ref[...] - (at_ref[0] * rows - 2 * MAPX)
    block_of, lane_of = place >> 7, place & (LANE - 1)
    block_index = lax.broadcasted_iota(jnp.int32, (blocks, LANE), 0)
    lane_index = lax.broadcasted_iota(jnp.int32, (LANE, LANE), 0)
    for o in range(each):
        block_hit = jnp.where(block_of[o : o + 1] == block_index, 1.0, 0.0).astype(jnp.bfloat16)
        lane_hit = jnp.where(lane_of[o : o + 1] == lane_index, 1.0, 0.0).astype(jnp.bfloat16)
        counts_ref[o] = lax.dot_general(
            block_hit, lane_hit, (((1,), (1,)), ((), ())), preferred_element_type=jnp.float32
        )
    scale = scale_ref[...]

    def weights(k, m):
        return weights_ref[k : k + 1, MAPX * m : MAPX * (m + 1)]

    maps = [
        scale * jnp.concatenate([counts_ref[:, 2 * m, :], counts_ref[:, 2 * m + 1, :]], axis=1)
        for m in range(window // MAPX)
    ]
    for first in (1, 2):
        moved = []
        for m in range(1, len(maps) - 1):
            t = m + first - 1
            here = maps[m]
            value = weights(0, t) * here + pltpu.roll(weights(1, t) * here, MAPX - 1, 1)
            value = value + pltpu.roll(weights(2, t) * here, 1, 1)
            value = value + weights(3, t + 1) * maps[m + 1] + weights(4, t - 1) * maps[m - 1]
            moved.append(value)
        maps = moved
    for m, value in enumerate(maps):
        out_ref[:, MAPX * m : MAPX * (m + 1)] = value


def observation_rows(at, obs_cells, obs_scale, weights, rows, pieces):
    obs_count, foot = obs_cells.shape
    each = obs_count // pieces

    def kernel(*refs):
        select_kernel(rows, *refs)

    return pl.pallas_call(
        kernel,
        out_shape=jax.ShapeDtypeStruct((obs_count, rows), jnp.float32),
        grid_spec=pltpu.PrefetchScalarGridSpec(
            num_scalar_prefetch=1,
            grid=(pieces,),
            in_specs=[
                pl.BlockSpec((each, foot), lambda s, a: (s ^ a[2], 0)),
                pl.BlockSpec((each, 1), lambda s, a: (s ^ a[2], 0)),
                pl.BlockSpec(weights.shape, lambda s, a: (0, 0)),
            ],
            out_specs=pl.BlockSpec((each, rows), lambda s, a: (s, 0)),
            scratch_shapes=[pltpu.VMEM((each, weights.shape[1] // LANE, LANE), jnp.float32)],
        ),
        compiler_params=SMALL,
        cost_estimate=pl.CostEstimate(flops=1 << 27, bytes_accessed=1 << 21, transcendentals=0),
        name="observation_rows",
    )(at[2:], obs_cells, obs_scale[:, None], weights)


def step_cols(before, here, behind, weights):
    width = here.shape[1]
    result = weights[0] * here + weights[1] * pltpu.roll(here, 1, 1)
    result = result + weights[2] * pltpu.roll(here, width - 1, 1)
    return result + weights[3] * before + weights[4] * behind


def cols_kernel(inner, unroll, core_ref, here_ref, near_ref, *refs):
    far_refs, (weights_ref, out_ref) = refs[:-2], refs[-2:]
    first = core_ref[0] == 0

    def weights(m):
        return [weights_ref[k : k + 1, MAPX * m : MAPX * (m + 1)] for k in range(5)]

    def body(t, carry):
        rows = pl.ds(pl.multiple_of(t * inner, inner), inner)
        near, here = near_ref[rows, :], here_ref[rows, :]
        far = far_refs[0][rows, :]
        for ref in far_refs[1:]:
            far = far + ref[rows, :]
        west = jnp.where(first, far, near)
        east = jnp.where(first, near, far)
        maps = [part[:, MAPX * k : MAPX * (k + 1)] for part in (west, here, east) for k in range(2)]
        once = [step_cols(maps[m], maps[m + 1], maps[m + 2], weights(m)) for m in range(4)]
        for m in range(2):
            out_ref[rows, MAPX * m : MAPX * (m + 1)] = step_cols(
                once[m], once[m + 1], once[m + 2], weights(m + 1)
            )
        return carry

    lax.fori_loop(0, here_ref.shape[0] // inner, body, 0, unroll=unroll)


def move_cols(core, here, near, fars, weights, rows):
    cols = here[0].shape[1]
    tile = min(rows, 128)
    inner = min(rows, 64)
    steps = rows // tile

    def kernel(*refs):
        cols_kernel(inner, tile // inner, *refs)

    def spec(at):
        return pl.BlockSpec((tile, cols), lambda s, c: (at * steps + s, 0))

    blocks = [here, near, *fars]
    return pl.pallas_call(
        kernel,
        out_shape=jax.ShapeDtypeStruct((rows, cols), jnp.float32),
        grid_spec=pltpu.PrefetchScalarGridSpec(
            num_scalar_prefetch=1,
            grid=(steps,),
            in_specs=[spec(at) for _, at in blocks]
            + [pl.BlockSpec(weights.shape, lambda s, c: (0, 0))],
            out_specs=spec(0),
        ),
        compiler_params=SMALL,
        cost_estimate=pl.CostEstimate(
            flops=27 * rows * cols, bytes_accessed=16 * rows * cols, transcendentals=0
        ),
        name="move_cols",
    )(core, *[array for array, _ in blocks], weights)


def rows_kernel(chunk, *refs):
    maps, (update_ref, weights_ref, out_ref, once_ref) = refs[:7], refs[7:]

    def step(source, base, before, behind, weights_at, emit):
        def body(c, carry):
            start = pl.multiple_of(c * chunk, chunk)
            low = pl.multiple_of(jnp.maximum(start - 8, 0), 8)
            high = pl.multiple_of(jnp.minimum(start + chunk, MAPX - 8), 8)
            here = source[pl.ds(base + start, chunk), :]
            wide = jnp.concatenate(
                [source[pl.ds(base + low, 8), :], here, source[pl.ds(base + high, 8), :]], axis=0
            )
            weights = weights_ref[pl.ds(weights_at + start, chunk), :]
            value = weights[:, 0:1] * here
            value = value + weights[:, 1:2] * pltpu.roll(wide, 1, 0)[8 : 8 + chunk]
            value = value + weights[:, 2:3] * pltpu.roll(wide, chunk + 15, 0)[8 : 8 + chunk]
            if before is not None:
                value = value + weights[:, 3:4] * before[0][pl.ds(before[1] + start, chunk), :]
            value = value + weights[:, 4:5] * behind[0][pl.ds(behind[1] + start, chunk), :]
            emit(start, value)
            return carry

        lax.fori_loop(0, MAPX // chunk, body, 0, unroll=MAPX // chunk)

    for m in range(6):

        def emit(start, value, m=m):
            once_ref[pl.ds(MAPX * m + start, chunk), :] = value

        step(maps[m], 0, (maps[m - 1], 0) if m > 0 else None, (maps[m + 1], 0), MAPX * m, emit)
    for m in range(1, 5):

        def emit(start, value, m=m):
            rows = pl.ds(MAPX * (m - 1) + start, chunk)
            out_ref[rows, :] = value - update_ref[rows, :]

        step(
            once_ref, MAPX * m, (once_ref, MAPX * (m - 1)), (once_ref, MAPX * (m + 1)), MAPX * m, emit
        )


def move_rows(maps, update, weights):
    rows, cols = update.shape

    def kernel(*refs):
        rows_kernel(64, *refs)

    def whole(array):
        return pl.BlockSpec(array.shape, lambda s: (0, 0))

    return pl.pallas_call(
        kernel,
        out_shape=jax.ShapeDtypeStruct((rows, cols), jnp.float32),
        grid=(1,),
        in_specs=[whole(array) for array in (*maps, update, weights)],
        out_specs=whole(update),
        scratch_shapes=[pltpu.VMEM((rows + 2 * MAPX, cols), jnp.float32)],
        compiler_params=SMALL,
        cost_estimate=pl.CostEstimate(
            flops=24 * rows * cols, bytes_accessed=16 * rows * cols, transcendentals=0
        ),
        name="move_rows",
    )(*maps, update, weights)


def last_kernel(result_ref, halo_ref, weights_ref, before_ref, out_ref):
    factor = weights_ref[:, 3:4] * before_ref[:, 3:4]
    out_ref[...] = result_ref[...] + factor * halo_ref[...]


def add_last(result, halo, weights):
    cols = result.shape[1]
    tile = 128
    steps = MAPX // tile
    block = pl.BlockSpec((tile, cols), lambda s: (s, 0))
    return pl.pallas_call(
        last_kernel,
        out_shape=jax.ShapeDtypeStruct(result.shape, result.dtype),
        grid=(steps,),
        in_specs=[
            block,
            block,
            pl.BlockSpec((tile, weights.shape[1]), lambda s: (steps + s, 0)),
            pl.BlockSpec((tile, weights.shape[1]), lambda s: (s, 0)),
        ],
        out_specs=block,
        input_output_aliases={0: 0},
        compiler_params=SMALL,
        cost_estimate=pl.CostEstimate(
            flops=2 * MAPX * cols, bytes_accessed=12 * MAPX * cols, transcendentals=0
        ),
        name="add_last",
    )(result, halo, weights, weights)


def local(covariance, wind_mask, wind_speed, obs_cells, obs_scale, gain):
    rows, cols = covariance.shape
    row_parts = lax.axis_size("row")
    col_parts = lax.axis_size("col")
    assert row_parts == 16 and rows == 4 * MAPX and cols == 2 * MAPX
    row_at = lax.axis_index("row")
    col_at = lax.axis_index("col")
    down = [(i, i + 1) for i in range(row_parts - 1)]
    up = [(i + 1, i) for i in range(row_parts - 1)]
    near_swap = [(j, j ^ 1) for j in range(col_parts)]
    far_swap = [(j, (j - 1 ^ 1) + 1) for j in range(1, col_parts - 1)]
    turning = [(a, b) for a, b in far_swap if a % 4 in (0, 3)]
    straight = [(a, b) for a, b in far_swap if a % 4 in (1, 2)]
    core = (col_at % 2).reshape(1)
    at = jnp.stack([row_at * (rows // MAPX), col_at * (cols // MAPX), row_at])

    def across(bit):
        return [(i, i ^ bit) for i in range(row_parts)]

    far_turning = lax.ppermute(covariance, "col", turning)
    near = lax.ppermute(covariance, "col", near_swap)

    row_weights, col_weights, down_weights = local_weights(at, wind_mask, wind_speed, rows, cols)
    select = observation_rows(at, obs_cells, obs_scale, row_weights, rows, row_parts)
    part = jnp.dot(select, covariance, precision=HIGH, preferred_element_type=jnp.float32)

    total = part
    for bit in (8, 4):
        half = total.shape[0] // 2
        total = total[:half] + lax.ppermute(total[half:], "row", across(bit))
    each = total.shape[0] // 4
    total = total[:each] + sum(
        lax.ppermute(total[each * bit : each * (bit + 1)], "row", across(bit))
        for bit in (1, 2, 3)
    )

    piece_far = lax.ppermute(total, "col", far_swap)
    order = (0, 3, 1, 2)
    late = after(covariance, select)
    far_straight = {n: lax.ppermute(along(late, MAPX * n, MAPX, 0), "col", straight) for n in order}
    piece_near = lax.ppermute(total, "col", near_swap)
    piece = move_cols(core, (total, 0), (piece_near, 0), [(piece_far, 0)], col_weights, each)
    gathered = [lax.ppermute(piece, "row", across(bit)) for bit in (1, 2, 3)]

    moved, halo = {}, {}
    for n in order:
        moved[n] = move_cols(
            core,
            (covariance, n),
            (near, n),
            [(far_turning, n), (far_straight[n], 0)],
            col_weights,
            MAPX,
        )
        halo[n] = lax.ppermute(moved[n], "row", up if n < 2 else down)

    observed = jnp.concatenate([after(piece, moved[2]), *gathered])
    for bit in (4, 8):
        observed = jnp.concatenate([observed, lax.ppermute(observed, "row", across(bit))])
    index = jnp.arange(gain.shape[1], dtype=jnp.int32)
    reorder = (index[:, None] ^ (row_at * each)) == index[None, :]
    ordered_gain = jnp.dot(gain, reorder.astype(gain.dtype), preferred_element_type=jnp.float32)
    update = jnp.dot(ordered_gain, observed, precision=HIGH, preferred_element_type=jnp.float32)

    maps = [halo[3], moved[0], moved[1], moved[2], moved[3], halo[0], halo[1]]
    result = move_rows(maps, update, down_weights)
    return add_last(result, halo[2], down_weights)


def solution(mesh):
    placed = (P("row", "col"), P(), P(), P(), P(), P("row", None))
    return jax.shard_map(
        local, mesh=mesh, in_specs=placed, out_specs=P("row", "col"), check_vma=False
    )
```

time: 256 us -> 198 us (0.77)
  the two profiles are of different devices: /device:TPU:93 before, /device:TPU:223 now
where the time goes in v1:
time: 198 us; the launch traced here: 197 us
  waiting for transfers between devices  80.1 us (40%)
  starting transfers between devices  78.3 us (40%)
  Pallas kernels  26 us (13%)
  local copies, waits for them, and re-layouts  6.36 us (3%)
  matrix products  5.95 us (3%)
    ppermute x2, waiting for transfers between devices, local(): lax.ppermute(observed, 'row', across(bit))  29.2 us
    ppermute x3, waiting for transfers between devices, local(): lax.ppermute(total[each * bit:each * (bit + 1)], 'row', across(bit))  21.3 us
    ppermute x4, starting transfers between devices, local(): lax.ppermute(along(late, MAPX * n, MAPX, 0), 'col', straight)  19.8 us
    ppermute x3, waiting for transfers between devices, local(): gathered = [lax.ppermute(piece, 'row', across(bit)) for bit in (1, 2, 3)]  17.4 us
    ppermute x2, starting transfers between devices, local(): lax.ppermute(observed, 'row', across(bit))  13.5 us
    pallas_call x1, Pallas kernels, observation_rows(): pl.pallas_call(kernel, out_shape=jax.ShapeDtypeStruct((obs_count, rows),...  9.45 us
    pallas_call x5, Pallas kernels, move_cols(): pl.pallas_call(kernel, out_shape=jax.ShapeDtypeStruct((rows, cols), jnp.f...  9.18 us
    ppermute x4, starting transfers between devices, local(): halo[n] = lax.ppermute(moved[n], 'row', up if n < 2 else down)  8.51 us
  transfers between devices with their start and end apart: 22, of which 6 were waited for; matrix products, arithmetic and copies ran while one was open for 4% of the time, Pallas kernels for 12%

profile of v1, /device:TPU:223, one launch (start us, length us, event | category | flops | bytes accessed | tf_op | source)
XLA Modules:
  0.0 197.5 jit_solution(16836733197660511848)
XLA Ops:
  2.1 8.2 %collective-permute-start = (f32[1024,512]{1,0:T(8,128)}, f32[1024,512]{1,0:T(8,128)}, u32[]{:S(2)}, u32[]{:S(2)}) collective-permute-start(f32[1024,512]{1,0:T(8,128)} %refs_1_.11), channel_id=1, source_target_pairs={{0,1},{1,0},{2,3},{3,2},{4,5},{5,4},{6,7},{7,6},{8,9},{9,8},{10,11... | collective-permute-start | bytes 6291464 | tf_op jit(solution)/shard_map/ppermute | solution.py:324
  14.8 9.5 %observation_rows.1 = f32[256,1024]{1,0:T(8,128)S(1)} custom-call(s32[1]{0:T(128)} %bitcast.1.refs_0_, s32[256,128]{1,0:T(8,128)S(1)} %copy-done.2, f32[256,1]{1,0:T(8,128)S(1)} %copy.8.refs_2_, f32[8,2048]{1,0:T(8,128)S(1)} %get-tuple-element.10.refs_3_), custom_call_target="tpu_custom_call" | custom-call | flops 134217728 | bytes 2097152 | tf_op jit(solution)/shard_map/observation_rows/pallas_call | solution.py:125
  24.2 3.7 %fusion.6 = f32[256,512]{1,0:T(8,128)S(1)} fusion(f32[256,1024]{1,0:T(8,128)S(1)} %observation_rows.1, f32[1024,512]{1,0:T(8,128)} %refs_1_.11), kind=kOutput, calls=%fused_computation.23 | convolution fusion | flops 1610612736 | bytes 3670016 | tf_op jit(solution)/shard_map/dot_general | solution.py:328
  27.9 3.0 %collective-permute-start.9 = (f32[128,512]{1,0:T(8,128)S(1)}, f32[128,512]{1,0:T(8,128)S(1)}, u32[]{:S(2)}, u32[]{:S(2)}) collective-permute-start(f32[128,512]{1,0:T(8,128)S(1)} %slice.49), channel_id=1, source_target_pairs={{0,256},{32,288},{64,320},{96,352},{128,384},{160,416},{192,448},{... | collective-permute-start | bytes 786440 | tf_op jit(solution)/shard_map/ppermute | solution.py:333
  31.0 8.3 %collective-permute-done.9 = f32[128,512]{1,0:T(8,128)S(1)} collective-permute-done((f32[128,512]{1,0:T(8,128)S(1)}, f32[128,512]{1,0:T(8,128)S(1)}, u32[]{:S(2)}, u32[]{:S(2)}) %collective-permute-start.9) | collective-permute-done | bytes 262176 | tf_op jit(solution)/shard_map/ppermute | solution.py:333
  39.4 2.5 %collective-permute-start.10 = (f32[64,512]{1,0:T(8,128)S(1)}, f32[64,512]{1,0:T(8,128)S(1)}, u32[]{:S(2)}, u32[]{:S(2)}) collective-permute-start(f32[64,512]{1,0:T(8,128)S(1)} %slice.51), channel_id=1, source_target_pairs={{0,128},{32,160},{64,192},{96,224},{128,0},{160,32},{192,64},{224,... | collective-permute-start | bytes 393224 | tf_op jit(solution)/shard_map/ppermute | solution.py:333
  43.2 4.7 %collective-permute-start.6 = (f32[256,512]{1,0:T(8,128)}, f32[256,512]{1,0:T(8,128)}, u32[]{:S(2)}, u32[]{:S(2)}) collective-permute-start(f32[256,512]{1,0:T(8,128)} %get-tuple-element.15), channel_id=1, source_target_pairs={{1,2},{2,1},{5,6},{6,5},{9,10},{10,9},{13,14},{14,13},{17,18},{18,... | collective-permute-start | bytes 1572872 | tf_op jit(solution)/shard_map/ppermute | solution.py:343
  49.9 3.4 %collective-permute-start.13 = (f32[16,512]{1,0:T(8,128)S(1)}, f32[16,512]{1,0:T(8,128)S(1)}, u32[]{:S(2)}, u32[]{:S(2)}) collective-permute-start(f32[16,512]{1,0:T(8,128)S(1)} %get-tuple-element.22), channel_id=1, source_target_pairs={{0,96},{32,64},{64,32},{96,0},{128,224},{160,192},{192,160},{224,1... | collective-permute-start | bytes 98312 | tf_op jit(solution)/shard_map/ppermute | solution.py:336
  53.2 18.6 %collective-permute-done.12 = f32[16,512]{1,0:T(8,128)S(1)} collective-permute-done((f32[16,512]{1,0:T(8,128)S(1)}, f32[16,512]{1,0:T(8,128)S(1)}, u32[]{:S(2)}, u32[]{:S(2)}) %collective-permute-start.12) | collective-permute-done | bytes 32800 | tf_op jit(solution)/shard_map/ppermute | solution.py:336
  73.8 2.7 %collective-permute-done.11 = f32[16,512]{1,0:T(8,128)S(1)} collective-permute-done((f32[16,512]{1,0:T(8,128)S(1)}, f32[16,512]{1,0:T(8,128)S(1)}, u32[]{:S(2)}, u32[]{:S(2)}) %collective-permute-start.11) | collective-permute-done | bytes 32800 | tf_op jit(solution)/shard_map/ppermute | solution.py:336
  76.5 2.5 %collective-permute-start.15 = (f32[16,512]{1,0:T(8,128)S(1)}, f32[16,512]{1,0:T(8,128)S(1)}, u32[]{:S(2)}, u32[]{:S(2)}) collective-permute-start(f32[16,512]{1,0:T(8,128)S(1)} %slice_add_fusion.2.refs_1_), channel_id=1, source_target_pairs={{1,2},{2,1},{3,4},{4,3},{5,6},{6,5},{7,8},{8,7},{9,10},{10,9},{11,... | collective-permute-start | bytes 98312 | tf_op jit(solution)/shard_map/ppermute | solution.py:340
  79.0 2.8 %collective-permute-start.14 = (f32[16,512]{1,0:T(8,128)S(1)}, f32[16,512]{1,0:T(8,128)S(1)}, u32[]{:S(2)}, u32[]{:S(2)}) collective-permute-start(f32[16,512]{1,0:T(8,128)S(1)} %slice_add_fusion.2.refs_1_), channel_id=1, source_target_pairs={{0,1},{1,0},{2,3},{3,2},{4,5},{5,4},{6,7},{7,6},{8,9},{9,8},{10,11... | collective-permute-start | bytes 98312 | tf_op jit(solution)/shard_map/ppermute | solution.py:344
  81.9 3.9 %collective-permute-done.15.refs_3_ = f32[16,512]{1,0:T(8,128)S(1)} collective-permute-done((f32[16,512]{1,0:T(8,128)S(1)}, f32[16,512]{1,0:T(8,128)S(1)}, u32[]{:S(2)}, u32[]{:S(2)}) %collective-permute-start.15) | collective-permute-done | bytes 32800 | tf_op jit(solution)/shard_map/ppermute | solution.py:340
  89.3 5.7 %collective-permute-start.2 = (f32[256,512]{1,0:T(8,128)}, f32[256,512]{1,0:T(8,128)}, u32[]{:S(2)}, u32[]{:S(2)}) collective-permute-start(f32[256,512]{1,0:T(8,128)} %get-tuple-element.18), channel_id=1, source_target_pairs={{1,2},{2,1},{5,6},{6,5},{9,10},{10,9},{13,14},{14,13},{17,18},{18,... | collective-permute-start | bytes 1572872 | tf_op jit(solution)/shard_map/ppermute | solution.py:343
  95.0 4.3 %collective-permute-start.4 = (f32[256,512]{1,0:T(8,128)}, f32[256,512]{1,0:T(8,128)}, u32[]{:S(2)}, u32[]{:S(2)}) collective-permute-start(f32[256,512]{1,0:T(8,128)} %get-tuple-element.17), channel_id=1, source_target_pairs={{1,2},{2,1},{5,6},{6,5},{9,10},{10,9},{13,14},{14,13},{17,18},{18,... | collective-permute-start | bytes 1572872 | tf_op jit(solution)/shard_map/ppermute | solution.py:343
  99.3 5.2 %collective-permute-start.5 = (f32[256,512]{1,0:T(8,128)}, f32[256,512]{1,0:T(8,128)}, u32[]{:S(2)}, u32[]{:S(2)}) collective-permute-start(f32[256,512]{1,0:T(8,128)} %get-tuple-element.16), channel_id=1, source_target_pairs={{1,2},{2,1},{5,6},{6,5},{9,10},{10,9},{13,14},{14,13},{17,18},{18,... | collective-permute-start | bytes 1572872 | tf_op jit(solution)/shard_map/ppermute | solution.py:343
  106.4 4.3 %collective-permute-start.16 = (f32[16,512]{1,0:T(8,128)S(1)}, f32[16,512]{1,0:T(8,128)S(1)}, u32[]{:S(2)}, u32[]{:S(2)}) collective-permute-start(f32[16,512]{1,0:T(8,128)S(1)} %move_cols.9), channel_id=1, source_target_pairs={{0,32},{32,0},{64,96},{96,64},{128,160},{160,128},{192,224},{224,1... | collective-permute-start | bytes 98312 | tf_op jit(solution)/shard_map/ppermute | solution.py:346
  110.8 2.3 %move_cols.8.refs_3_ = f32[256,512]{1,0:T(8,128)S(1)} custom-call(s32[1]{0:T(128)} %bitcast.refs_0_, f32[1024,512]{1,0:T(8,128)S(1)} %copy-done.1, f32[1024,512]{1,0:T(8,128)} %collective-permute-done.refs_2_, f32[1024,512]{1,0:T(8,128)} %collective-permute-done.1.refs_3_, f32[256,512]{1,0:T(8,128)} %collective-permute-done.6.refs_4_, ...), custom_call_target="tpu_custom_call" | custom-call | flops 3538944 | bytes 2097152 | tf_op jit(solution)/shard_map/move_cols/pallas_call | solution.py:191
  113.0 17.4 %collective-permute-done.17 = f32[16,512]{1,0:T(8,128)S(1)} collective-permute-done((f32[16,512]{1,0:T(8,128)S(1)}, f32[16,512]{1,0:T(8,128)S(1)}, u32[]{:S(2)}, u32[]{:S(2)}) %collective-permute-start.17) | collective-permute-done | bytes 32800 | tf_op jit(solution)/shard_map/ppermute | solution.py:346
  131.7 11.1 %collective-permute-start.19 = (f32[64,512]{1,0:T(8,128)S(1)}, f32[64,512]{1,0:T(8,128)S(1)}, u32[]{:S(2)}, u32[]{:S(2)}) collective-permute-start(f32[64,512]{1,0:T(8,128)S(1)} %pad_maximum_fusion), channel_id=1, source_target_pairs={{0,128},{32,160},{64,192},{96,224},{128,0},{160,32},{192,64},{224,... | collective-permute-start | bytes 393224 | tf_op jit(solution)/shard_map/ppermute | solution.py:362
  148.7 4.0 %collective-permute-start.7 = (f32[256,512]{1,0:T(8,128)S(1)}, f32[256,512]{1,0:T(8,128)S(1)}, u32[]{:S(2)}, u32[]{:S(2)}) collective-permute-start(f32[256,512]{1,0:T(8,128)S(1)} %move_cols.6.refs_1_), channel_id=1, source_target_pairs={{32,0},{64,32},{96,64},{128,96},{160,128},{192,160},{224,192},{256... | collective-permute-start | bytes 1572872 | tf_op jit(solution)/shard_map/ppermute | solution.py:358
  157.0 2.4 %collective-permute-start.20 = (f32[128,512]{1,0:T(8,128)S(1)}, f32[128,512]{1,0:T(8,128)S(1)}, u32[]{:S(2)}, u32[]{:S(2)}) collective-permute-start(f32[128,512]{1,0:T(8,128)S(1)} %get-tuple-element.19), channel_id=1, source_target_pairs={{0,256},{32,288},{64,320},{96,352},{128,384},{160,416},{192,448},{... | collective-permute-start | bytes 786440 | tf_op jit(solution)/shard_map/ppermute | solution.py:362
  159.9 29.2 %collective-permute-done.20 = f32[128,512]{1,0:T(8,128)S(1)} collective-permute-done((f32[128,512]{1,0:T(8,128)S(1)}, f32[128,512]{1,0:T(8,128)S(1)}, u32[]{:S(2)}, u32[]{:S(2)}) %collective-permute-start.20) | collective-permute-done | bytes 262176 | tf_op jit(solution)/shard_map/ppermute | solution.py:362
  190.9 4.7 %move_rows.1.result_ref = f32[1024,512]{1,0:T(8,128)} custom-call(f32[256,512]{1,0:T(8,128)S(1)} %collective-permute-done.3.refs_0_, f32[256,512]{1,0:T(8,128)S(1)} %move_cols.6.refs_1_, f32[256,512]{1,0:T(8,128)S(1)} %move_cols.7.refs_2_, f32[256,512]{1,0:T(8,128)S(1)} %move_cols.8.refs_3_, f32[256,512]{1,0:T(8,128)S(1)} %move_cols.5.refs_4_, ...), custom_call_target="tpu_custom_call" | custom-call | flops 12582912 | bytes 8388608 | tf_op jit(solution)/shard_map/move_rows/pallas_call | solution.py:259
  (63 shorter events, 32.7 us)
Async XLA Ops:
  0.0 159.4 %copy-start = (bf16[1024,256]{1,0:T(8,128)(2,1)S(1)}, bf16[1024,256]{1,0:T(8,128)(2,1)}, u32[]{:S(2)}) copy-start(bf16[1024,256]{1,0:T(8,128)(2,1)} %param.11) | copy-start | bytes 1572868
  0.0 104.5 %collective-permute-start.1 = (f32[1024,512]{1,0:T(8,128)}, f32[1024,512]{1,0:T(8,128)}, u32[]{:S(2)}, u32[]{:S(2)}) collective-permute-start(f32[1024,512]{1,0:T(8,128)} %refs_1_.11), channel_id=1, source_target_pairs={{3,4},{4,3},{7,8},{8,7},{11,12},{12,11},{15,16},{16,15},{19,20},{2... | collective-permute-start | bytes 6291464 | tf_op jit(solution)/shard_map/ppermute | solution.py:323
  2.1 104.3 %collective-permute-start = (f32[1024,512]{1,0:T(8,128)}, f32[1024,512]{1,0:T(8,128)}, u32[]{:S(2)}, u32[]{:S(2)}) collective-permute-start(f32[1024,512]{1,0:T(8,128)} %refs_1_.11), channel_id=1, source_target_pairs={{0,1},{1,0},{2,3},{3,2},{4,5},{5,4},{6,7},{7,6},{8,9},{9,8},{10,11... | collective-permute-start | bytes 6291464 | tf_op jit(solution)/shard_map/ppermute | solution.py:324
  24.2 17.6 %copy-start.1 = (f32[1024,512]{1,0:T(8,128)S(1)}, f32[1024,512]{1,0:T(8,128)}, u32[]{:S(2)}) copy-start(f32[1024,512]{1,0:T(8,128)} %refs_1_.11) | copy-start | bytes 6291460
  27.9 11.4 %collective-permute-start.9 = (f32[128,512]{1,0:T(8,128)S(1)}, f32[128,512]{1,0:T(8,128)S(1)}, u32[]{:S(2)}, u32[]{:S(2)}) collective-permute-start(f32[128,512]{1,0:T(8,128)S(1)} %slice.49), channel_id=1, source_target_pairs={{0,256},{32,288},{64,320},{96,352},{128,384},{160,416},{192,448},{... | collective-permute-start | bytes 786440 | tf_op jit(solution)/shard_map/ppermute | solution.py:333
  39.4 8.5 %collective-permute-start.10 = (f32[64,512]{1,0:T(8,128)S(1)}, f32[64,512]{1,0:T(8,128)S(1)}, u32[]{:S(2)}, u32[]{:S(2)}) collective-permute-start(f32[64,512]{1,0:T(8,128)S(1)} %slice.51), channel_id=1, source_target_pairs={{0,128},{32,160},{64,192},{96,224},{128,0},{160,32},{192,64},{224,... | collective-permute-start | bytes 393224 | tf_op jit(solution)/shard_map/ppermute | solution.py:333
  43.2 56.1 %collective-permute-start.6 = (f32[256,512]{1,0:T(8,128)}, f32[256,512]{1,0:T(8,128)}, u32[]{:S(2)}, u32[]{:S(2)}) collective-permute-start(f32[256,512]{1,0:T(8,128)} %get-tuple-element.15), channel_id=1, source_target_pairs={{1,2},{2,1},{5,6},{6,5},{9,10},{10,9},{13,14},{14,13},{17,18},{18,... | collective-permute-start | bytes 1572872 | tf_op jit(solution)/shard_map/ppermute | solution.py:343
  47.9 23.9 %collective-permute-start.12 = (f32[16,512]{1,0:T(8,128)S(1)}, f32[16,512]{1,0:T(8,128)S(1)}, u32[]{:S(2)}, u32[]{:S(2)}) collective-permute-start(f32[16,512]{1,0:T(8,128)S(1)} %get-tuple-element.21), channel_id=1, source_target_pairs={{0,64},{32,96},{64,0},{96,32},{128,192},{160,224},{192,128},{224,1... | collective-permute-start | bytes 98312 | tf_op jit(solution)/shard_map/ppermute | solution.py:336
  49.9 23.9 %collective-permute-start.13 = (f32[16,512]{1,0:T(8,128)S(1)}, f32[16,512]{1,0:T(8,128)S(1)}, u32[]{:S(2)}, u32[]{:S(2)}) collective-permute-start(f32[16,512]{1,0:T(8,128)S(1)} %get-tuple-element.22), channel_id=1, source_target_pairs={{0,96},{32,64},{64,32},{96,0},{128,224},{160,192},{192,160},{224,1... | collective-permute-start | bytes 98312 | tf_op jit(solution)/shard_map/ppermute | solution.py:336
  71.8 4.6 %collective-permute-start.11 = (f32[16,512]{1,0:T(8,128)S(1)}, f32[16,512]{1,0:T(8,128)S(1)}, u32[]{:S(2)}, u32[]{:S(2)}) collective-permute-start(f32[16,512]{1,0:T(8,128)S(1)} %get-tuple-element.23), channel_id=1, source_target_pairs={{0,32},{32,0},{64,96},{96,64},{128,160},{160,128},{192,224},{224,1... | collective-permute-start | bytes 98312 | tf_op jit(solution)/shard_map/ppermute | solution.py:336
  76.5 9.3 %collective-permute-start.15 = (f32[16,512]{1,0:T(8,128)S(1)}, f32[16,512]{1,0:T(8,128)S(1)}, u32[]{:S(2)}, u32[]{:S(2)}) collective-permute-start(f32[16,512]{1,0:T(8,128)S(1)} %slice_add_fusion.2.refs_1_), channel_id=1, source_target_pairs={{1,2},{2,1},{3,4},{4,3},{5,6},{6,5},{7,8},{8,7},{9,10},{10,9},{11,... | collective-permute-start | bytes 98312 | tf_op jit(solution)/shard_map/ppermute | solution.py:340
  79.0 6.8 %collective-permute-start.14 = (f32[16,512]{1,0:T(8,128)S(1)}, f32[16,512]{1,0:T(8,128)S(1)}, u32[]{:S(2)}, u32[]{:S(2)}) collective-permute-start(f32[16,512]{1,0:T(8,128)S(1)} %slice_add_fusion.2.refs_1_), channel_id=1, source_target_pairs={{0,1},{1,0},{2,3},{3,2},{4,5},{5,4},{6,7},{7,6},{8,9},{9,8},{10,11... | collective-permute-start | bytes 98312 | tf_op jit(solution)/shard_map/ppermute | solution.py:344
  87.4 7.6 %collective-permute-start.18 = (f32[16,512]{1,0:T(8,128)S(1)}, f32[16,512]{1,0:T(8,128)S(1)}, u32[]{:S(2)}, u32[]{:S(2)}) collective-permute-start(f32[16,512]{1,0:T(8,128)S(1)} %move_cols.9), channel_id=1, source_target_pairs={{0,96},{32,64},{64,32},{96,0},{128,224},{160,192},{192,160},{224,1... | collective-permute-start | bytes 98312 | tf_op jit(solution)/shard_map/ppermute | solution.py:346
  89.3 53.6 %collective-permute-start.2 = (f32[256,512]{1,0:T(8,128)}, f32[256,512]{1,0:T(8,128)}, u32[]{:S(2)}, u32[]{:S(2)}) collective-permute-start(f32[256,512]{1,0:T(8,128)} %get-tuple-element.18), channel_id=1, source_target_pairs={{1,2},{2,1},{5,6},{6,5},{9,10},{10,9},{13,14},{14,13},{17,18},{18,... | collective-permute-start | bytes 1572872 | tf_op jit(solution)/shard_map/ppermute | solution.py:343
  95.0 51.5 %collective-permute-start.4 = (f32[256,512]{1,0:T(8,128)}, f32[256,512]{1,0:T(8,128)}, u32[]{:S(2)}, u32[]{:S(2)}) collective-permute-start(f32[256,512]{1,0:T(8,128)} %get-tuple-element.17), channel_id=1, source_target_pairs={{1,2},{2,1},{5,6},{6,5},{9,10},{10,9},{13,14},{14,13},{17,18},{18,... | collective-permute-start | bytes 1572872 | tf_op jit(solution)/shard_map/ppermute | solution.py:343
  99.3 53.5 %collective-permute-start.5 = (f32[256,512]{1,0:T(8,128)}, f32[256,512]{1,0:T(8,128)}, u32[]{:S(2)}, u32[]{:S(2)}) collective-permute-start(f32[256,512]{1,0:T(8,128)} %get-tuple-element.16), channel_id=1, source_target_pairs={{1,2},{2,1},{5,6},{6,5},{9,10},{10,9},{13,14},{14,13},{17,18},{18,... | collective-permute-start | bytes 1572872 | tf_op jit(solution)/shard_map/ppermute | solution.py:343
  104.5 25.9 %collective-permute-start.17 = (f32[16,512]{1,0:T(8,128)S(1)}, f32[16,512]{1,0:T(8,128)S(1)}, u32[]{:S(2)}, u32[]{:S(2)}) collective-permute-start(f32[16,512]{1,0:T(8,128)S(1)} %move_cols.9), channel_id=1, source_target_pairs={{0,64},{32,96},{64,0},{96,32},{128,192},{160,224},{192,128},{224,1... | collective-permute-start | bytes 98312 | tf_op jit(solution)/shard_map/ppermute | solution.py:346
  106.4 25.3 %collective-permute-start.16 = (f32[16,512]{1,0:T(8,128)S(1)}, f32[16,512]{1,0:T(8,128)S(1)}, u32[]{:S(2)}, u32[]{:S(2)}) collective-permute-start(f32[16,512]{1,0:T(8,128)S(1)} %move_cols.9), channel_id=1, source_target_pairs={{0,32},{32,0},{64,96},{96,64},{128,160},{160,128},{192,224},{224,1... | collective-permute-start | bytes 98312 | tf_op jit(solution)/shard_map/ppermute | solution.py:346
  130.4 65.2 %collective-permute-start.21 = (f32[256,512]{1,0:T(8,128)S(1)}, f32[256,512]{1,0:T(8,128)S(1)}, u32[]{:S(2)}, u32[]{:S(2)}) collective-permute-start(f32[256,512]{1,0:T(8,128)S(1)} %move_cols.8.refs_3_), channel_id=1, source_target_pairs={{0,32},{32,64},{64,96},{96,128},{128,160},{160,192},{192,224},{224... | collective-permute-start | bytes 1572872 | tf_op jit(solution)/shard_map/ppermute | solution.py:358
  131.7 25.3 %collective-permute-start.19 = (f32[64,512]{1,0:T(8,128)S(1)}, f32[64,512]{1,0:T(8,128)S(1)}, u32[]{:S(2)}, u32[]{:S(2)}) collective-permute-start(f32[64,512]{1,0:T(8,128)S(1)} %pad_maximum_fusion), channel_id=1, source_target_pairs={{0,128},{32,160},{64,192},{96,224},{128,0},{160,32},{192,64},{224,... | collective-permute-start | bytes 393224 | tf_op jit(solution)/shard_map/ppermute | solution.py:362
  145.1 45.8 %collective-permute-start.3 = (f32[256,512]{1,0:T(8,128)S(1)}, f32[256,512]{1,0:T(8,128)S(1)}, u32[]{:S(2)}, u32[]{:S(2)}) collective-permute-start(f32[256,512]{1,0:T(8,128)S(1)} %move_cols.5.refs_4_), channel_id=1, source_target_pairs={{0,32},{32,64},{64,96},{96,128},{128,160},{160,192},{192,224},{224... | collective-permute-start | bytes 1572872 | tf_op jit(solution)/shard_map/ppermute | solution.py:358
  148.7 42.2 %collective-permute-start.7 = (f32[256,512]{1,0:T(8,128)S(1)}, f32[256,512]{1,0:T(8,128)S(1)}, u32[]{:S(2)}, u32[]{:S(2)}) collective-permute-start(f32[256,512]{1,0:T(8,128)S(1)} %move_cols.6.refs_1_), channel_id=1, source_target_pairs={{32,0},{64,32},{96,64},{128,96},{160,128},{192,160},{224,192},{256... | collective-permute-start | bytes 1572872 | tf_op jit(solution)/shard_map/ppermute | solution.py:358
  155.0 35.9 %collective-permute-start.8 = (f32[256,512]{1,0:T(8,128)S(1)}, f32[256,512]{1,0:T(8,128)S(1)}, u32[]{:S(2)}, u32[]{:S(2)}) collective-permute-start(f32[256,512]{1,0:T(8,128)S(1)} %move_cols.7.refs_2_), channel_id=1, source_target_pairs={{32,0},{64,32},{96,64},{128,96},{160,128},{192,160},{224,192},{256... | collective-permute-start | bytes 1572872 | tf_op jit(solution)/shard_map/ppermute | solution.py:358
  157.0 32.0 %collective-permute-start.20 = (f32[128,512]{1,0:T(8,128)S(1)}, f32[128,512]{1,0:T(8,128)S(1)}, u32[]{:S(2)}, u32[]{:S(2)}) collective-permute-start(f32[128,512]{1,0:T(8,128)S(1)} %get-tuple-element.19), channel_id=1, source_target_pairs={{0,256},{32,288},{64,320},{96,352},{128,384},{160,416},{192,448},{... | collective-permute-start | bytes 786440 | tf_op jit(solution)/shard_map/ppermute | solution.py:362
  (5 other events, 4.1 us)

commit v2 on v1

--- a/solution.py
+++ b/solution.py
@@ -23,88 +23,68 @@
     return lax.slice_in_dim(array, start, start + size, axis=dim)
 
 
-def weights_kernel(map_total, ahead, at_ref, mask_ref, speed_ref, rows_ref, cols_ref, down_ref):
-    for ref, number in ((rows_ref, 0), (cols_ref, 1)):
-        for m in range(ref.shape[1] // MAPX):
-            map_row = at_ref[number] + m - ahead[number]
-            inside = (map_row >= 0) & (map_row < map_total)
-            cells = pl.ds(pl.multiple_of(jnp.clip(map_row, 0, map_total - 1) * MAPX, MAPX), MAPX)
-            speed = speed_ref[:, cells]
-            sign = mask_ref[:, cells].astype(jnp.float32)
-            column = lax.broadcasted_iota(jnp.int32, (1, MAPX), 1)
-            speed_x, speed_y = speed[0:1], speed[1:2]
-            sign_x, sign_y = sign[0:1], sign[1:2]
-            middle = 1.0 - speed_x - speed_y - 4.0 * diffusion
-            western = jnp.where(column > 0, speed_x * sign_x + diffusion, 0.0)
-            eastern = jnp.where(column < MAPX - 1, speed_x * (1.0 - sign_x) + diffusion, 0.0)
-            northern = jnp.where(map_row > 0, speed_y * sign_y + diffusion, 0.0)
-            southern = jnp.where(map_row < map_total - 1, speed_y * (1.0 - sign_y) + diffusion, 0.0)
-            zero = jnp.zeros_like(middle)
-            table = jnp.concatenate(
-                [middle, western, eastern, northern, southern, zero, zero, zero], axis=0
+def weights_table(map_total, map_row, mask_ref, speed_ref):
+    inside = (map_row >= 0) & (map_row < map_total)
+    cells = pl.ds(pl.multiple_of(jnp.clip(map_row, 0, map_total - 1) * MAPX, MAPX), MAPX)
+    speed = speed_ref[:, cells]
+    sign = mask_ref[:, cells].astype(jnp.float32)
+    column = lax.broadcasted_iota(jnp.int32, (1, MAPX), 1)
+    speed_x, speed_y = speed[0:1], speed[1:2]
+    sign_x, sign_y = sign[0:1], sign[1:2]
+    middle = 1.0 - speed_x - speed_y - 4.0 * diffusion
+    western = jnp.where(column > 0, speed_x * sign_x + diffusion, 0.0)
+    eastern = jnp.where(column < MAPX - 1, speed_x * (1.0 - sign_x) + diffusion, 0.0)
+    northern = jnp.where(map_row > 0, speed_y * sign_y + diffusion, 0.0)
+    southern = jnp.where(map_row < map_total - 1, speed_y * (1.0 - sign_y) + diffusion, 0.0)
+    zero = jnp.zeros_like(middle)
+    table = jnp.concatenate(
+        [middle, western, eastern, northern, southern, zero, zero, zero], axis=0
+    )
+    return jnp.where(inside, table, 0.0)
+
+
+def prepare_kernel(rows, map_total, at_ref, mask_ref, speed_ref, *refs):
+    cell_refs, (out_ref, cols_ref, down_ref, rows_ref, counts_ref) = refs[:-5], refs[-5:]
+
+    @pl.when(pl.program_id(0) == 0)
+    def _():
+        last = rows_ref.shape[1] // MAPX - 1
+        for m in range(last + 1):
+            table = weights_table(map_total, at_ref[0] + m - 2, mask_ref, speed_ref)
+            rows_ref[:, MAPX * m : MAPX * (m + 1)] = table
+            if 0 < m < last:
+                down_ref[MAPX * (m - 1) : MAPX * m, :] = table.T
+        for m in range(cols_ref.shape[1] // MAPX):
+            cols_ref[:, MAPX * m : MAPX * (m + 1)] = weights_table(
+                map_total, at_ref[1] + m - 1, mask_ref, speed_ref
             )
-            table = jnp.where(inside, table, 0.0)
-            ref[:, MAPX * m : MAPX * (m + 1)] = table
-            if number == 0 and 0 < m < ref.shape[1] // MAPX - 1:
-                down_ref[MAPX * (m - 1) : MAPX * m, :] = table.T
-
-
-def local_weights(at, wind_mask, wind_speed, rows, cols):
-    map_total = wind_speed.shape[1] // MAPX
-
-    def kernel(*refs):
-        weights_kernel(map_total, (2, 1), *refs)
-
-    return pl.pallas_call(
-        kernel,
-        out_shape=(
-            jax.ShapeDtypeStruct((8, rows + 4 * MAPX), jnp.float32),
-            jax.ShapeDtypeStruct((8, cols + 2 * MAPX), jnp.float32),
-            jax.ShapeDtypeStruct((rows + 2 * MAPX, 8), jnp.float32),
-        ),
-        grid_spec=pltpu.PrefetchScalarGridSpec(
-            num_scalar_prefetch=1,
-            grid=(1,),
-            in_specs=[pl.BlockSpec(wind_mask.shape, lambda s, a: (0, 0))] * 2,
-            out_specs=(
-                pl.BlockSpec((8, rows + 4 * MAPX), lambda s, a: (0, 0)),
-                pl.BlockSpec((8, cols + 2 * MAPX), lambda s, a: (0, 0)),
-                pl.BlockSpec((rows + 2 * MAPX, 8), lambda s, a: (0, 0)),
-            ),
-        ),
-        compiler_params=SMALL,
-        cost_estimate=pl.CostEstimate(flops=1 << 16, bytes_accessed=1 << 20, transcendentals=0),
-        name="local_weights",
-    )(at, wind_mask, wind_speed)
-
-
-def select_kernel(rows, at_ref, cells_ref, scale_ref, weights_ref, out_ref, counts_ref):
-    each = cells_ref.shape[0]
-    window = weights_ref.shape[1]
+
+    each = cell_refs[0].shape[0]
+    window = rows_ref.shape[1]
     blocks = window // LANE
-    place = cells_ref[...] - (at_ref[0] * rows - 2 * MAPX)
-    block_of, lane_of = place >> 7, place & (LANE - 1)
     block_index = lax.broadcasted_iota(jnp.int32, (blocks, LANE), 0)
     lane_index = lax.broadcasted_iota(jnp.int32, (LANE, LANE), 0)
-    for o in range(each):
-        block_hit = jnp.where(block_of[o : o + 1] == block_index, 1.0, 0.0).astype(jnp.bfloat16)
-        lane_hit = jnp.where(lane_of[o : o + 1] == lane_index, 1.0, 0.0).astype(jnp.bfloat16)
-        counts_ref[o] = lax.dot_general(
-            block_hit, lane_hit, (((1,), (1,)), ((), ())), preferred_element_type=jnp.float32
-        )
-    scale = scale_ref[...]
+    for n, cells_ref in enumerate(cell_refs):
+        place = cells_ref[...] - (at_ref[2] * rows - 2 * MAPX)
+        block_of, lane_of = place >> 7, place & (LANE - 1)
+        for o in range(each):
+            block_hit = jnp.where(block_of[o : o + 1] == block_index, 1.0, 0.0).astype(jnp.bfloat16)
+            lane_hit = jnp.where(lane_of[o : o + 1] == lane_index, 1.0, 0.0).astype(jnp.bfloat16)
+            counts_ref[n * each + o] = lax.dot_general(
+                block_hit, lane_hit, (((1,), (1,)), ((), ())), preferred_element_type=jnp.float32
+            )
 
     def weights(k, m):
-        return weights_ref[k : k + 1, MAPX * m : MAPX * (m + 1)]
+        return rows_ref[k : k + 1, MAPX * m : MAPX * (m + 1)]
 
     maps = [
-        scale * jnp.concatenate([counts_ref[:, 2 * m, :], counts_ref[:, 2 * m + 1, :]], axis=1)
+        jnp.concatenate([counts_ref[:, 2 * m, :], counts_ref[:, 2 * m + 1, :]], axis=1)
         for m in range(window // MAPX)
     ]
-    for first in (1, 2):
+    for first in (0, 1):
         moved = []
         for m in range(1, len(maps) - 1):
-            t = m + first - 1
+            t = m + first
             here = maps[m]
             value = weights(0, t) * here + pltpu.roll(weights(1, t) * here, MAPX - 1, 1)
             value = value + pltpu.roll(weights(2, t) * here, 1, 1)
@@ -115,31 +95,48 @@
         out_ref[:, MAPX * m : MAPX * (m + 1)] = value
 
 
-def observation_rows(at, obs_cells, obs_scale, weights, rows, pieces):
+def prepare(at, wind_mask, wind_speed, obs_cells, rows, cols, pieces, group=4):
     obs_count, foot = obs_cells.shape
     each = obs_count // pieces
+    map_total = wind_speed.shape[1] // MAPX
 
     def kernel(*refs):
-        select_kernel(rows, *refs)
-
+        prepare_kernel(rows, map_total, *refs)
+
+    def fixed(shape):
+        return pl.BlockSpec(shape, lambda s, a: (0, 0))
+
+    col_shape = (8, cols + 2 * MAPX)
+    down_shape = (rows + 2 * MAPX, 8)
+    window = rows + 4 * MAPX
     return pl.pallas_call(
         kernel,
-        out_shape=jax.ShapeDtypeStruct((obs_count, rows), jnp.float32),
+        out_shape=(
+            jax.ShapeDtypeStruct((obs_count, rows), jnp.float32),
+            jax.ShapeDtypeStruct(col_shape, jnp.float32),
+            jax.ShapeDtypeStruct(down_shape, jnp.float32),
+        ),
         grid_spec=pltpu.PrefetchScalarGridSpec(
             num_scalar_prefetch=1,
-            grid=(pieces,),
-            in_specs=[
-                pl.BlockSpec((each, foot), lambda s, a: (s ^ a[2], 0)),
-                pl.BlockSpec((each, 1), lambda s, a: (s ^ a[2], 0)),
-                pl.BlockSpec(weights.shape, lambda s, a: (0, 0)),
+            grid=(pieces // group,),
+            in_specs=[fixed(wind_mask.shape), fixed(wind_speed.shape)]
+            + [
+                pl.BlockSpec((each, foot), lambda s, a, n=n: (s * group + n ^ a[2], 0))
+                for n in range(group)
             ],
-            out_specs=pl.BlockSpec((each, rows), lambda s, a: (s, 0)),
-            scratch_shapes=[pltpu.VMEM((each, weights.shape[1] // LANE, LANE), jnp.float32)],
-        ),
-        compiler_params=SMALL,
+            out_specs=(
+                pl.BlockSpec((each * group, rows), lambda s, a: (s, 0)),
+                fixed(col_shape),
+                fixed(down_shape),
+            ),
+            scratch_shapes=[
+                pltpu.VMEM((8, window), jnp.float32),
+                pltpu.VMEM((each * group, window // LANE, LANE), jnp.float32),
+            ],
+        ),
         cost_estimate=pl.CostEstimate(flops=1 << 27, bytes_accessed=1 << 21, transcendentals=0),
-        name="observation_rows",
-    )(at[2:], obs_cells, obs_scale[:, None], weights)
+        name="prepare",
+    )(at, wind_mask, wind_speed, *[obs_cells] * group)
 
 
 def step_cols(before, here, behind, weights):
@@ -250,8 +247,9 @@
 def move_rows(maps, update, weights):
     rows, cols = update.shape
 
-    def kernel(*refs):
-        rows_kernel(64, *refs)
+    def kernel(above, first, third, fourth, below, *refs):
+        halves = [ref.at[pl.ds(MAPX * k, MAPX), :] for ref in (first, below) for k in range(2)]
+        rows_kernel(64, above, *halves[:2], third, fourth, *halves[2:], *refs)
 
     def whole(array):
         return pl.BlockSpec(array.shape, lambda s: (0, 0))
@@ -323,51 +321,76 @@
     far_turning = lax.ppermute(covariance, "col", turning)
     near = lax.ppermute(covariance, "col", near_swap)
 
-    row_weights, col_weights, down_weights = local_weights(at, wind_mask, wind_speed, rows, cols)
-    select = observation_rows(at, obs_cells, obs_scale, row_weights, rows, row_parts)
+    select, col_weights, down_weights = prepare(
+        at, wind_mask, wind_speed, obs_cells, rows, cols, row_parts
+    )
     part = jnp.dot(select, covariance, precision=HIGH, preferred_element_type=jnp.float32)
 
-    total = part
-    for bit in (8, 4):
-        half = total.shape[0] // 2
-        total = total[:half] + lax.ppermute(total[half:], "row", across(bit))
-    each = total.shape[0] // 4
-    total = total[:each] + sum(
-        lax.ppermute(total[each * bit : each * (bit + 1)], "row", across(bit))
-        for bit in (1, 2, 3)
-    )
+    def sum_over(value, bits):
+        size = value.shape[0] // (len(bits) + 1)
+        total = value[:size]
+        for n, bit in enumerate(bits, 1):
+            piece = value[size * n : size * (n + 1)]
+            total = total + lax.ppermute(piece, "row", across(bit))
+        return total
+
+    def all_of(value, bits):
+        return [value] + [lax.ppermute(value, "row", across(bit)) for bit in bits]
+
+    total = sum_over(part, X_BITS)
+    total = sum_over(total, Z_BITS)
+    each = total.shape[0]
+
+    late = after(covariance, select)
+
+    def far_part(start, size):
+        return lax.ppermute(along(late, start, size, 0), "col", straight)
 
     piece_far = lax.ppermute(total, "col", far_swap)
-    order = (0, 3, 1, 2)
-    late = after(covariance, select)
-    far_straight = {n: lax.ppermute(along(late, MAPX * n, MAPX, 0), "col", straight) for n in order}
+    far_straight = {"far_up": far_part(0, 2 * MAPX)}
     piece_near = lax.ppermute(total, "col", near_swap)
     piece = move_cols(core, (total, 0), (piece_near, 0), [(piece_far, 0)], col_weights, each)
-    gathered = [lax.ppermute(piece, "row", across(bit)) for bit in (1, 2, 3)]
-
-    moved, halo = {}, {}
-    for n in order:
-        moved[n] = move_cols(
+    observed = all_of(piece, Z_BITS)
+    far_straight["far3"] = far_part(3 * MAPX, MAPX)
+    far_straight["far2"] = far_part(2 * MAPX, MAPX)
+
+    def move(name, block, size, *earlier):
+        return move_cols(
             core,
-            (covariance, n),
-            (near, n),
-            [(far_turning, n), (far_straight[n], 0)],
+            (covariance, block),
+            (near, block),
+            [(far_turning, block), (after(far_straight[name], *earlier), 0)],
             col_weights,
-            MAPX,
+            size,
         )
-        halo[n] = lax.ppermute(moved[n], "row", up if n < 2 else down)
-
-    observed = jnp.concatenate([after(piece, moved[2]), *gathered])
-    for bit in (4, 8):
-        observed = jnp.concatenate([observed, lax.ppermute(observed, "row", across(bit))])
+
+    moved_up = move("far_up", 0, 2 * MAPX)
+    halo_up = lax.ppermute(moved_up, "row", up)
+    observed = jnp.concatenate([after(observed[0], moved_up), *observed[1:]])
+    observed = jnp.concatenate(all_of(observed, X_BITS))
     index = jnp.arange(gain.shape[1], dtype=jnp.int32)
     reorder = (index[:, None] ^ (row_at * each)) == index[None, :]
     ordered_gain = jnp.dot(gain, reorder.astype(gain.dtype), preferred_element_type=jnp.float32)
-    update = jnp.dot(ordered_gain, observed, precision=HIGH, preferred_element_type=jnp.float32)
-
-    maps = [halo[3], moved[0], moved[1], moved[2], moved[3], halo[0], halo[1]]
-    result = move_rows(maps, update, down_weights)
-    return add_last(result, halo[2], down_weights)
+    ordered_scale = jnp.sum(jnp.where(reorder, obs_scale[:, None], 0.0), axis=0)
+    ordered_gain = ordered_gain * ordered_scale[None, :]
+
+    moved3 = move("far3", 3, MAPX)
+    halo3 = lax.ppermute(moved3, "row", down)
+    update = jnp.dot(
+        ordered_gain,
+        after(observed, moved3),
+        precision=HIGH,
+        preferred_element_type=jnp.float32,
+    )
+    moved2 = move("far2", 2, MAPX, update)
+    halo2 = lax.ppermute(moved2, "row", down)
+
+    result = move_rows([halo3, moved_up, moved2, moved3, halo_up], update, down_weights)
+    return add_last(result, halo2, down_weights)
+
+
+X_BITS = (4, 8, 12)
+Z_BITS = (1, 2, 3)
 
 
 def solution(mesh):

time: 198 us -> 198 us (level)
  the two profiles are of different devices: /device:TPU:223 before, /device:TPU:90 now
where the time goes in v2:
time: 198 us
  waiting for transfers between devices  100 us (51%)
  starting transfers between devices  64.2 us (32%)
  Pallas kernels  23.7 us (12%)
  matrix products  6.26 us (3%)
  local copies, waits for them, and re-layouts  2.04 us (1%)
    ppermute x6, waiting for transfers between devices, sum_over(): total = total + lax.ppermute(piece, 'row', across(bit))  45.2 us
    ppermute x1, waiting for transfers between devices, local(): halo3 = lax.ppermute(moved3, 'row', down)  25.3 us
    ppermute x6, starting transfers between devices, all_of(): return [value] + [lax.ppermute(value, 'row', across(bit)) for bit in bits]  19 us
    ppermute x6, starting transfers between devices, sum_over(): total = total + lax.ppermute(piece, 'row', across(bit))  17.8 us
    ppermute x6, waiting for transfers between devices, all_of(): return [value] + [lax.ppermute(value, 'row', across(bit)) for bit in bits]  13.4 us
    ppermute x1, starting transfers between devices, local(): far_turning = lax.ppermute(covariance, 'col', turning)  10 us
    ppermute x1, waiting for transfers between devices, local(): halo_up = lax.ppermute(moved_up, 'row', up)  8.72 us
    pallas_call x1, Pallas kernels, prepare(): pl.pallas_call(kernel, out_shape=(jax.ShapeDtypeStruct((obs_count, rows),...  8.65 us
  transfers between devices with their start and end apart: 22, of which 8 were waited for; matrix products, arithmetic and copies ran while one was open for 5% of the time, Pallas kernels for 11%

profile of v2, /device:TPU:90, one launch (start us, length us, event | category | flops | bytes accessed | tf_op | source)
XLA Modules:
  0.0 197.5 jit_solution(14517986507505917185)
XLA Ops:
  2.1 10.0 %collective-permute-start.1 = (f32[1024,512]{1,0:T(8,128)}, f32[1024,512]{1,0:T(8,128)}, u32[]{:S(2)}, u32[]{:S(2)}) collective-permute-start(f32[1024,512]{1,0:T(8,128)} %refs_1_.7), channel_id=1, source_target_pairs={{3,4},{4,3},{7,8},{8,7},{11,12},{12,11},{15,16},{16,15},{19,20},{2... | collective-permute-start | bytes 6291464 | tf_op jit(solution)/shard_map/ppermute | solution.py:321
  12.7 8.7 %prepare.1 = (f32[256,1024]{1,0:T(8,128)}, f32[8,1024]{1,0:T(8,128)}, f32[1536,8]{1,0:T(8,128)}) custom-call(s32[3]{0:T(128)} %pad_add_fusion.refs_0_, s32[2,16384]{1,0:T(2,128)} %refs_1_.4, f32[2,16384]{1,0:T(2,128)} %refs_2_.1, s32[256,128]{1,0:T(8,128)} %refs_6_.1, s32[256,128]{1,0:T(8,128)} %refs_6_.1, s32[256,128]{1,0:T(8,128)} %refs_6_.1, ...), custom_call_target="tpu_custom_call" | custom-call | flops 134217728 | bytes 2097152 | tf_op jit(solution)/shard_map/prepare/pallas_call | solution.py:112
  21.4 4.0 %fusion.10 = f32[256,512]{1,0:T(8,128)S(1)} fusion(f32[256,1024]{1,0:T(8,128)} %get-tuple-element.12, f32[1024,512]{1,0:T(8,128)} %refs_1_.7), kind=kOutput, calls=%fused_computation.27 | convolution fusion | flops 1610612736 | bytes 3670016 | tf_op jit(solution)/shard_map/dot_general | solution.py:327
  25.4 2.4 %collective-permute-start.6 = (f32[64,512]{1,0:T(8,128)S(1)}, f32[64,512]{1,0:T(8,128)S(1)}, u32[]{:S(2)}, u32[]{:S(2)}) collective-permute-start(f32[64,512]{1,0:T(8,128)S(1)} %get-tuple-element.21), channel_id=1, source_target_pairs={{0,128},{32,160},{64,192},{96,224},{128,0},{160,32},{192,64},{224,... | collective-permute-start | bytes 393224 | tf_op jit(solution)/shard_map/ppermute | solution.py:334
  27.9 4.3 %collective-permute-start.7 = (f32[64,512]{1,0:T(8,128)S(1)}, f32[64,512]{1,0:T(8,128)S(1)}, u32[]{:S(2)}, u32[]{:S(2)}) collective-permute-start(f32[64,512]{1,0:T(8,128)S(1)} %get-tuple-element.23), channel_id=1, source_target_pairs={{0,256},{32,288},{64,320},{96,352},{128,384},{160,416},{192,448},{... | collective-permute-start | bytes 393224 | tf_op jit(solution)/shard_map/ppermute | solution.py:334
  32.2 2.4 %collective-permute-start.8 = (f32[64,512]{1,0:T(8,128)S(1)}, f32[64,512]{1,0:T(8,128)S(1)}, u32[]{:S(2)}, u32[]{:S(2)}) collective-permute-start(f32[64,512]{1,0:T(8,128)S(1)} %get-tuple-element.22), channel_id=1, source_target_pairs={{0,384},{32,416},{64,448},{96,480},{128,256},{160,288},{192,320},{... | collective-permute-start | bytes 393224 | tf_op jit(solution)/shard_map/ppermute | solution.py:334
  39.1 4.3 %collective-permute-start.10 = (f32[16,512]{1,0:T(8,128)S(1)}, f32[16,512]{1,0:T(8,128)S(1)}, u32[]{:S(2)}, u32[]{:S(2)}) collective-permute-start(f32[16,512]{1,0:T(8,128)S(1)} %get-tuple-element.26), channel_id=1, source_target_pairs={{0,64},{32,96},{64,0},{96,32},{128,192},{160,224},{192,128},{224,1... | collective-permute-start | bytes 98312 | tf_op jit(solution)/shard_map/ppermute | solution.py:334
  46.2 40.3 %collective-permute-done.10 = f32[16,512]{1,0:T(8,128)S(1)} collective-permute-done((f32[16,512]{1,0:T(8,128)S(1)}, f32[16,512]{1,0:T(8,128)S(1)}, u32[]{:S(2)}, u32[]{:S(2)}) %collective-permute-start.10) | collective-permute-done | bytes 32800 | tf_op jit(solution)/shard_map/ppermute | solution.py:334
  86.5 2.4 %collective-permute-start.9 = (f32[16,512]{1,0:T(8,128)S(1)}, f32[16,512]{1,0:T(8,128)S(1)}, u32[]{:S(2)}, u32[]{:S(2)}) collective-permute-start(f32[16,512]{1,0:T(8,128)S(1)} %get-tuple-element.24), channel_id=1, source_target_pairs={{0,32},{32,0},{64,96},{96,64},{128,160},{160,128},{192,224},{224,1... | collective-permute-start | bytes 98312 | tf_op jit(solution)/shard_map/ppermute | solution.py:334
  88.9 3.4 %collective-permute-done.9 = f32[16,512]{1,0:T(8,128)S(1)} collective-permute-done((f32[16,512]{1,0:T(8,128)S(1)}, f32[16,512]{1,0:T(8,128)S(1)}, u32[]{:S(2)}, u32[]{:S(2)}) %collective-permute-start.9) | collective-permute-done | bytes 32800 | tf_op jit(solution)/shard_map/ppermute | solution.py:334
  97.0 7.3 %collective-permute-done.13.refs_3_ = f32[16,512]{1,0:T(8,128)S(1)} collective-permute-done((f32[16,512]{1,0:T(8,128)S(1)}, f32[16,512]{1,0:T(8,128)S(1)}, u32[]{:S(2)}, u32[]{:S(2)}) %collective-permute-start.13) | collective-permute-done | bytes 32800 | tf_op jit(solution)/shard_map/ppermute | solution.py:349
  107.6 5.1 %collective-permute-start.15 = (f32[16,512]{1,0:T(8,128)S(1)}, f32[16,512]{1,0:T(8,128)S(1)}, u32[]{:S(2)}, u32[]{:S(2)}) collective-permute-start(f32[16,512]{1,0:T(8,128)S(1)} %move_cols.6), channel_id=1, source_target_pairs={{0,64},{32,96},{64,0},{96,32},{128,192},{160,224},{192,128},{224,1... | collective-permute-start | bytes 98312 | tf_op jit(solution)/shard_map/ppermute | solution.py:338
  112.7 2.5 %collective-permute-start.16 = (f32[16,512]{1,0:T(8,128)S(1)}, f32[16,512]{1,0:T(8,128)S(1)}, u32[]{:S(2)}, u32[]{:S(2)}) collective-permute-start(f32[16,512]{1,0:T(8,128)S(1)} %move_cols.6), channel_id=1, source_target_pairs={{0,96},{32,64},{64,32},{96,0},{128,224},{160,192},{192,160},{224,1... | collective-permute-start | bytes 98312 | tf_op jit(solution)/shard_map/ppermute | solution.py:338
  115.2 4.0 %move_cols.5.first = f32[512,512]{1,0:T(8,128)S(1)} custom-call(s32[1]{0:T(128)} %bitcast.refs_0_, f32[1024,512]{1,0:T(8,128)S(1)} %copy-done.1, f32[1024,512]{1,0:T(8,128)} %collective-permute-done.refs_2_, f32[1024,512]{1,0:T(8,128)} %collective-permute-done.1.refs_3_, f32[512,512]{1,0:T(8,128)} %collective-permute-done.4.refs_4_, f32[8,1024]{1,0:T(8,128)S(1)} %copy-done.3), custom_call_target="tpu_custom_call" | custom-call | flops 7077888 | bytes 4194304 | tf_op jit(solution)/shard_map/move_cols/pallas_call | solution.py:188
  119.2 4.4 %collective-permute-done.15 = f32[16,512]{1,0:T(8,128)S(1)} collective-permute-done((f32[16,512]{1,0:T(8,128)S(1)}, f32[16,512]{1,0:T(8,128)S(1)}, u32[]{:S(2)}, u32[]{:S(2)}) %collective-permute-start.15) | collective-permute-done | bytes 32800 | tf_op jit(solution)/shard_map/ppermute | solution.py:338
  123.6 9.0 %collective-permute-done.16 = f32[16,512]{1,0:T(8,128)S(1)} collective-permute-done((f32[16,512]{1,0:T(8,128)S(1)}, f32[16,512]{1,0:T(8,128)S(1)}, u32[]{:S(2)}, u32[]{:S(2)}) %collective-permute-start.16) | collective-permute-done | bytes 32800 | tf_op jit(solution)/shard_map/ppermute | solution.py:338
  134.6 4.3 %collective-permute-start.18 = (f32[64,512]{1,0:T(8,128)S(1)}, f32[64,512]{1,0:T(8,128)S(1)}, u32[]{:S(2)}, u32[]{:S(2)}) collective-permute-start(f32[64,512]{1,0:T(8,128)S(1)} %get-tuple-element.27), channel_id=1, source_target_pairs={{0,256},{32,288},{64,320},{96,352},{128,384},{160,416},{192,448},{... | collective-permute-start | bytes 393224 | tf_op jit(solution)/shard_map/ppermute | solution.py:338
  139.4 2.8 %collective-permute-start.19 = (f32[64,512]{1,0:T(8,128)S(1)}, f32[64,512]{1,0:T(8,128)S(1)}, u32[]{:S(2)}, u32[]{:S(2)}) collective-permute-start(f32[64,512]{1,0:T(8,128)S(1)} %get-tuple-element.27), channel_id=1, source_target_pairs={{0,384},{32,416},{64,448},{96,480},{128,256},{160,288},{192,320},{... | collective-permute-start | bytes 393224 | tf_op jit(solution)/shard_map/ppermute | solution.py:338
  142.3 2.7 %collective-permute-start.20 = (f32[512,512]{1,0:T(8,128)S(1)}, f32[512,512]{1,0:T(8,128)S(1)}, u32[]{:S(2)}, u32[]{:S(2)}) collective-permute-start(f32[512,512]{1,0:T(8,128)S(1)} %move_cols.5.first), channel_id=1, source_target_pairs={{32,0},{64,32},{96,64},{128,96},{160,128},{192,160},{224,192},{256... | collective-permute-start | bytes 3145736 | tf_op jit(solution)/shard_map/ppermute | solution.py:368
  147.1 3.1 %collective-permute-start.3 = (f32[256,512]{1,0:T(8,128)S(1)}, f32[256,512]{1,0:T(8,128)S(1)}, u32[]{:S(2)}, u32[]{:S(2)}) collective-permute-start(f32[256,512]{1,0:T(8,128)S(1)} %move_cols.4.fourth), channel_id=1, source_target_pairs={{0,32},{32,64},{64,96},{96,128},{128,160},{160,192},{192,224},{224... | collective-permute-start | bytes 1572872 | tf_op jit(solution)/shard_map/ppermute | solution.py:378
  154.5 2.5 %collective-permute-start.21 = (f32[256,512]{1,0:T(8,128)S(1)}, f32[256,512]{1,0:T(8,128)S(1)}, u32[]{:S(2)}, u32[]{:S(2)}) collective-permute-start(f32[256,512]{1,0:T(8,128)S(1)} %move_cols.7.third), channel_id=1, source_target_pairs={{0,32},{32,64},{64,96},{96,128},{128,160},{160,192},{192,224},{224... | collective-permute-start | bytes 1572872 | tf_op jit(solution)/shard_map/ppermute | solution.py:386
  157.0 25.3 %collective-permute-done.3.above = f32[256,512]{1,0:T(8,128)S(1)} collective-permute-done((f32[256,512]{1,0:T(8,128)S(1)}, f32[256,512]{1,0:T(8,128)S(1)}, u32[]{:S(2)}, u32[]{:S(2)}) %collective-permute-start.3) | collective-permute-done | bytes 524320 | tf_op jit(solution)/shard_map/ppermute | solution.py:378
  182.2 8.7 %collective-permute-done.20.below = f32[512,512]{1,0:T(8,128)S(1)} collective-permute-done((f32[512,512]{1,0:T(8,128)S(1)}, f32[512,512]{1,0:T(8,128)S(1)}, u32[]{:S(2)}, u32[]{:S(2)}) %collective-permute-start.20) | collective-permute-done | bytes 1048608 | tf_op jit(solution)/shard_map/ppermute | solution.py:368
  191.0 4.7 %move_rows.1.result_ref = f32[1024,512]{1,0:T(8,128)} custom-call(f32[256,512]{1,0:T(8,128)S(1)} %collective-permute-done.3.above, f32[512,512]{1,0:T(8,128)S(1)} %move_cols.5.first, f32[256,512]{1,0:T(8,128)S(1)} %move_cols.7.third, f32[256,512]{1,0:T(8,128)S(1)} %move_cols.4.fourth, f32[512,512]{1,0:T(8,128)S(1)} %collective-permute-done.20.below, ...), custom_call_target="tpu_custom_call" | custom-call | flops 12582912 | bytes 8388608 | tf_op jit(solution)/shard_map/move_rows/pallas_call | solution.py:257
  (56 shorter events, 28.5 us)
Async XLA Ops:
  0.0 139.0 %copy-start = (bf16[1024,256]{1,0:T(8,128)(2,1)S(1)}, bf16[1024,256]{1,0:T(8,128)(2,1)}, u32[]{:S(2)}) copy-start(bf16[1024,256]{1,0:T(8,128)(2,1)} %param.11) | copy-start | bytes 1572868
  0.0 107.6 %collective-permute-start = (f32[1024,512]{1,0:T(8,128)}, f32[1024,512]{1,0:T(8,128)}, u32[]{:S(2)}, u32[]{:S(2)}) collective-permute-start(f32[1024,512]{1,0:T(8,128)} %refs_1_.7), channel_id=1, source_target_pairs={{0,1},{1,0},{2,3},{3,2},{4,5},{5,4},{6,7},{7,6},{8,9},{9,8},{10,11... | collective-permute-start | bytes 6291464 | tf_op jit(solution)/shard_map/ppermute | solution.py:322
  2.1 110.6 %collective-permute-start.1 = (f32[1024,512]{1,0:T(8,128)}, f32[1024,512]{1,0:T(8,128)}, u32[]{:S(2)}, u32[]{:S(2)}) collective-permute-start(f32[1024,512]{1,0:T(8,128)} %refs_1_.7), channel_id=1, source_target_pairs={{3,4},{4,3},{7,8},{8,7},{11,12},{12,11},{15,16},{16,15},{19,20},{2... | collective-permute-start | bytes 6291464 | tf_op jit(solution)/shard_map/ppermute | solution.py:321
  25.4 10.3 %collective-permute-start.6 = (f32[64,512]{1,0:T(8,128)S(1)}, f32[64,512]{1,0:T(8,128)S(1)}, u32[]{:S(2)}, u32[]{:S(2)}) collective-permute-start(f32[64,512]{1,0:T(8,128)S(1)} %get-tuple-element.21), channel_id=1, source_target_pairs={{0,128},{32,160},{64,192},{96,224},{128,0},{160,32},{192,64},{224,... | collective-permute-start | bytes 393224 | tf_op jit(solution)/shard_map/ppermute | solution.py:334
  27.9 9.7 %collective-permute-start.7 = (f32[64,512]{1,0:T(8,128)S(1)}, f32[64,512]{1,0:T(8,128)S(1)}, u32[]{:S(2)}, u32[]{:S(2)}) collective-permute-start(f32[64,512]{1,0:T(8,128)S(1)} %get-tuple-element.23), channel_id=1, source_target_pairs={{0,256},{32,288},{64,320},{96,352},{128,384},{160,416},{192,448},{... | collective-permute-start | bytes 393224 | tf_op jit(solution)/shard_map/ppermute | solution.py:334
  32.2 6.9 %collective-permute-start.8 = (f32[64,512]{1,0:T(8,128)S(1)}, f32[64,512]{1,0:T(8,128)S(1)}, u32[]{:S(2)}, u32[]{:S(2)}) collective-permute-start(f32[64,512]{1,0:T(8,128)S(1)} %get-tuple-element.22), channel_id=1, source_target_pairs={{0,384},{32,416},{64,448},{96,480},{128,256},{160,288},{192,320},{... | collective-permute-start | bytes 393224 | tf_op jit(solution)/shard_map/ppermute | solution.py:334
  35.7 69.4 %copy-start.3 = (f32[8,1024]{1,0:T(8,128)S(1)}, f32[8,1024]{1,0:T(8,128)}, u32[]{:S(2)}) copy-start(f32[8,1024]{1,0:T(8,128)} %get-tuple-element.14.refs_5_.refs_4_) | copy-start | bytes 98308
  35.7 69.5 %collective-permute-start.4 = (f32[512,512]{1,0:T(8,128)}, f32[512,512]{1,0:T(8,128)}, u32[]{:S(2)}, u32[]{:S(2)}) collective-permute-start(f32[512,512]{1,0:T(8,128)} %slice.34), channel_id=1, source_target_pairs={{1,2},{2,1},{5,6},{6,5},{9,10},{10,9},{13,14},{14,13},{17,18},{18,... | collective-permute-start | bytes 3145736 | tf_op jit(solution)/shard_map/ppermute | solution.py:347
  39.1 47.4 %collective-permute-start.10 = (f32[16,512]{1,0:T(8,128)S(1)}, f32[16,512]{1,0:T(8,128)S(1)}, u32[]{:S(2)}, u32[]{:S(2)}) collective-permute-start(f32[16,512]{1,0:T(8,128)S(1)} %get-tuple-element.26), channel_id=1, source_target_pairs={{0,64},{32,96},{64,0},{96,32},{128,192},{160,224},{192,128},{224,1... | collective-permute-start | bytes 98312 | tf_op jit(solution)/shard_map/ppermute | solution.py:334
  44.3 44.6 %collective-permute-start.11 = (f32[16,512]{1,0:T(8,128)S(1)}, f32[16,512]{1,0:T(8,128)S(1)}, u32[]{:S(2)}, u32[]{:S(2)}) collective-permute-start(f32[16,512]{1,0:T(8,128)S(1)} %get-tuple-element.25), channel_id=1, source_target_pairs={{0,96},{32,64},{64,32},{96,0},{128,224},{160,192},{192,160},{224,1... | collective-permute-start | bytes 98312 | tf_op jit(solution)/shard_map/ppermute | solution.py:334
  86.5 5.8 %collective-permute-start.9 = (f32[16,512]{1,0:T(8,128)S(1)}, f32[16,512]{1,0:T(8,128)S(1)}, u32[]{:S(2)}, u32[]{:S(2)}) collective-permute-start(f32[16,512]{1,0:T(8,128)S(1)} %get-tuple-element.24), channel_id=1, source_target_pairs={{0,32},{32,0},{64,96},{96,64},{128,160},{160,128},{192,224},{224,1... | collective-permute-start | bytes 98312 | tf_op jit(solution)/shard_map/ppermute | solution.py:334
  92.3 4.0 %collective-permute-start.12 = (f32[16,512]{1,0:T(8,128)S(1)}, f32[16,512]{1,0:T(8,128)S(1)}, u32[]{:S(2)}, u32[]{:S(2)}) collective-permute-start(f32[16,512]{1,0:T(8,128)S(1)} %fusion.6.refs_1_), channel_id=1, source_target_pairs={{0,1},{1,0},{2,3},{3,2},{4,5},{5,4},{6,7},{7,6},{8,9},{9,8},{10,11... | collective-permute-start | bytes 98312 | tf_op jit(solution)/shard_map/ppermute | solution.py:351
  94.2 10.1 %collective-permute-start.13 = (f32[16,512]{1,0:T(8,128)S(1)}, f32[16,512]{1,0:T(8,128)S(1)}, u32[]{:S(2)}, u32[]{:S(2)}) collective-permute-start(f32[16,512]{1,0:T(8,128)S(1)} %fusion.6.refs_1_), channel_id=1, source_target_pairs={{1,2},{2,1},{3,4},{4,3},{5,6},{6,5},{7,8},{8,7},{9,10},{10,9},{11,... | collective-permute-start | bytes 98312 | tf_op jit(solution)/shard_map/ppermute | solution.py:349
  96.3 43.1 %collective-permute-start.2 = (f32[256,512]{1,0:T(8,128)}, f32[256,512]{1,0:T(8,128)S(1)}, u32[]{:S(2)}, u32[]{:S(2)}) collective-permute-start(f32[256,512]{1,0:T(8,128)} %get-tuple-element.20), channel_id=1, source_target_pairs={{1,2},{2,1},{5,6},{6,5},{9,10},{10,9},{13,14},{14,13},{17,18},{18,... | collective-permute-start | bytes 1572872 | tf_op jit(solution)/shard_map/ppermute | solution.py:347
  104.4 47.9 %collective-permute-start.5 = (f32[256,512]{1,0:T(8,128)S(1)}, f32[256,512]{1,0:T(8,128)S(1)}, u32[]{:S(2)}, u32[]{:S(2)}) collective-permute-start(f32[256,512]{1,0:T(8,128)S(1)} %get-tuple-element.19), channel_id=1, source_target_pairs={{1,2},{2,1},{5,6},{6,5},{9,10},{10,9},{13,14},{14,13},{17,18},{18,... | collective-permute-start | bytes 1572872 | tf_op jit(solution)/shard_map/ppermute | solution.py:347
  105.3 13.9 %collective-permute-start.14 = (f32[16,512]{1,0:T(8,128)S(1)}, f32[16,512]{1,0:T(8,128)S(1)}, u32[]{:S(2)}, u32[]{:S(2)}) collective-permute-start(f32[16,512]{1,0:T(8,128)S(1)} %move_cols.6), channel_id=1, source_target_pairs={{0,32},{32,0},{64,96},{96,64},{128,160},{160,128},{192,224},{224,1... | collective-permute-start | bytes 98312 | tf_op jit(solution)/shard_map/ppermute | solution.py:338
  107.6 16.0 %collective-permute-start.15 = (f32[16,512]{1,0:T(8,128)S(1)}, f32[16,512]{1,0:T(8,128)S(1)}, u32[]{:S(2)}, u32[]{:S(2)}) collective-permute-start(f32[16,512]{1,0:T(8,128)S(1)} %move_cols.6), channel_id=1, source_target_pairs={{0,64},{32,96},{64,0},{96,32},{128,192},{160,224},{192,128},{224,1... | collective-permute-start | bytes 98312 | tf_op jit(solution)/shard_map/ppermute | solution.py:338
  112.7 19.9 %collective-permute-start.16 = (f32[16,512]{1,0:T(8,128)S(1)}, f32[16,512]{1,0:T(8,128)S(1)}, u32[]{:S(2)}, u32[]{:S(2)}) collective-permute-start(f32[16,512]{1,0:T(8,128)S(1)} %move_cols.6), channel_id=1, source_target_pairs={{0,96},{32,64},{64,32},{96,0},{128,224},{160,192},{192,160},{224,1... | collective-permute-start | bytes 98312 | tf_op jit(solution)/shard_map/ppermute | solution.py:338
  132.6 14.6 %collective-permute-start.17 = (f32[64,512]{1,0:T(8,128)S(1)}, f32[64,512]{1,0:T(8,128)S(1)}, u32[]{:S(2)}, u32[]{:S(2)}) collective-permute-start(f32[64,512]{1,0:T(8,128)S(1)} %get-tuple-element.27), channel_id=1, source_target_pairs={{0,128},{32,160},{64,192},{96,224},{128,0},{160,32},{192,64},{224,... | collective-permute-start | bytes 393224 | tf_op jit(solution)/shard_map/ppermute | solution.py:338
  134.6 15.7 %collective-permute-start.18 = (f32[64,512]{1,0:T(8,128)S(1)}, f32[64,512]{1,0:T(8,128)S(1)}, u32[]{:S(2)}, u32[]{:S(2)}) collective-permute-start(f32[64,512]{1,0:T(8,128)S(1)} %get-tuple-element.27), channel_id=1, source_target_pairs={{0,256},{32,288},{64,320},{96,352},{128,384},{160,416},{192,448},{... | collective-permute-start | bytes 393224 | tf_op jit(solution)/shard_map/ppermute | solution.py:338
  139.4 10.9 %collective-permute-start.19 = (f32[64,512]{1,0:T(8,128)S(1)}, f32[64,512]{1,0:T(8,128)S(1)}, u32[]{:S(2)}, u32[]{:S(2)}) collective-permute-start(f32[64,512]{1,0:T(8,128)S(1)} %get-tuple-element.27), channel_id=1, source_target_pairs={{0,384},{32,416},{64,448},{96,480},{128,256},{160,288},{192,320},{... | collective-permute-start | bytes 393224 | tf_op jit(solution)/shard_map/ppermute | solution.py:338
  142.3 48.7 %collective-permute-start.20 = (f32[512,512]{1,0:T(8,128)S(1)}, f32[512,512]{1,0:T(8,128)S(1)}, u32[]{:S(2)}, u32[]{:S(2)}) collective-permute-start(f32[512,512]{1,0:T(8,128)S(1)} %move_cols.5.first), channel_id=1, source_target_pairs={{32,0},{64,32},{96,64},{128,96},{160,128},{192,160},{224,192},{256... | collective-permute-start | bytes 3145736 | tf_op jit(solution)/shard_map/ppermute | solution.py:368
  147.1 35.1 %collective-permute-start.3 = (f32[256,512]{1,0:T(8,128)S(1)}, f32[256,512]{1,0:T(8,128)S(1)}, u32[]{:S(2)}, u32[]{:S(2)}) collective-permute-start(f32[256,512]{1,0:T(8,128)S(1)} %move_cols.4.fourth), channel_id=1, source_target_pairs={{0,32},{32,64},{64,96},{96,128},{128,160},{160,192},{192,224},{224... | collective-permute-start | bytes 1572872 | tf_op jit(solution)/shard_map/ppermute | solution.py:378
  154.5 41.2 %collective-permute-start.21 = (f32[256,512]{1,0:T(8,128)S(1)}, f32[256,512]{1,0:T(8,128)S(1)}, u32[]{:S(2)}, u32[]{:S(2)}) collective-permute-start(f32[256,512]{1,0:T(8,128)S(1)} %move_cols.7.third), channel_id=1, source_target_pairs={{0,32},{32,64},{64,96},{96,128},{128,160},{160,192},{192,224},{224... | collective-permute-start | bytes 1572872 | tf_op jit(solution)/shard_map/ppermute | solution.py:386
  (3 other events, 116.0 us)

commit v3 on v2

--- a/solution.py
+++ b/solution.py
@@ -17,10 +17,6 @@
 
 def after(value, *earlier):
     return lax.optimization_barrier((value,) + earlier)[0]
-
-
-def along(array, start, size, dim):
-    return lax.slice_in_dim(array, start, start + size, axis=dim)
 
 
 def weights_table(map_total, map_row, mask_ref, speed_ref):
@@ -146,9 +142,9 @@
     return result + weights[3] * before + weights[4] * behind
 
 
-def cols_kernel(inner, unroll, core_ref, here_ref, near_ref, *refs):
+def cols_kernel(inner, unroll, at_ref, here_ref, near_ref, *refs):
     far_refs, (weights_ref, out_ref) = refs[:-2], refs[-2:]
-    first = core_ref[0] == 0
+    first = at_ref[0] == 0
 
     def weights(m):
         return [weights_ref[k : k + 1, MAPX * m : MAPX * (m + 1)] for k in range(5)]
@@ -172,7 +168,7 @@
     lax.fori_loop(0, here_ref.shape[0] // inner, body, 0, unroll=unroll)
 
 
-def move_cols(core, here, near, fars, weights, rows):
+def move_cols(at, here, near, fars, weights, rows):
     cols = here[0].shape[1]
     tile = min(rows, 128)
     inner = min(rows, 64)
@@ -181,8 +177,11 @@
     def kernel(*refs):
         cols_kernel(inner, tile // inner, *refs)
 
-    def spec(at):
-        return pl.BlockSpec((tile, cols), lambda s, c: (at * steps + s, 0))
+    def spec(block):
+        if isinstance(block, str):
+            entry = HALVES[block]
+            return pl.BlockSpec((tile, cols), lambda s, a: (a[entry] * steps + s, 0))
+        return pl.BlockSpec((tile, cols), lambda s, a: (block * steps + s, 0))
 
     blocks = [here, near, *fars]
     return pl.pallas_call(
@@ -191,8 +190,8 @@
         grid_spec=pltpu.PrefetchScalarGridSpec(
             num_scalar_prefetch=1,
             grid=(steps,),
-            in_specs=[spec(at) for _, at in blocks]
-            + [pl.BlockSpec(weights.shape, lambda s, c: (0, 0))],
+            in_specs=[spec(block) for _, block in blocks]
+            + [pl.BlockSpec(weights.shape, lambda s, a: (0, 0))],
             out_specs=spec(0),
         ),
         compiler_params=SMALL,
@@ -200,103 +199,169 @@
             flops=27 * rows * cols, bytes_accessed=16 * rows * cols, transcendentals=0
         ),
         name="move_cols",
-    )(core, *[array for array, _ in blocks], weights)
-
-
-def rows_kernel(chunk, *refs):
-    maps, (update_ref, weights_ref, out_ref, once_ref) = refs[:7], refs[7:]
-
-    def step(source, base, before, behind, weights_at, emit):
-        def body(c, carry):
-            start = pl.multiple_of(c * chunk, chunk)
-            low = pl.multiple_of(jnp.maximum(start - 8, 0), 8)
-            high = pl.multiple_of(jnp.minimum(start + chunk, MAPX - 8), 8)
-            here = source[pl.ds(base + start, chunk), :]
-            wide = jnp.concatenate(
-                [source[pl.ds(base + low, 8), :], here, source[pl.ds(base + high, 8), :]], axis=0
-            )
-            weights = weights_ref[pl.ds(weights_at + start, chunk), :]
-            value = weights[:, 0:1] * here
-            value = value + weights[:, 1:2] * pltpu.roll(wide, 1, 0)[8 : 8 + chunk]
-            value = value + weights[:, 2:3] * pltpu.roll(wide, chunk + 15, 0)[8 : 8 + chunk]
-            if before is not None:
-                value = value + weights[:, 3:4] * before[0][pl.ds(before[1] + start, chunk), :]
-            value = value + weights[:, 4:5] * behind[0][pl.ds(behind[1] + start, chunk), :]
-            emit(start, value)
-            return carry
-
-        lax.fori_loop(0, MAPX // chunk, body, 0, unroll=MAPX // chunk)
-
-    for m in range(6):
-
-        def emit(start, value, m=m):
-            once_ref[pl.ds(MAPX * m + start, chunk), :] = value
-
-        step(maps[m], 0, (maps[m - 1], 0) if m > 0 else None, (maps[m + 1], 0), MAPX * m, emit)
-    for m in range(1, 5):
-
-        def emit(start, value, m=m):
-            rows = pl.ds(MAPX * (m - 1) + start, chunk)
-            out_ref[rows, :] = value - update_ref[rows, :]
-
-        step(
-            once_ref, MAPX * m, (once_ref, MAPX * (m - 1)), (once_ref, MAPX * (m + 1)), MAPX * m, emit
-        )
-
-
-def move_rows(maps, update, weights):
+    )(at, *[array for array, _ in blocks], weights)
+
+
+def load(parts, start, size):
+    value = None
+    for ref, base in parts:
+        part = ref[pl.ds(base + start, size), :]
+        value = part if value is None else value + part
+    return value
+
+
+def step_rows(chunk, before, here, behind, weights_ref, weights_at, emit):
+    def body(c, carry):
+        start = pl.multiple_of(c * chunk, chunk)
+        low = pl.multiple_of(jnp.maximum(start - 8, 0), 8)
+        high = pl.multiple_of(jnp.minimum(start + chunk, MAPX - 8), 8)
+        weights = weights_ref[pl.ds(weights_at + start, chunk), :]
+        terms = []
+        if here:
+            center = load(here, start, chunk)
+            wide = jnp.concatenate([load(here, low, 8), center, load(here, high, 8)], axis=0)
+            terms.append(weights[:, 0:1] * center)
+            terms.append(weights[:, 1:2] * pltpu.roll(wide, 1, 0)[8 : 8 + chunk])
+            terms.append(weights[:, 2:3] * pltpu.roll(wide, chunk + 15, 0)[8 : 8 + chunk])
+        if before:
+            terms.append(weights[:, 3:4] * load(before, start, chunk))
+        if behind:
+            terms.append(weights[:, 4:5] * load(behind, start, chunk))
+        value = terms[0]
+        for term in terms[1:]:
+            value = value + term
+        emit(start, value)
+        return carry
+
+    lax.fori_loop(0, MAPX // chunk, body, 0, unroll=MAPX // chunk)
+
+
+def two(*refs):
+    return [[(ref, MAPX * k) for ref in refs] for k in range(2)]
+
+
+def rows_kernel(chunk, at_ref, a_ref, b_ref, one_ref, other_ref, update_ref, weights_ref, out_ref, once_ref):
+    def run(maps):
+        once = {}
+        for m in range(1, 7):
+            at = MAPX * (m - 1)
+
+            def emit(start, value, at=at):
+                once_ref[pl.ds(at + start, chunk), :] = value
+
+            step_rows(chunk, maps[m - 1], maps[m], maps[m + 1], weights_ref, at, emit)
+            once[m] = [(once_ref, at)]
+        for m in range(2, 6):
+            at = MAPX * (m - 2)
+
+            def emit(start, value, at=at):
+                rows = pl.ds(at + start, chunk)
+                out_ref[rows, :] = value - update_ref[rows, :]
+
+            step_rows(chunk, once[m - 1], once[m], once[m + 1], weights_ref, MAPX * (m - 1), emit)
+
+    odd = at_ref[HALVES["first"]] == 1
+    none = [[], []]
+
+    @pl.when(odd)
+    def _():
+        run(none + two(b_ref) + two(a_ref) + two(one_ref, other_ref))
+
+    @pl.when(jnp.logical_not(odd))
+    def _():
+        run(two(one_ref, other_ref) + two(a_ref) + two(b_ref) + none)
+
+
+def move_rows(at, first, second, halo, update, weights):
     rows, cols = update.shape
 
-    def kernel(above, first, third, fourth, below, *refs):
-        halves = [ref.at[pl.ds(MAPX * k, MAPX), :] for ref in (first, below) for k in range(2)]
-        rows_kernel(64, above, *halves[:2], third, fourth, *halves[2:], *refs)
+    def kernel(*refs):
+        rows_kernel(64, *refs)
 
     def whole(array):
-        return pl.BlockSpec(array.shape, lambda s: (0, 0))
+        return pl.BlockSpec(array.shape, lambda s, a: (0, 0))
 
     return pl.pallas_call(
         kernel,
         out_shape=jax.ShapeDtypeStruct((rows, cols), jnp.float32),
-        grid=(1,),
-        in_specs=[whole(array) for array in (*maps, update, weights)],
-        out_specs=whole(update),
-        scratch_shapes=[pltpu.VMEM((rows + 2 * MAPX, cols), jnp.float32)],
+        grid_spec=pltpu.PrefetchScalarGridSpec(
+            num_scalar_prefetch=1,
+            grid=(1,),
+            in_specs=[whole(array) for array in (first, second, *halo, update, weights)],
+            out_specs=whole(update),
+            scratch_shapes=[pltpu.VMEM((rows + 2 * MAPX, cols), jnp.float32)],
+        ),
+        compiler_params=pltpu.CompilerParams(vmem_limit_bytes=20 << 20),
+        cost_estimate=pl.CostEstimate(
+            flops=24 * rows * cols, bytes_accessed=16 * rows * cols, transcendentals=0
+        ),
+        name="move_rows",
+    )(at, first, second, *halo, update, weights)
+
+
+def last_kernel(chunk, at_ref, result_ref, one_ref, other_ref, weights_ref, out_ref, once_ref):
+    near, far = [(once_ref, 0)], [(once_ref, MAPX)]
+
+    def into(at):
+        def emit(start, value):
+            once_ref[pl.ds(at + start, chunk), :] = value
+
+        return emit
+
+    def add(at):
+        def emit(start, value):
+            rows = pl.ds(at + start, chunk)
+            out_ref[rows, :] = result_ref[rows, :] + value
+
+        return emit
+
+    def step(before, here, behind, m, emit):
+        step_rows(chunk, before, here, behind, weights_ref, MAPX * (m - 1), emit)
+
+    odd = at_ref[HALVES["first"]] == 1
+    halo = two(one_ref, other_ref)
+
+    @pl.when(odd)
+    def _():
+        step(halo[0], halo[1], [], 1, into(MAPX))
+        step(halo[1], [], [], 2, into(0))
+        step(far, near, [], 2, add(0))
+        step(near, [], [], 3, add(MAPX))
+
+    @pl.when(jnp.logical_not(odd))
+    def _():
+        step([], halo[0], halo[1], 6, into(MAPX))
+        step([], [], halo[0], 5, into(0))
+        step([], near, far, 5, add(MAPX))
+        step([], [], near, 4, add(0))
+
+
+def add_last(at, result, halo, weights):
+    rows, cols = result.shape
+    tile = 256
+    block = pl.BlockSpec((rows // 2, tile), lambda s, a: (a[HALVES["second"]], s))
+    part = pl.BlockSpec((rows // 2, tile), lambda s, a: (0, s))
+
+    def kernel(*refs):
+        last_kernel(64, *refs)
+
+    return pl.pallas_call(
+        kernel,
+        out_shape=jax.ShapeDtypeStruct(result.shape, result.dtype),
+        grid_spec=pltpu.PrefetchScalarGridSpec(
+            num_scalar_prefetch=1,
+            grid=(cols // tile,),
+            in_specs=[block, part, part, pl.BlockSpec(weights.shape, lambda s, a: (0, 0))],
+            out_specs=block,
+            scratch_shapes=[pltpu.VMEM((2 * MAPX, tile), jnp.float32)],
+        ),
+        input_output_aliases={1: 0},
         compiler_params=SMALL,
         cost_estimate=pl.CostEstimate(
-            flops=24 * rows * cols, bytes_accessed=16 * rows * cols, transcendentals=0
-        ),
-        name="move_rows",
-    )(*maps, update, weights)
-
-
-def last_kernel(result_ref, halo_ref, weights_ref, before_ref, out_ref):
-    factor = weights_ref[:, 3:4] * before_ref[:, 3:4]
-    out_ref[...] = result_ref[...] + factor * halo_ref[...]
-
-
-def add_last(result, halo, weights):
-    cols = result.shape[1]
-    tile = 128
-    steps = MAPX // tile
-    block = pl.BlockSpec((tile, cols), lambda s: (s, 0))
-    return pl.pallas_call(
-        last_kernel,
-        out_shape=jax.ShapeDtypeStruct(result.shape, result.dtype),
-        grid=(steps,),
-        in_specs=[
-            block,
-            block,
-            pl.BlockSpec((tile, weights.shape[1]), lambda s: (steps + s, 0)),
-            pl.BlockSpec((tile, weights.shape[1]), lambda s: (s, 0)),
-        ],
-        out_specs=block,
-        input_output_aliases={0: 0},
-        compiler_params=SMALL,
-        cost_estimate=pl.CostEstimate(
-            flops=2 * MAPX * cols, bytes_accessed=12 * MAPX * cols, transcendentals=0
+            flops=10 * rows * cols, bytes_accessed=8 * rows * cols, transcendentals=0
         ),
         name="add_last",
-    )(result, halo, weights, weights)
+    )(at, result, *halo, weights)
 
 
 def local(covariance, wind_mask, wind_speed, obs_cells, obs_scale, gain):
@@ -306,20 +371,31 @@
     assert row_parts == 16 and rows == 4 * MAPX and cols == 2 * MAPX
     row_at = lax.axis_index("row")
     col_at = lax.axis_index("col")
-    down = [(i, i + 1) for i in range(row_parts - 1)]
-    up = [(i + 1, i) for i in range(row_parts - 1)]
     near_swap = [(j, j ^ 1) for j in range(col_parts)]
     far_swap = [(j, (j - 1 ^ 1) + 1) for j in range(1, col_parts - 1)]
     turning = [(a, b) for a, b in far_swap if a % 4 in (0, 3)]
     straight = [(a, b) for a, b in far_swap if a % 4 in (1, 2)]
-    core = (col_at % 2).reshape(1)
+    first, second = row_at % 2, 1 - row_at % 2
     at = jnp.stack([row_at * (rows // MAPX), col_at * (cols // MAPX), row_at])
+    place = jnp.stack([col_at % 2, first, second])
+    half = rows // 2
+
+    def row_swap(odd, kinds):
+        cells = [(i, (i - odd ^ 1) + odd) for i in range(odd, row_parts - odd)]
+        columns = [j for j in range(col_parts) if j % 4 in kinds]
+        return [(a * col_parts + j, b * col_parts + j) for a, b in cells for j in columns]
 
     def across(bit):
         return [(i, i ^ bit) for i in range(row_parts)]
 
     far_turning = lax.ppermute(covariance, "col", turning)
     near = lax.ppermute(covariance, "col", near_swap)
+
+    def far_part(number, source):
+        block = lax.dynamic_slice_in_dim(source, number * half, half, 0)
+        return lax.ppermute(block, "col", straight)
+
+    far_first = far_part(first, covariance)
 
     select, col_weights, down_weights = prepare(
         at, wind_mask, wind_speed, obs_cells, rows, cols, row_parts
@@ -341,54 +417,42 @@
     total = sum_over(total, Z_BITS)
     each = total.shape[0]
 
-    late = after(covariance, select)
-
-    def far_part(start, size):
-        return lax.ppermute(along(late, start, size, 0), "col", straight)
-
+    def move(block, *straight_parts):
+        fars = [(far_turning, block)] + [(part, 0) for part in straight_parts]
+        return move_cols(place, (covariance, block), (near, block), fars, col_weights, half)
+
+    def swap_rows(block, odd, kinds):
+        return lax.ppermute(block, ("row", "col"), row_swap(odd, kinds))
+
+    early_first = move("first")
+    early_second = move("second")
     piece_far = lax.ppermute(total, "col", far_swap)
-    far_straight = {"far_up": far_part(0, 2 * MAPX)}
+    far_second = far_part(second, after(covariance, early_second))
+    halo_first = [swap_rows(early_first, 1, (0, 3))]
+    halo_second = [swap_rows(early_second, 0, (0, 3))]
+
+    moved_first = move("first", far_first)
+    halo_first.append(swap_rows(moved_first, 1, (1, 2)))
     piece_near = lax.ppermute(total, "col", near_swap)
-    piece = move_cols(core, (total, 0), (piece_near, 0), [(piece_far, 0)], col_weights, each)
+    piece = move_cols(place, (total, 0), (piece_near, 0), [(piece_far, 0)], col_weights, each)
     observed = all_of(piece, Z_BITS)
-    far_straight["far3"] = far_part(3 * MAPX, MAPX)
-    far_straight["far2"] = far_part(2 * MAPX, MAPX)
-
-    def move(name, block, size, *earlier):
-        return move_cols(
-            core,
-            (covariance, block),
-            (near, block),
-            [(far_turning, block), (after(far_straight[name], *earlier), 0)],
-            col_weights,
-            size,
-        )
-
-    moved_up = move("far_up", 0, 2 * MAPX)
-    halo_up = lax.ppermute(moved_up, "row", up)
-    observed = jnp.concatenate([after(observed[0], moved_up), *observed[1:]])
+    moved_second = move("second", far_second)
+    halo_second.append(swap_rows(moved_second, 0, (1, 2)))
+
+    observed = jnp.concatenate([after(observed[0], moved_second), *observed[1:]])
     observed = jnp.concatenate(all_of(observed, X_BITS))
     index = jnp.arange(gain.shape[1], dtype=jnp.int32)
     reorder = (index[:, None] ^ (row_at * each)) == index[None, :]
     ordered_gain = jnp.dot(gain, reorder.astype(gain.dtype), preferred_element_type=jnp.float32)
     ordered_scale = jnp.sum(jnp.where(reorder, obs_scale[:, None], 0.0), axis=0)
     ordered_gain = ordered_gain * ordered_scale[None, :]
-
-    moved3 = move("far3", 3, MAPX)
-    halo3 = lax.ppermute(moved3, "row", down)
-    update = jnp.dot(
-        ordered_gain,
-        after(observed, moved3),
-        precision=HIGH,
-        preferred_element_type=jnp.float32,
-    )
-    moved2 = move("far2", 2, MAPX, update)
-    halo2 = lax.ppermute(moved2, "row", down)
-
-    result = move_rows([halo3, moved_up, moved2, moved3, halo_up], update, down_weights)
-    return add_last(result, halo2, down_weights)
-
-
+    update = jnp.dot(ordered_gain, observed, precision=HIGH, preferred_element_type=jnp.float32)
+
+    result = move_rows(place, moved_first, moved_second, halo_first, update, down_weights)
+    return add_last(place, result, halo_second, down_weights)
+
+
+HALVES = {"first": 1, "second": 2}
 X_BITS = (4, 8, 12)
 Z_BITS = (1, 2, 3)
 

time: 198 us -> 210 us (1.061)
  the two profiles are of different devices: /device:TPU:90 before, /device:TPU:30 now
where the time goes in v3:
time: 210 us; the launch traced here: 209 us
  waiting for transfers between devices  94.8 us (45%)
  starting transfers between devices  67.3 us (32%)
  Pallas kernels  36 us (17%)
  matrix products  5.44 us (3%)
  local copies, waits for them, and re-layouts  4.52 us (2%)
    ppermute x6, waiting for transfers between devices, all_of(): return [value] + [lax.ppermute(value, 'row', across(bit)) for bit in bits]  34.5 us
    ppermute x1, waiting for transfers between devices, local(): far_turning = lax.ppermute(covariance, 'col', turning)  30.2 us
    ppermute x6, waiting for transfers between devices, sum_over(): total = total + lax.ppermute(piece, 'row', across(bit))  21.8 us
    ppermute x6, starting transfers between devices, sum_over(): total = total + lax.ppermute(piece, 'row', across(bit))  21 us
    pallas_call x5, Pallas kernels, move_cols(): pl.pallas_call(kernel, out_shape=jax.ShapeDtypeStruct((rows, cols), jnp.f...  18.4 us
    ppermute x6, starting transfers between devices, all_of(): return [value] + [lax.ppermute(value, 'row', across(bit)) for bit in bits]  17.5 us
    ppermute x1, starting transfers between devices, local(): far_turning = lax.ppermute(covariance, 'col', turning)  10.9 us
    pallas_call x1, Pallas kernels, prepare(): pl.pallas_call(kernel, out_shape=(jax.ShapeDtypeStruct((obs_count, rows),...  8.65 us
  transfers between devices with their start and end apart: 22, of which 8 were waited for; matrix products, arithmetic and copies ran while one was open for 5% of the time, Pallas kernels for 16%

profile of v3, /device:TPU:30, one launch (start us, length us, event | category | flops | bytes accessed | tf_op | source)
XLA Modules:
  0.0 209.4 jit_solution(195616335124983195)
XLA Ops:
  2.2 10.9 %collective-permute-start.1 = (f32[1024,512]{1,0:T(8,128)}, f32[1024,512]{1,0:T(8,128)}, u32[]{:S(2)}, u32[]{:S(2)}) collective-permute-start(f32[1024,512]{1,0:T(8,128)} %refs_1_.9), channel_id=1, source_target_pairs={{3,4},{4,3},{7,8},{8,7},{11,12},{12,11},{15,16},{16,15},{19,20},{2... | collective-permute-start | bytes 6291464 | tf_op jit(solution)/shard_map/ppermute | solution.py:391
  17.7 8.7 %prepare.1 = (f32[256,1024]{1,0:T(8,128)}, f32[8,1024]{1,0:T(8,128)}, f32[1536,8]{1,0:T(8,128)}) custom-call(s32[3]{0:T(128)} %pad_add_fusion.1.refs_0_, s32[2,16384]{1,0:T(2,128)} %refs_1_.5, f32[2,16384]{1,0:T(2,128)} %refs_2_.1, s32[256,128]{1,0:T(8,128)} %refs_6_.1, s32[256,128]{1,0:T(8,128)} %refs_6_.1, s32[256,128]{1,0:T(8,128)} %refs_6_.1, ...), custom_call_target="tpu_custom_call" | custom-call | flops 134217728 | bytes 2097152 | tf_op jit(solution)/shard_map/prepare/pallas_call | solution.py:108
  26.4 3.2 %fusion.9 = f32[256,512]{1,0:T(8,128)S(1)} fusion(f32[256,1024]{1,0:T(8,128)} %get-tuple-element.12, f32[1024,512]{1,0:T(8,128)S(1)} %copy-done.1), kind=kOutput, calls=%fused_computation.29 | convolution fusion | flops 1610612736 | bytes 3670016 | tf_op jit(solution)/shard_map/dot_general | solution.py:403
  29.6 30.2 %collective-permute-done.1.refs_3_ = f32[1024,512]{1,0:T(8,128)} collective-permute-done((f32[1024,512]{1,0:T(8,128)}, f32[1024,512]{1,0:T(8,128)}, u32[]{:S(2)}, u32[]{:S(2)}) %collective-permute-start.1) | collective-permute-done | bytes 2097184 | tf_op jit(solution)/shard_map/ppermute | solution.py:391
  59.8 4.3 %move_cols.6 = f32[512,512]{1,0:T(8,128)S(1)} custom-call(s32[3]{0:T(128)S(1)} %pad_add_fusion.refs_0_, f32[1024,512]{1,0:T(8,128)S(1)} %copy-done.1, f32[1024,512]{1,0:T(8,128)} %collective-permute-done.refs_2_, f32[1024,512]{1,0:T(8,128)} %collective-permute-done.1.refs_3_, f32[8,1024]{1,0:T(8,128)S(1)} %copy-done.5), custom_call_target="tpu_custom_call" | custom-call | flops 7077888 | bytes 4194304 | tf_op jit(solution)/shard_map/move_cols/pallas_call | solution.py:187
  70.3 4.3 %collective-permute-start.7 = (f32[64,512]{1,0:T(8,128)S(1)}, f32[64,512]{1,0:T(8,128)S(1)}, u32[]{:S(2)}, u32[]{:S(2)}) collective-permute-start(f32[64,512]{1,0:T(8,128)S(1)} %get-tuple-element.17), channel_id=1, source_target_pairs={{0,256},{32,288},{64,320},{96,352},{128,384},{160,416},{192,448},{... | collective-permute-start | bytes 393224 | tf_op jit(solution)/shard_map/ppermute | solution.py:410
  74.6 3.1 %collective-permute-start.6 = (f32[64,512]{1,0:T(8,128)S(1)}, f32[64,512]{1,0:T(8,128)S(1)}, u32[]{:S(2)}, u32[]{:S(2)}) collective-permute-start(f32[64,512]{1,0:T(8,128)S(1)} %get-tuple-element.15), channel_id=1, source_target_pairs={{0,128},{32,160},{64,192},{96,224},{128,0},{160,32},{192,64},{224,... | collective-permute-start | bytes 393224 | tf_op jit(solution)/shard_map/ppermute | solution.py:410
  78.7 2.8 %collective-permute-done.6 = f32[64,512]{1,0:T(8,128)S(1)} collective-permute-done((f32[64,512]{1,0:T(8,128)S(1)}, f32[64,512]{1,0:T(8,128)S(1)}, u32[]{:S(2)}, u32[]{:S(2)}) %collective-permute-start.6) | collective-permute-done | bytes 131104 | tf_op jit(solution)/shard_map/ppermute | solution.py:410
  81.6 6.7 %collective-permute-start.11 = (f32[16,512]{1,0:T(8,128)S(1)}, f32[16,512]{1,0:T(8,128)S(1)}, u32[]{:S(2)}, u32[]{:S(2)}) collective-permute-start(f32[16,512]{1,0:T(8,128)S(1)} %get-tuple-element.19), channel_id=1, source_target_pairs={{0,96},{32,64},{64,32},{96,0},{128,224},{160,192},{192,160},{224,1... | collective-permute-start | bytes 98312 | tf_op jit(solution)/shard_map/ppermute | solution.py:410
  92.8 18.1 %collective-permute-done.10 = f32[16,512]{1,0:T(8,128)S(1)} collective-permute-done((f32[16,512]{1,0:T(8,128)S(1)}, f32[16,512]{1,0:T(8,128)S(1)}, u32[]{:S(2)}, u32[]{:S(2)}) %collective-permute-start.10) | collective-permute-done | bytes 32800 | tf_op jit(solution)/shard_map/ppermute | solution.py:410
  110.9 2.7 %collective-permute-start.12 = (f32[16,512]{1,0:T(8,128)S(1)}, f32[16,512]{1,0:T(8,128)S(1)}, u32[]{:S(2)}, u32[]{:S(2)}) collective-permute-start(f32[16,512]{1,0:T(8,128)S(1)} %fusion.6.refs_1_), channel_id=1, source_target_pairs={{0,1},{1,0},{2,3},{3,2},{4,5},{5,4},{6,7},{7,6},{8,9},{9,8},{10,11... | collective-permute-start | bytes 98312 | tf_op jit(solution)/shard_map/ppermute | solution.py:436
  115.6 8.2 %collective-permute-done.13.refs_3_ = f32[16,512]{1,0:T(8,128)S(1)} collective-permute-done((f32[16,512]{1,0:T(8,128)S(1)}, f32[16,512]{1,0:T(8,128)S(1)}, u32[]{:S(2)}, u32[]{:S(2)}) %collective-permute-start.13) | collective-permute-done | bytes 32800 | tf_op jit(solution)/shard_map/ppermute | solution.py:429
  126.6 4.6 %collective-permute-start.15 = (f32[16,512]{1,0:T(8,128)S(1)}, f32[16,512]{1,0:T(8,128)S(1)}, u32[]{:S(2)}, u32[]{:S(2)}) collective-permute-start(f32[16,512]{1,0:T(8,128)S(1)} %move_cols.9), channel_id=1, source_target_pairs={{0,64},{32,96},{64,0},{96,32},{128,192},{160,224},{192,128},{224,1... | collective-permute-start | bytes 98312 | tf_op jit(solution)/shard_map/ppermute | solution.py:414
  131.1 3.6 %collective-permute-start.16 = (f32[16,512]{1,0:T(8,128)S(1)}, f32[16,512]{1,0:T(8,128)S(1)}, u32[]{:S(2)}, u32[]{:S(2)}) collective-permute-start(f32[16,512]{1,0:T(8,128)S(1)} %move_cols.9), channel_id=1, source_target_pairs={{0,96},{32,64},{64,32},{96,0},{128,224},{160,192},{192,160},{224,1... | collective-permute-start | bytes 98312 | tf_op jit(solution)/shard_map/ppermute | solution.py:414
  134.8 4.3 %move_cols.8 = f32[512,512]{1,0:T(8,128)S(1)} custom-call(s32[3]{0:T(128)S(1)} %pad_add_fusion.refs_0_, f32[1024,512]{1,0:T(8,128)S(1)} %copy-done.1, f32[1024,512]{1,0:T(8,128)} %collective-permute-done.refs_2_, f32[1024,512]{1,0:T(8,128)} %collective-permute-done.1.refs_3_, f32[8,1024]{1,0:T(8,128)S(1)} %copy-done.5), custom_call_target="tpu_custom_call" | custom-call | flops 7077888 | bytes 4194304 | tf_op jit(solution)/shard_map/move_cols/pallas_call | solution.py:187
  141.1 4.5 %move_cols.5.refs_1_ = f32[512,512]{1,0:T(8,128)S(1)} custom-call(s32[3]{0:T(128)S(1)} %pad_add_fusion.refs_0_, f32[1024,512]{1,0:T(8,128)S(1)} %copy-done.1, f32[1024,512]{1,0:T(8,128)} %collective-permute-done.refs_2_, f32[1024,512]{1,0:T(8,128)} %collective-permute-done.1.refs_3_, f32[512,512]{1,0:T(8,128)} %collective-permute-done.2.refs_4_, ...), custom_call_target="tpu_custom_call" | custom-call | flops 7077888 | bytes 4194304 | tf_op jit(solution)/shard_map/move_cols/pallas_call | solution.py:187
  145.6 4.3 %collective-permute-start.4 = (f32[512,512]{1,0:T(8,128)S(1)}, f32[512,512]{1,0:T(8,128)S(1)}, u32[]{:S(2)}, u32[]{:S(2)}) collective-permute-start(f32[512,512]{1,0:T(8,128)S(1)} %move_cols.8), channel_id=1, source_target_pairs={{32,64},{35,67},{36,68},{39,71},{40,72},{43,75},{44,76},{47,79},{4... | collective-permute-start | bytes 3145736 | tf_op jit(solution)/shard_map/ppermute | solution.py:425
  149.9 4.5 %move_cols.7.refs_2_ = f32[512,512]{1,0:T(8,128)S(1)} custom-call(s32[3]{0:T(128)S(1)} %pad_add_fusion.refs_0_, f32[1024,512]{1,0:T(8,128)S(1)} %copy-done.1, f32[1024,512]{1,0:T(8,128)} %collective-permute-done.refs_2_, f32[1024,512]{1,0:T(8,128)} %collective-permute-done.1.refs_3_, f32[512,512]{1,0:T(8,128)} %collective-permute-done.3.refs_4_, ...), custom_call_target="tpu_custom_call" | custom-call | flops 7077888 | bytes 4194304 | tf_op jit(solution)/shard_map/move_cols/pallas_call | solution.py:187
  158.7 23.0 %collective-permute-done.17 = f32[64,512]{1,0:T(8,128)S(1)} collective-permute-done((f32[64,512]{1,0:T(8,128)S(1)}, f32[64,512]{1,0:T(8,128)S(1)}, u32[]{:S(2)}, u32[]{:S(2)}) %collective-permute-start.17) | collective-permute-done | bytes 131104 | tf_op jit(solution)/shard_map/ppermute | solution.py:414
  181.7 2.9 %collective-permute-start.18 = (f32[64,512]{1,0:T(8,128)S(1)}, f32[64,512]{1,0:T(8,128)S(1)}, u32[]{:S(2)}, u32[]{:S(2)}) collective-permute-start(f32[64,512]{1,0:T(8,128)S(1)} %get-tuple-element.21), channel_id=1, source_target_pairs={{0,256},{32,288},{64,320},{96,352},{128,384},{160,416},{192,448},{... | collective-permute-start | bytes 393224 | tf_op jit(solution)/shard_map/ppermute | solution.py:414
  185.0 5.4 %collective-permute-done.18 = f32[64,512]{1,0:T(8,128)S(1)} collective-permute-done((f32[64,512]{1,0:T(8,128)S(1)}, f32[64,512]{1,0:T(8,128)S(1)}, u32[]{:S(2)}, u32[]{:S(2)}) %collective-permute-start.18) | collective-permute-done | bytes 131104 | tf_op jit(solution)/shard_map/ppermute | solution.py:414
  192.4 6.1 %collective-permute-done.19 = f32[64,512]{1,0:T(8,128)S(1)} collective-permute-done((f32[64,512]{1,0:T(8,128)S(1)}, f32[64,512]{1,0:T(8,128)S(1)}, u32[]{:S(2)}, u32[]{:S(2)}) %collective-permute-start.19) | collective-permute-done | bytes 131104 | tf_op jit(solution)/shard_map/ppermute | solution.py:414
  200.4 5.5 %move_rows.1.refs_1_ = f32[1024,512]{1,0:T(8,128)} custom-call(s32[3]{0:T(128)S(1)} %pad_add_fusion.refs_0_, f32[512,512]{1,0:T(8,128)S(1)} %move_cols.5.refs_1_, f32[512,512]{1,0:T(8,128)S(1)} %move_cols.7.refs_2_, f32[512,512]{1,0:T(8,128)S(1)} %collective-permute-done.4.refs_3_, f32[512,512]{1,0:T(8,128)S(1)} %collective-permute-done.5.refs_4_, ...), custom_call_target="tpu_custom_call" | custom-call | flops 12582912 | bytes 8388608 | tf_op jit(solution)/shard_map/move_rows/pallas_call | solution.py:284
  205.9 3.5 %add_last.1 = f32[1024,512]{1,0:T(8,128)} custom-call(s32[3]{0:T(128)S(1)} %pad_add_fusion.refs_0_, f32[1024,512]{1,0:T(8,128)} %move_rows.1.refs_1_, f32[512,512]{1,0:T(8,128)S(1)} %collective-permute-done.20.refs_2_, f32[512,512]{1,0:T(8,128)S(1)} %collective-permute-done.21.refs_3_, f32[1536,8]{1,0:T(8,128)S(1)} %copy-done.2), custom_call_target="tpu_custom_call", output_to_operand_aliasing={{}: (1, {})} | custom-call | flops 5242880 | bytes 4194304 | tf_op jit(solution)/shard_map/add_last/pallas_call | solution.py:348
  (62 shorter events, 33.4 us)
Async XLA Ops:
  0.0 184.6 %copy-start = (bf16[1024,256]{1,0:T(8,128)(2,1)S(1)}, bf16[1024,256]{1,0:T(8,128)(2,1)}, u32[]{:S(2)}) copy-start(bf16[1024,256]{1,0:T(8,128)(2,1)} %param.11) | copy-start | bytes 1572868
  0.0 29.6 %collective-permute-start = (f32[1024,512]{1,0:T(8,128)}, f32[1024,512]{1,0:T(8,128)}, u32[]{:S(2)}, u32[]{:S(2)}) collective-permute-start(f32[1024,512]{1,0:T(8,128)} %refs_1_.9), channel_id=1, source_target_pairs={{0,1},{1,0},{2,3},{3,2},{4,5},{5,4},{6,7},{7,6},{8,9},{9,8},{10,11... | collective-permute-start | bytes 6291464 | tf_op jit(solution)/shard_map/ppermute | solution.py:392
  2.2 57.6 %collective-permute-start.1 = (f32[1024,512]{1,0:T(8,128)}, f32[1024,512]{1,0:T(8,128)}, u32[]{:S(2)}, u32[]{:S(2)}) collective-permute-start(f32[1024,512]{1,0:T(8,128)} %refs_1_.9), channel_id=1, source_target_pairs={{3,4},{4,3},{7,8},{8,7},{11,12},{12,11},{15,16},{16,15},{19,20},{2... | collective-permute-start | bytes 6291464 | tf_op jit(solution)/shard_map/ppermute | solution.py:391
  15.4 123.7 %collective-permute-start.2 = (f32[512,512]{1,0:T(8,128)}, f32[512,512]{1,0:T(8,128)}, u32[]{:S(2)}, u32[]{:S(2)}) collective-permute-start(f32[512,512]{1,0:T(8,128)} %constant_dynamic-slice_fusion.1), channel_id=1, source_target_pairs={{1,2},{2,1},{5,6},{6,5},{9,10},{10,9},{13,14},{14,13},{17,18},{18,... | collective-permute-start | bytes 3145736 | tf_op jit(solution)/shard_map/ppermute | solution.py:396
  26.4 33.4 %copy-start.5 = (f32[8,1024]{1,0:T(8,128)S(1)}, f32[8,1024]{1,0:T(8,128)}, u32[]{:S(2)}) copy-start(f32[8,1024]{1,0:T(8,128)} %get-tuple-element.10.refs_5_.refs_4_) | copy-start | bytes 98308
  66.2 79.4 %collective-permute-start.3 = (f32[512,512]{1,0:T(8,128)}, f32[512,512]{1,0:T(8,128)}, u32[]{:S(2)}, u32[]{:S(2)}) collective-permute-start(f32[512,512]{1,0:T(8,128)} %constant_dynamic-slice_fusion), channel_id=1, source_target_pairs={{1,2},{2,1},{5,6},{6,5},{9,10},{10,9},{13,14},{14,13},{17,18},{18,... | collective-permute-start | bytes 3145736 | tf_op jit(solution)/shard_map/ppermute | solution.py:396
  67.9 9.8 %collective-permute-start.8 = (f32[64,512]{1,0:T(8,128)S(1)}, f32[64,512]{1,0:T(8,128)S(1)}, u32[]{:S(2)}, u32[]{:S(2)}) collective-permute-start(f32[64,512]{1,0:T(8,128)S(1)} %get-tuple-element.16), channel_id=1, source_target_pairs={{0,384},{32,416},{64,448},{96,480},{128,256},{160,288},{192,320},{... | collective-permute-start | bytes 393224 | tf_op jit(solution)/shard_map/ppermute | solution.py:410
  70.3 8.4 %collective-permute-start.7 = (f32[64,512]{1,0:T(8,128)S(1)}, f32[64,512]{1,0:T(8,128)S(1)}, u32[]{:S(2)}, u32[]{:S(2)}) collective-permute-start(f32[64,512]{1,0:T(8,128)S(1)} %get-tuple-element.17), channel_id=1, source_target_pairs={{0,256},{32,288},{64,320},{96,352},{128,384},{160,416},{192,448},{... | collective-permute-start | bytes 393224 | tf_op jit(solution)/shard_map/ppermute | solution.py:410
  74.6 6.9 %collective-permute-start.6 = (f32[64,512]{1,0:T(8,128)S(1)}, f32[64,512]{1,0:T(8,128)S(1)}, u32[]{:S(2)}, u32[]{:S(2)}) collective-permute-start(f32[64,512]{1,0:T(8,128)S(1)} %get-tuple-element.15), channel_id=1, source_target_pairs={{0,128},{32,160},{64,192},{96,224},{128,0},{160,32},{192,64},{224,... | collective-permute-start | bytes 393224 | tf_op jit(solution)/shard_map/ppermute | solution.py:410
  81.6 11.2 %collective-permute-start.11 = (f32[16,512]{1,0:T(8,128)S(1)}, f32[16,512]{1,0:T(8,128)S(1)}, u32[]{:S(2)}, u32[]{:S(2)}) collective-permute-start(f32[16,512]{1,0:T(8,128)S(1)} %get-tuple-element.19), channel_id=1, source_target_pairs={{0,96},{32,64},{64,32},{96,0},{128,224},{160,192},{192,160},{224,1... | collective-permute-start | bytes 98312 | tf_op jit(solution)/shard_map/ppermute | solution.py:410
  88.3 22.6 %collective-permute-start.10 = (f32[16,512]{1,0:T(8,128)S(1)}, f32[16,512]{1,0:T(8,128)S(1)}, u32[]{:S(2)}, u32[]{:S(2)}) collective-permute-start(f32[16,512]{1,0:T(8,128)S(1)} %get-tuple-element.20), channel_id=1, source_target_pairs={{0,64},{32,96},{64,0},{96,32},{128,192},{160,224},{192,128},{224,1... | collective-permute-start | bytes 98312 | tf_op jit(solution)/shard_map/ppermute | solution.py:410
  90.3 20.6 %collective-permute-start.9 = (f32[16,512]{1,0:T(8,128)S(1)}, f32[16,512]{1,0:T(8,128)S(1)}, u32[]{:S(2)}, u32[]{:S(2)}) collective-permute-start(f32[16,512]{1,0:T(8,128)S(1)} %get-tuple-element.18), channel_id=1, source_target_pairs={{0,32},{32,0},{64,96},{96,64},{128,160},{160,128},{192,224},{224,1... | collective-permute-start | bytes 98312 | tf_op jit(solution)/shard_map/ppermute | solution.py:410
  110.9 4.7 %collective-permute-start.12 = (f32[16,512]{1,0:T(8,128)S(1)}, f32[16,512]{1,0:T(8,128)S(1)}, u32[]{:S(2)}, u32[]{:S(2)}) collective-permute-start(f32[16,512]{1,0:T(8,128)S(1)} %fusion.6.refs_1_), channel_id=1, source_target_pairs={{0,1},{1,0},{2,3},{3,2},{4,5},{5,4},{6,7},{7,6},{8,9},{9,8},{10,11... | collective-permute-start | bytes 98312 | tf_op jit(solution)/shard_map/ppermute | solution.py:436
  113.6 10.2 %collective-permute-start.13 = (f32[16,512]{1,0:T(8,128)S(1)}, f32[16,512]{1,0:T(8,128)S(1)}, u32[]{:S(2)}, u32[]{:S(2)}) collective-permute-start(f32[16,512]{1,0:T(8,128)S(1)} %fusion.6.refs_1_), channel_id=1, source_target_pairs={{1,2},{2,1},{3,4},{4,3},{5,6},{6,5},{7,8},{8,7},{9,10},{10,9},{11,... | collective-permute-start | bytes 98312 | tf_op jit(solution)/shard_map/ppermute | solution.py:429
  124.5 30.0 %collective-permute-start.14 = (f32[16,512]{1,0:T(8,128)S(1)}, f32[16,512]{1,0:T(8,128)S(1)}, u32[]{:S(2)}, u32[]{:S(2)}) collective-permute-start(f32[16,512]{1,0:T(8,128)S(1)} %move_cols.9), channel_id=1, source_target_pairs={{0,32},{32,0},{64,96},{96,64},{128,160},{160,128},{192,224},{224,1... | collective-permute-start | bytes 98312 | tf_op jit(solution)/shard_map/ppermute | solution.py:414
  126.6 28.7 %collective-permute-start.15 = (f32[16,512]{1,0:T(8,128)S(1)}, f32[16,512]{1,0:T(8,128)S(1)}, u32[]{:S(2)}, u32[]{:S(2)}) collective-permute-start(f32[16,512]{1,0:T(8,128)S(1)} %move_cols.9), channel_id=1, source_target_pairs={{0,64},{32,96},{64,0},{96,32},{128,192},{160,224},{192,128},{224,1... | collective-permute-start | bytes 98312 | tf_op jit(solution)/shard_map/ppermute | solution.py:414
  131.1 24.9 %collective-permute-start.16 = (f32[16,512]{1,0:T(8,128)S(1)}, f32[16,512]{1,0:T(8,128)S(1)}, u32[]{:S(2)}, u32[]{:S(2)}) collective-permute-start(f32[16,512]{1,0:T(8,128)S(1)} %move_cols.9), channel_id=1, source_target_pairs={{0,96},{32,64},{64,32},{96,0},{128,224},{160,192},{192,160},{224,1... | collective-permute-start | bytes 98312 | tf_op jit(solution)/shard_map/ppermute | solution.py:414
  139.1 66.8 %collective-permute-start.20 = (f32[512,512]{1,0:T(8,128)S(1)}, f32[512,512]{1,0:T(8,128)S(1)}, u32[]{:S(2)}, u32[]{:S(2)}) collective-permute-start(f32[512,512]{1,0:T(8,128)S(1)} %copy-done.4), channel_id=1, source_target_pairs={{0,32},{3,35},{4,36},{7,39},{8,40},{11,43},{12,44},{15,47},{16,48}... | collective-permute-start | bytes 3145736 | tf_op jit(solution)/shard_map/ppermute | solution.py:425
  145.6 54.8 %collective-permute-start.4 = (f32[512,512]{1,0:T(8,128)S(1)}, f32[512,512]{1,0:T(8,128)S(1)}, u32[]{:S(2)}, u32[]{:S(2)}) collective-permute-start(f32[512,512]{1,0:T(8,128)S(1)} %move_cols.8), channel_id=1, source_target_pairs={{32,64},{35,67},{36,68},{39,71},{40,72},{43,75},{44,76},{47,79},{4... | collective-permute-start | bytes 3145736 | tf_op jit(solution)/shard_map/ppermute | solution.py:425
  154.5 45.9 %collective-permute-start.5 = (f32[512,512]{1,0:T(8,128)S(1)}, f32[512,512]{1,0:T(8,128)S(1)}, u32[]{:S(2)}, u32[]{:S(2)}) collective-permute-start(f32[512,512]{1,0:T(8,128)S(1)} %move_cols.5.refs_1_), channel_id=1, source_target_pairs={{33,65},{34,66},{37,69},{38,70},{41,73},{42,74},{45,77},{46,78},{4... | collective-permute-start | bytes 3145736 | tf_op jit(solution)/shard_map/ppermute | solution.py:425
  155.3 50.7 %collective-permute-start.21 = (f32[512,512]{1,0:T(8,128)S(1)}, f32[512,512]{1,0:T(8,128)S(1)}, u32[]{:S(2)}, u32[]{:S(2)}) collective-permute-start(f32[512,512]{1,0:T(8,128)S(1)} %move_cols.7.refs_2_), channel_id=1, source_target_pairs={{1,33},{2,34},{5,37},{6,38},{9,41},{10,42},{13,45},{14,46},{17,49}... | collective-permute-start | bytes 3145736 | tf_op jit(solution)/shard_map/ppermute | solution.py:425
  156.0 25.6 %collective-permute-start.17 = (f32[64,512]{1,0:T(8,128)S(1)}, f32[64,512]{1,0:T(8,128)S(1)}, u32[]{:S(2)}, u32[]{:S(2)}) collective-permute-start(f32[64,512]{1,0:T(8,128)S(1)} %get-tuple-element.21), channel_id=1, source_target_pairs={{0,128},{32,160},{64,192},{96,224},{128,0},{160,32},{192,64},{224,... | collective-permute-start | bytes 393224 | tf_op jit(solution)/shard_map/ppermute | solution.py:414
  181.7 8.8 %collective-permute-start.18 = (f32[64,512]{1,0:T(8,128)S(1)}, f32[64,512]{1,0:T(8,128)S(1)}, u32[]{:S(2)}, u32[]{:S(2)}) collective-permute-start(f32[64,512]{1,0:T(8,128)S(1)} %get-tuple-element.21), channel_id=1, source_target_pairs={{0,256},{32,288},{64,320},{96,352},{128,384},{160,416},{192,448},{... | collective-permute-start | bytes 393224 | tf_op jit(solution)/shard_map/ppermute | solution.py:414
  190.5 8.1 %collective-permute-start.19 = (f32[64,512]{1,0:T(8,128)S(1)}, f32[64,512]{1,0:T(8,128)S(1)}, u32[]{:S(2)}, u32[]{:S(2)}) collective-permute-start(f32[64,512]{1,0:T(8,128)S(1)} %get-tuple-element.21), channel_id=1, source_target_pairs={{0,384},{32,416},{64,448},{96,480},{128,256},{160,288},{192,320},{... | collective-permute-start | bytes 393224 | tf_op jit(solution)/shard_map/ppermute | solution.py:414
  (5 other events, 63.0 us)

commit v4 on v3

--- a/solution.py
+++ b/solution.py
@@ -168,20 +168,28 @@
     lax.fori_loop(0, here_ref.shape[0] // inner, body, 0, unroll=unroll)
 
 
-def move_cols(at, here, near, fars, weights, rows):
+def move_cols(at, here, near, fars, weights, rows, only=None):
     cols = here[0].shape[1]
     tile = min(rows, 128)
     inner = min(rows, 64)
     steps = rows // tile
 
-    def kernel(*refs):
-        cols_kernel(inner, tile // inner, *refs)
+    def kernel(at_ref, *refs):
+        if only is None:
+            cols_kernel(inner, tile // inner, at_ref, *refs)
+        else:
+
+            @pl.when(at_ref[HALVES[only]] == 1)
+            def _():
+                cols_kernel(inner, tile // inner, at_ref, *refs)
 
     def spec(block):
-        if isinstance(block, str):
-            entry = HALVES[block]
-            return pl.BlockSpec((tile, cols), lambda s, a: (a[entry] * steps + s, 0))
-        return pl.BlockSpec((tile, cols), lambda s, a: (block * steps + s, 0))
+        def index(s, a):
+            at_block = a[HALVES[block]] if isinstance(block, str) else block
+            row = at_block * steps + s
+            return (row if only is None else row * a[HALVES[only]], 0)
+
+        return pl.BlockSpec((tile, cols), index)
 
     blocks = [here, near, *fars]
     return pl.pallas_call(
@@ -377,7 +385,8 @@
     straight = [(a, b) for a, b in far_swap if a % 4 in (1, 2)]
     first, second = row_at % 2, 1 - row_at % 2
     at = jnp.stack([row_at * (rows // MAPX), col_at * (cols // MAPX), row_at])
-    place = jnp.stack([col_at % 2, first, second])
+    turns = jnp.where((col_at % 4 == 0) | (col_at % 4 == 3), 1, 0)
+    place = jnp.stack([col_at % 2, first, second, turns])
     half = rows // 2
 
     def row_swap(odd, kinds):
@@ -395,7 +404,6 @@
         block = lax.dynamic_slice_in_dim(source, number * half, half, 0)
         return lax.ppermute(block, "col", straight)
 
-    far_first = far_part(first, covariance)
 
     select, col_weights, down_weights = prepare(
         at, wind_mask, wind_speed, obs_cells, rows, cols, row_parts
@@ -417,29 +425,29 @@
     total = sum_over(total, Z_BITS)
     each = total.shape[0]
 
-    def move(block, *straight_parts):
+    def move(block, *straight_parts, only=None):
         fars = [(far_turning, block)] + [(part, 0) for part in straight_parts]
-        return move_cols(place, (covariance, block), (near, block), fars, col_weights, half)
+        return move_cols(place, (covariance, block), (near, block), fars, col_weights, half, only)
 
     def swap_rows(block, odd, kinds):
         return lax.ppermute(block, ("row", "col"), row_swap(odd, kinds))
 
-    early_first = move("first")
-    early_second = move("second")
     piece_far = lax.ppermute(total, "col", far_swap)
-    far_second = far_part(second, after(covariance, early_second))
-    halo_first = [swap_rows(early_first, 1, (0, 3))]
-    halo_second = [swap_rows(early_second, 0, (0, 3))]
-
-    moved_first = move("first", far_first)
-    halo_first.append(swap_rows(moved_first, 1, (1, 2)))
+    far_first = far_part(first, after(covariance, select))
     piece_near = lax.ppermute(total, "col", near_swap)
     piece = move_cols(place, (total, 0), (piece_near, 0), [(piece_far, 0)], col_weights, each)
     observed = all_of(piece, Z_BITS)
-    moved_second = move("second", far_second)
-    halo_second.append(swap_rows(moved_second, 0, (1, 2)))
-
-    observed = jnp.concatenate([after(observed[0], moved_second), *observed[1:]])
+    far_second = far_part(second, after(covariance, select))
+
+    early_first = move("first", only="turns")
+    halo_first = [swap_rows(early_first, 1, (0, 3))]
+    early_second = move("second", only="turns")
+    halo_second = [swap_rows(early_second, 0, (0, 3))]
+
+    moved_first = move("first", far_first)
+    halo_first.append(swap_rows(moved_first, 1, (1, 2)))
+
+    observed = jnp.concatenate([after(observed[0], moved_first), *observed[1:]])
     observed = jnp.concatenate(all_of(observed, X_BITS))
     index = jnp.arange(gain.shape[1], dtype=jnp.int32)
     reorder = (index[:, None] ^ (row_at * each)) == index[None, :]
@@ -448,11 +456,14 @@
     ordered_gain = ordered_gain * ordered_scale[None, :]
     update = jnp.dot(ordered_gain, observed, precision=HIGH, preferred_element_type=jnp.float32)
 
+    moved_second = move("second", after(far_second, update))
+    halo_second.append(swap_rows(moved_second, 0, (1, 2)))
+
     result = move_rows(place, moved_first, moved_second, halo_first, update, down_weights)
     return add_last(place, result, halo_second, down_weights)
 
 
-HALVES = {"first": 1, "second": 2}
+HALVES = {"first": 1, "second": 2, "turns": 3}
 X_BITS = (4, 8, 12)
 Z_BITS = (1, 2, 3)
 

time: 210 us -> 195 us (0.929)
  the two profiles are of different devices: /device:TPU:30 before, /device:TPU:37 now
where the time goes in v4:
time: 195 us; the launch traced here: 194 us
  waiting for transfers between devices  85.7 us (44%)
  starting transfers between devices  66.3 us (34%)
  Pallas kernels  30.3 us (16%)
  matrix products  6.28 us (3%)
  local copies, waits for them, and re-layouts  3.08 us (2%)
    ppermute x6, waiting for transfers between devices, sum_over(): total = total + lax.ppermute(piece, 'row', across(bit))  40 us
    ppermute x4, waiting for transfers between devices, swap_rows(): return lax.ppermute(block, ('row', 'col'), row_swap(odd, kinds))  29.9 us
    ppermute x6, starting transfers between devices, all_of(): return [value] + [lax.ppermute(value, 'row', across(bit)) for bit in bits]  18.3 us
    ppermute x6, starting transfers between devices, sum_over(): total = total + lax.ppermute(piece, 'row', across(bit))  18 us
    pallas_call x5, Pallas kernels, move_cols(): pl.pallas_call(kernel, out_shape=jax.ShapeDtypeStruct((rows, cols), jnp.f...  12.7 us
    ppermute x6, waiting for transfers between devices, all_of(): return [value] + [lax.ppermute(value, 'row', across(bit)) for bit in bits]  11 us
    ppermute x1, starting transfers between devices, local(): near = lax.ppermute(covariance, 'col', near_swap)  10.8 us
    pallas_call x1, Pallas kernels, prepare(): pl.pallas_call(kernel, out_shape=(jax.ShapeDtypeStruct((obs_count, rows),...  8.65 us
  transfers between devices with their start and end apart: 22, of which 6 were waited for; matrix products, arithmetic and copies ran while one was open for 5% of the time, Pallas kernels for 14%

profile of v4, /device:TPU:37, one launch (start us, length us, event | category | flops | bytes accessed | tf_op | source)
XLA Modules:
  0.0 193.9 jit_solution(11411457534834358526)
XLA Ops:
  2.1 10.8 %collective-permute-start = (f32[1024,512]{1,0:T(8,128)}, f32[1024,512]{1,0:T(8,128)}, u32[]{:S(2)}, u32[]{:S(2)}) collective-permute-start(f32[1024,512]{1,0:T(8,128)} %refs_0_.7), channel_id=1, source_target_pairs={{0,1},{1,0},{2,3},{3,2},{4,5},{5,4},{6,7},{7,6},{8,9},{9,8},{10,11... | collective-permute-start | bytes 6291464 | tf_op jit(solution)/shard_map/ppermute | solution.py:401
  13.6 8.7 %prepare.1 = (f32[256,1024]{1,0:T(8,128)}, f32[8,1024]{1,0:T(8,128)}, f32[1536,8]{1,0:T(8,128)}) custom-call(s32[3]{0:T(128)} %pad_add_fusion.1.refs_0_, s32[2,16384]{1,0:T(2,128)} %refs_1_.1, f32[2,16384]{1,0:T(2,128)} %refs_2_.1, s32[256,128]{1,0:T(8,128)} %refs_6_.1, s32[256,128]{1,0:T(8,128)} %refs_6_.1, s32[256,128]{1,0:T(8,128)} %refs_6_.1, ...), custom_call_target="tpu_custom_call" | custom-call | flops 134217728 | bytes 2097152 | tf_op jit(solution)/shard_map/prepare/pallas_call | solution.py:108
  22.2 4.0 %fusion.9 = f32[256,512]{1,0:T(8,128)S(1)} fusion(f32[256,1024]{1,0:T(8,128)} %get-tuple-element.11, f32[1024,512]{1,0:T(8,128)} %refs_0_.7), kind=kOutput, calls=%fused_computation.29 | convolution fusion | flops 1610612736 | bytes 3670016 | tf_op jit(solution)/shard_map/dot_general | solution.py:411
  27.0 2.8 %collective-permute-start.4 = (f32[64,512]{1,0:T(8,128)}, f32[64,512]{1,0:T(8,128)S(1)}, u32[]{:S(2)}, u32[]{:S(2)}) collective-permute-start(f32[64,512]{1,0:T(8,128)} %get-tuple-element.19), channel_id=1, source_target_pairs={{0,128},{32,160},{64,192},{96,224},{128,0},{160,32},{192,64},{224,... | collective-permute-start | bytes 393224 | tf_op jit(solution)/shard_map/ppermute | solution.py:418
  31.8 4.2 %collective-permute-start.5 = (f32[64,512]{1,0:T(8,128)}, f32[64,512]{1,0:T(8,128)}, u32[]{:S(2)}, u32[]{:S(2)}) collective-permute-start(f32[64,512]{1,0:T(8,128)} %get-tuple-element.21), channel_id=1, source_target_pairs={{0,256},{32,288},{64,320},{96,352},{128,384},{160,416},{192,448},{... | collective-permute-start | bytes 393224 | tf_op jit(solution)/shard_map/ppermute | solution.py:418
  37.6 3.1 %collective-permute-start.2 = (f32[512,512]{1,0:T(8,128)}, f32[512,512]{1,0:T(8,128)}, u32[]{:S(2)}, u32[]{:S(2)}) collective-permute-start(f32[512,512]{1,0:T(8,128)} %get-tuple-element.18), channel_id=1, source_target_pairs={{1,2},{2,1},{5,6},{6,5},{9,10},{10,9},{13,14},{14,13},{17,18},{18,... | collective-permute-start | bytes 3145736 | tf_op jit(solution)/shard_map/ppermute | solution.py:405
  42.4 3.1 %collective-permute-start.7 = (f32[16,512]{1,0:T(8,128)S(1)}, f32[16,512]{1,0:T(8,128)S(1)}, u32[]{:S(2)}, u32[]{:S(2)}) collective-permute-start(f32[16,512]{1,0:T(8,128)S(1)} %get-tuple-element.22), channel_id=1, source_target_pairs={{0,32},{32,0},{64,96},{96,64},{128,160},{160,128},{192,224},{224,1... | collective-permute-start | bytes 98312 | tf_op jit(solution)/shard_map/ppermute | solution.py:418
  45.5 4.0 %collective-permute-start.9 = (f32[16,512]{1,0:T(8,128)S(1)}, f32[16,512]{1,0:T(8,128)S(1)}, u32[]{:S(2)}, u32[]{:S(2)}) collective-permute-start(f32[16,512]{1,0:T(8,128)S(1)} %get-tuple-element.23), channel_id=1, source_target_pairs={{0,96},{32,64},{64,32},{96,0},{128,224},{160,192},{192,160},{224,1... | collective-permute-start | bytes 98312 | tf_op jit(solution)/shard_map/ppermute | solution.py:418
  49.5 36.5 %collective-permute-done.7 = f32[16,512]{1,0:T(8,128)S(1)} collective-permute-done((f32[16,512]{1,0:T(8,128)S(1)}, f32[16,512]{1,0:T(8,128)S(1)}, u32[]{:S(2)}, u32[]{:S(2)}) %collective-permute-start.7) | collective-permute-done | bytes 32800 | tf_op jit(solution)/shard_map/ppermute | solution.py:418
  88.2 3.4 %collective-permute-done.8 = f32[16,512]{1,0:T(8,128)S(1)} collective-permute-done((f32[16,512]{1,0:T(8,128)S(1)}, f32[16,512]{1,0:T(8,128)S(1)}, u32[]{:S(2)}, u32[]{:S(2)}) %collective-permute-start.8) | collective-permute-done | bytes 32800 | tf_op jit(solution)/shard_map/ppermute | solution.py:418
  91.6 2.4 %collective-permute-start.11 = (f32[16,512]{1,0:T(8,128)S(1)}, f32[16,512]{1,0:T(8,128)S(1)}, u32[]{:S(2)}, u32[]{:S(2)}) collective-permute-start(f32[16,512]{1,0:T(8,128)S(1)} %fusion.6.refs_0_), channel_id=1, source_target_pairs={{1,2},{2,1},{3,4},{4,3},{5,6},{6,5},{7,8},{8,7},{9,10},{10,9},{11,... | collective-permute-start | bytes 98312 | tf_op jit(solution)/shard_map/ppermute | solution.py:435
  96.0 4.7 %collective-permute-done.11.refs_2_ = f32[16,512]{1,0:T(8,128)S(1)} collective-permute-done((f32[16,512]{1,0:T(8,128)S(1)}, f32[16,512]{1,0:T(8,128)S(1)}, u32[]{:S(2)}, u32[]{:S(2)}) %collective-permute-start.11) | collective-permute-done | bytes 32800 | tf_op jit(solution)/shard_map/ppermute | solution.py:435
  105.8 3.3 %collective-permute-start.13 = (f32[16,512]{1,0:T(8,128)S(1)}, f32[16,512]{1,0:T(8,128)S(1)}, u32[]{:S(2)}, u32[]{:S(2)}) collective-permute-start(f32[16,512]{1,0:T(8,128)S(1)} %move_cols.6), channel_id=1, source_target_pairs={{0,64},{32,96},{64,0},{96,32},{128,192},{160,224},{192,128},{224,1... | collective-permute-start | bytes 98312 | tf_op jit(solution)/shard_map/ppermute | solution.py:422
  109.1 4.1 %collective-permute-start.12 = (f32[16,512]{1,0:T(8,128)S(1)}, f32[16,512]{1,0:T(8,128)S(1)}, u32[]{:S(2)}, u32[]{:S(2)}) collective-permute-start(f32[16,512]{1,0:T(8,128)S(1)} %move_cols.6), channel_id=1, source_target_pairs={{0,32},{32,0},{64,96},{96,64},{128,160},{160,128},{192,224},{224,1... | collective-permute-start | bytes 98312 | tf_op jit(solution)/shard_map/ppermute | solution.py:422
  113.2 4.5 %move_cols.5.refs_1_ = f32[512,512]{1,0:T(8,128)S(1)} custom-call(s32[4]{0:T(128)S(1)} %pad_add_fusion.at_ref.refs_0_, f32[1024,512]{1,0:T(8,128)S(1)} %copy-done.1, f32[1024,512]{1,0:T(8,128)} %collective-permute-done.refs_1_, f32[1024,512]{1,0:T(8,128)} %collective-permute-done.1.refs_2_, f32[512,512]{1,0:T(8,128)} %collective-permute-done.2.refs_3_, ...), custom_call_target="tpu_custom_call" | custom-call | flops 7077888 | bytes 4194304 | tf_op jit(solution)/shard_map/move_cols/pallas_call | solution.py:195
  117.7 11.0 %collective-permute-done.12 = f32[16,512]{1,0:T(8,128)S(1)} collective-permute-done((f32[16,512]{1,0:T(8,128)S(1)}, f32[16,512]{1,0:T(8,128)S(1)}, u32[]{:S(2)}, u32[]{:S(2)}) %collective-permute-start.12) | collective-permute-done | bytes 32800 | tf_op jit(solution)/shard_map/ppermute | solution.py:422
  131.0 4.3 %collective-permute-start.15 = (f32[64,512]{1,0:T(8,128)S(1)}, f32[64,512]{1,0:T(8,128)S(1)}, u32[]{:S(2)}, u32[]{:S(2)}) collective-permute-start(f32[64,512]{1,0:T(8,128)S(1)} %get-tuple-element.25), channel_id=1, source_target_pairs={{0,128},{32,160},{64,192},{96,224},{128,0},{160,32},{192,64},{224,... | collective-permute-start | bytes 393224 | tf_op jit(solution)/shard_map/ppermute | solution.py:422
  135.7 2.5 %collective-permute-start.17 = (f32[64,512]{1,0:T(8,128)S(1)}, f32[64,512]{1,0:T(8,128)S(1)}, u32[]{:S(2)}, u32[]{:S(2)}) collective-permute-start(f32[64,512]{1,0:T(8,128)S(1)} %get-tuple-element.25), channel_id=1, source_target_pairs={{0,384},{32,416},{64,448},{96,480},{128,256},{160,288},{192,320},{... | collective-permute-start | bytes 393224 | tf_op jit(solution)/shard_map/ppermute | solution.py:422
  138.2 4.0 %collective-permute-start.19 = (f32[512,512]{1,0:T(8,128)S(1)}, f32[512,512]{1,0:T(8,128)S(1)}, u32[]{:S(2)}, u32[]{:S(2)}) collective-permute-start(f32[512,512]{1,0:T(8,128)S(1)} %move_cols.5.refs_1_), channel_id=1, source_target_pairs={{33,65},{34,66},{37,69},{38,70},{41,73},{42,74},{45,77},{46,78},{4... | collective-permute-start | bytes 3145736 | tf_op jit(solution)/shard_map/ppermute | solution.py:433
  148.8 4.3 %move_cols.7.refs_2_ = f32[512,512]{1,0:T(8,128)S(1)} custom-call(s32[4]{0:T(128)S(1)} %pad_add_fusion.at_ref.refs_0_, f32[1024,512]{1,0:T(8,128)S(1)} %copy-done.1, f32[1024,512]{1,0:T(8,128)} %collective-permute-done.refs_1_, f32[1024,512]{1,0:T(8,128)} %collective-permute-done.1.refs_2_, f32[512,512]{1,0:T(8,128)S(1)} %collective-permute-done.3.refs_3_, ...), custom_call_target="tpu_custom_call" | custom-call | flops 7077888 | bytes 4194304 | tf_op jit(solution)/shard_map/move_cols/pallas_call | solution.py:195
  155.1 6.4 %collective-permute-done.19.refs_4_ = f32[512,512]{1,0:T(8,128)S(1)} collective-permute-done((f32[512,512]{1,0:T(8,128)S(1)}, f32[512,512]{1,0:T(8,128)S(1)}, u32[]{:S(2)}, u32[]{:S(2)}) %collective-permute-start.19) | collective-permute-done | bytes 1048608 | tf_op jit(solution)/shard_map/ppermute | solution.py:433
  161.4 5.5 %move_rows.1.refs_1_ = f32[1024,512]{1,0:T(8,128)} custom-call(s32[4]{0:T(128)S(1)} %pad_add_fusion.at_ref.refs_0_, f32[512,512]{1,0:T(8,128)S(1)} %move_cols.5.refs_1_, f32[512,512]{1,0:T(8,128)S(1)} %move_cols.7.refs_2_, f32[512,512]{1,0:T(8,128)S(1)} %collective-permute-done.18.refs_3_, f32[512,512]{1,0:T(8,128)S(1)} %collective-permute-done.19.refs_4_, ...), custom_call_target="tpu_custom_call" | custom-call | flops 12582912 | bytes 8388608 | tf_op jit(solution)/shard_map/move_rows/pallas_call | solution.py:292
  166.9 23.6 %collective-permute-done.21.refs_3_ = f32[512,512]{1,0:T(8,128)S(1)} collective-permute-done((f32[512,512]{1,0:T(8,128)S(1)}, f32[512,512]{1,0:T(8,128)S(1)}, u32[]{:S(2)}, u32[]{:S(2)}) %collective-permute-start.21) | collective-permute-done | bytes 1048608 | tf_op jit(solution)/shard_map/ppermute | solution.py:433
  190.5 3.4 %add_last.1 = f32[1024,512]{1,0:T(8,128)} custom-call(s32[4]{0:T(128)S(1)} %pad_add_fusion.at_ref.refs_0_, f32[1024,512]{1,0:T(8,128)} %move_rows.1.refs_1_, f32[512,512]{1,0:T(8,128)S(1)} %collective-permute-done.20.refs_2_, f32[512,512]{1,0:T(8,128)S(1)} %collective-permute-done.21.refs_3_, f32[1536,8]{1,0:T(8,128)S(1)} %copy-done.2), custom_call_target="tpu_custom_call", output_to_operand_aliasing={{}: (1, {})} | custom-call | flops 5242880 | bytes 4194304 | tf_op jit(solution)/shard_map/add_last/pallas_call | solution.py:356
  (59 shorter events, 28.9 us)
Async XLA Ops:
  0.0 135.3 %copy-start = (bf16[1024,256]{1,0:T(8,128)(2,1)S(1)}, bf16[1024,256]{1,0:T(8,128)(2,1)}, u32[]{:S(2)}) copy-start(bf16[1024,256]{1,0:T(8,128)(2,1)} %param.11) | copy-start | bytes 1572868
  0.0 109.1 %collective-permute-start.1 = (f32[1024,512]{1,0:T(8,128)}, f32[1024,512]{1,0:T(8,128)}, u32[]{:S(2)}, u32[]{:S(2)}) collective-permute-start(f32[1024,512]{1,0:T(8,128)} %refs_0_.7), channel_id=1, source_target_pairs={{3,4},{4,3},{7,8},{8,7},{11,12},{12,11},{15,16},{16,15},{19,20},{2... | collective-permute-start | bytes 6291464 | tf_op jit(solution)/shard_map/ppermute | solution.py:400
  2.1 111.1 %collective-permute-start = (f32[1024,512]{1,0:T(8,128)}, f32[1024,512]{1,0:T(8,128)}, u32[]{:S(2)}, u32[]{:S(2)}) collective-permute-start(f32[1024,512]{1,0:T(8,128)} %refs_0_.7), channel_id=1, source_target_pairs={{0,1},{1,0},{2,3},{3,2},{4,5},{5,4},{6,7},{7,6},{8,9},{9,8},{10,11... | collective-permute-start | bytes 6291464 | tf_op jit(solution)/shard_map/ppermute | solution.py:401
  27.0 10.6 %collective-permute-start.4 = (f32[64,512]{1,0:T(8,128)}, f32[64,512]{1,0:T(8,128)S(1)}, u32[]{:S(2)}, u32[]{:S(2)}) collective-permute-start(f32[64,512]{1,0:T(8,128)} %get-tuple-element.19), channel_id=1, source_target_pairs={{0,128},{32,160},{64,192},{96,224},{128,0},{160,32},{192,64},{224,... | collective-permute-start | bytes 393224 | tf_op jit(solution)/shard_map/ppermute | solution.py:418
  29.8 10.9 %collective-permute-start.6 = (f32[64,512]{1,0:T(8,128)}, f32[64,512]{1,0:T(8,128)S(1)}, u32[]{:S(2)}, u32[]{:S(2)}) collective-permute-start(f32[64,512]{1,0:T(8,128)} %get-tuple-element.20), channel_id=1, source_target_pairs={{0,384},{32,416},{64,448},{96,480},{128,256},{160,288},{192,320},{... | collective-permute-start | bytes 393224 | tf_op jit(solution)/shard_map/ppermute | solution.py:418
  31.8 9.6 %collective-permute-start.5 = (f32[64,512]{1,0:T(8,128)}, f32[64,512]{1,0:T(8,128)}, u32[]{:S(2)}, u32[]{:S(2)}) collective-permute-start(f32[64,512]{1,0:T(8,128)} %get-tuple-element.21), channel_id=1, source_target_pairs={{0,256},{32,288},{64,320},{96,352},{128,384},{160,416},{192,448},{... | collective-permute-start | bytes 393224 | tf_op jit(solution)/shard_map/ppermute | solution.py:418
  36.0 67.1 %copy-start.3 = (f32[8,1024]{1,0:T(8,128)S(1)}, f32[8,1024]{1,0:T(8,128)}, u32[]{:S(2)}) copy-start(f32[8,1024]{1,0:T(8,128)} %get-tuple-element.13.refs_4_.refs_3_) | copy-start | bytes 98308
  37.6 68.2 %collective-permute-start.2 = (f32[512,512]{1,0:T(8,128)}, f32[512,512]{1,0:T(8,128)}, u32[]{:S(2)}, u32[]{:S(2)}) collective-permute-start(f32[512,512]{1,0:T(8,128)} %get-tuple-element.18), channel_id=1, source_target_pairs={{1,2},{2,1},{5,6},{6,5},{9,10},{10,9},{13,14},{14,13},{17,18},{18,... | collective-permute-start | bytes 3145736 | tf_op jit(solution)/shard_map/ppermute | solution.py:405
  42.4 43.7 %collective-permute-start.7 = (f32[16,512]{1,0:T(8,128)S(1)}, f32[16,512]{1,0:T(8,128)S(1)}, u32[]{:S(2)}, u32[]{:S(2)}) collective-permute-start(f32[16,512]{1,0:T(8,128)S(1)} %get-tuple-element.22), channel_id=1, source_target_pairs={{0,32},{32,0},{64,96},{96,64},{128,160},{160,128},{192,224},{224,1... | collective-permute-start | bytes 98312 | tf_op jit(solution)/shard_map/ppermute | solution.py:418
  45.5 42.6 %collective-permute-start.9 = (f32[16,512]{1,0:T(8,128)S(1)}, f32[16,512]{1,0:T(8,128)S(1)}, u32[]{:S(2)}, u32[]{:S(2)}) collective-permute-start(f32[16,512]{1,0:T(8,128)S(1)} %get-tuple-element.23), channel_id=1, source_target_pairs={{0,96},{32,64},{64,32},{96,0},{128,224},{160,192},{192,160},{224,1... | collective-permute-start | bytes 98312 | tf_op jit(solution)/shard_map/ppermute | solution.py:418
  86.1 5.5 %collective-permute-start.8 = (f32[16,512]{1,0:T(8,128)S(1)}, f32[16,512]{1,0:T(8,128)S(1)}, u32[]{:S(2)}, u32[]{:S(2)}) collective-permute-start(f32[16,512]{1,0:T(8,128)S(1)} %get-tuple-element.24), channel_id=1, source_target_pairs={{0,64},{32,96},{64,0},{96,32},{128,192},{160,224},{192,128},{224,1... | collective-permute-start | bytes 98312 | tf_op jit(solution)/shard_map/ppermute | solution.py:418
  91.6 9.1 %collective-permute-start.11 = (f32[16,512]{1,0:T(8,128)S(1)}, f32[16,512]{1,0:T(8,128)S(1)}, u32[]{:S(2)}, u32[]{:S(2)}) collective-permute-start(f32[16,512]{1,0:T(8,128)S(1)} %fusion.6.refs_0_), channel_id=1, source_target_pairs={{1,2},{2,1},{3,4},{4,3},{5,6},{6,5},{7,8},{8,7},{9,10},{10,9},{11,... | collective-permute-start | bytes 98312 | tf_op jit(solution)/shard_map/ppermute | solution.py:435
  94.0 9.1 %collective-permute-start.10 = (f32[16,512]{1,0:T(8,128)S(1)}, f32[16,512]{1,0:T(8,128)S(1)}, u32[]{:S(2)}, u32[]{:S(2)}) collective-permute-start(f32[16,512]{1,0:T(8,128)S(1)} %fusion.6.refs_0_), channel_id=1, source_target_pairs={{0,1},{1,0},{2,3},{3,2},{4,5},{5,4},{6,7},{7,6},{8,9},{9,8},{10,11... | collective-permute-start | bytes 98312 | tf_op jit(solution)/shard_map/ppermute | solution.py:437
  100.8 48.0 %collective-permute-start.3 = (f32[512,512]{1,0:T(8,128)}, f32[512,512]{1,0:T(8,128)S(1)}, u32[]{:S(2)}, u32[]{:S(2)}) collective-permute-start(f32[512,512]{1,0:T(8,128)} %get-tuple-element.17), channel_id=1, source_target_pairs={{1,2},{2,1},{5,6},{6,5},{9,10},{10,9},{13,14},{14,13},{17,18},{18,... | collective-permute-start | bytes 3145736 | tf_op jit(solution)/shard_map/ppermute | solution.py:405
  103.9 24.9 %collective-permute-start.14 = (f32[16,512]{1,0:T(8,128)S(1)}, f32[16,512]{1,0:T(8,128)S(1)}, u32[]{:S(2)}, u32[]{:S(2)}) collective-permute-start(f32[16,512]{1,0:T(8,128)S(1)} %move_cols.6), channel_id=1, source_target_pairs={{0,96},{32,64},{64,32},{96,0},{128,224},{160,192},{192,160},{224,1... | collective-permute-start | bytes 98312 | tf_op jit(solution)/shard_map/ppermute | solution.py:422
  105.8 22.9 %collective-permute-start.13 = (f32[16,512]{1,0:T(8,128)S(1)}, f32[16,512]{1,0:T(8,128)S(1)}, u32[]{:S(2)}, u32[]{:S(2)}) collective-permute-start(f32[16,512]{1,0:T(8,128)S(1)} %move_cols.6), channel_id=1, source_target_pairs={{0,64},{32,96},{64,0},{96,32},{128,192},{160,224},{192,128},{224,1... | collective-permute-start | bytes 98312 | tf_op jit(solution)/shard_map/ppermute | solution.py:422
  109.1 19.6 %collective-permute-start.12 = (f32[16,512]{1,0:T(8,128)S(1)}, f32[16,512]{1,0:T(8,128)S(1)}, u32[]{:S(2)}, u32[]{:S(2)}) collective-permute-start(f32[16,512]{1,0:T(8,128)S(1)} %move_cols.6), channel_id=1, source_target_pairs={{0,32},{32,0},{64,96},{96,64},{128,160},{160,128},{192,224},{224,1... | collective-permute-start | bytes 98312 | tf_op jit(solution)/shard_map/ppermute | solution.py:422
  128.8 17.3 %collective-permute-start.16 = (f32[64,512]{1,0:T(8,128)S(1)}, f32[64,512]{1,0:T(8,128)S(1)}, u32[]{:S(2)}, u32[]{:S(2)}) collective-permute-start(f32[64,512]{1,0:T(8,128)S(1)} %get-tuple-element.25), channel_id=1, source_target_pairs={{0,256},{32,288},{64,320},{96,352},{128,384},{160,416},{192,448},{... | collective-permute-start | bytes 393224 | tf_op jit(solution)/shard_map/ppermute | solution.py:422
  131.0 14.4 %collective-permute-start.15 = (f32[64,512]{1,0:T(8,128)S(1)}, f32[64,512]{1,0:T(8,128)S(1)}, u32[]{:S(2)}, u32[]{:S(2)}) collective-permute-start(f32[64,512]{1,0:T(8,128)S(1)} %get-tuple-element.25), channel_id=1, source_target_pairs={{0,128},{32,160},{64,192},{96,224},{128,0},{160,32},{192,64},{224,... | collective-permute-start | bytes 393224 | tf_op jit(solution)/shard_map/ppermute | solution.py:422
  135.7 11.1 %collective-permute-start.17 = (f32[64,512]{1,0:T(8,128)S(1)}, f32[64,512]{1,0:T(8,128)S(1)}, u32[]{:S(2)}, u32[]{:S(2)}) collective-permute-start(f32[64,512]{1,0:T(8,128)S(1)} %get-tuple-element.25), channel_id=1, source_target_pairs={{0,384},{32,416},{64,448},{96,480},{128,256},{160,288},{192,320},{... | collective-permute-start | bytes 393224 | tf_op jit(solution)/shard_map/ppermute | solution.py:422
  138.2 23.2 %collective-permute-start.19 = (f32[512,512]{1,0:T(8,128)S(1)}, f32[512,512]{1,0:T(8,128)S(1)}, u32[]{:S(2)}, u32[]{:S(2)}) collective-permute-start(f32[512,512]{1,0:T(8,128)S(1)} %move_cols.5.refs_1_), channel_id=1, source_target_pairs={{33,65},{34,66},{37,69},{38,70},{41,73},{42,74},{45,77},{46,78},{4... | collective-permute-start | bytes 3145736 | tf_op jit(solution)/shard_map/ppermute | solution.py:433
  145.4 9.7 %collective-permute-start.18 = (f32[512,512]{1,0:T(8,128)S(1)}, f32[512,512]{1,0:T(8,128)S(1)}, u32[]{:S(2)}, u32[]{:S(2)}) collective-permute-start(f32[512,512]{1,0:T(8,128)S(1)} %move_cols.8), channel_id=1, source_target_pairs={{32,64},{35,67},{36,68},{39,71},{40,72},{43,75},{44,76},{47,79},{4... | collective-permute-start | bytes 3145736 | tf_op jit(solution)/shard_map/ppermute | solution.py:433
  146.1 20.8 %collective-permute-start.20 = (f32[512,512]{1,0:T(8,128)S(1)}, f32[512,512]{1,0:T(8,128)S(1)}, u32[]{:S(2)}, u32[]{:S(2)}) collective-permute-start(f32[512,512]{1,0:T(8,128)S(1)} %move_cols.9), channel_id=1, source_target_pairs={{0,32},{3,35},{4,36},{7,39},{8,40},{11,43},{12,44},{15,47},{16,48}... | collective-permute-start | bytes 3145736 | tf_op jit(solution)/shard_map/ppermute | solution.py:433
  153.1 37.4 %collective-permute-start.21 = (f32[512,512]{1,0:T(8,128)S(1)}, f32[512,512]{1,0:T(8,128)S(1)}, u32[]{:S(2)}, u32[]{:S(2)}) collective-permute-start(f32[512,512]{1,0:T(8,128)S(1)} %move_cols.7.refs_2_), channel_id=1, source_target_pairs={{1,33},{2,34},{5,37},{6,38},{9,41},{10,42},{13,45},{14,46},{17,49}... | collective-permute-start | bytes 3145736 | tf_op jit(solution)/shard_map/ppermute | solution.py:433
  (4 other events, 79.0 us)

commit v5 on v4

--- a/solution.py
+++ b/solution.py
@@ -142,8 +142,9 @@
     return result + weights[3] * before + weights[4] * behind
 
 
-def cols_kernel(inner, unroll, at_ref, here_ref, near_ref, *refs):
+def cols_kernel(inner, unroll, spans, at_ref, here_ref, near_ref, *refs):
     far_refs, (weights_ref, out_ref) = refs[:-2], refs[-2:]
+    step = pl.program_id(0)
     first = at_ref[0] == 0
 
     def weights(m):
@@ -153,8 +154,8 @@
         rows = pl.ds(pl.multiple_of(t * inner, inner), inner)
         near, here = near_ref[rows, :], here_ref[rows, :]
         far = far_refs[0][rows, :]
-        for ref in far_refs[1:]:
-            far = far + ref[rows, :]
+        for ref, (low, count) in zip(far_refs[1:], spans[1:]):
+            far = far + jnp.where((step >= low) & (step < low + count), ref[rows, :], 0.0)
         west = jnp.where(first, far, near)
         east = jnp.where(first, near, far)
         maps = [part[:, MAPX * k : MAPX * (k + 1)] for part in (west, here, east) for k in range(2)]
@@ -173,15 +174,19 @@
     tile = min(rows, 128)
     inner = min(rows, 64)
     steps = rows // tile
+    spans, covered = [(0, steps)], 0
+    for array, _ in fars[1:]:
+        spans.append((covered, array.shape[0] // tile))
+        covered += array.shape[0] // tile
 
     def kernel(at_ref, *refs):
         if only is None:
-            cols_kernel(inner, tile // inner, at_ref, *refs)
+            cols_kernel(inner, tile // inner, spans, at_ref, *refs)
         else:
 
             @pl.when(at_ref[HALVES[only]] == 1)
             def _():
-                cols_kernel(inner, tile // inner, at_ref, *refs)
+                cols_kernel(inner, tile // inner, spans, at_ref, *refs)
 
     def spec(block):
         def index(s, a):
@@ -191,7 +196,11 @@
 
         return pl.BlockSpec((tile, cols), index)
 
-    blocks = [here, near, *fars]
+    def part_spec(low, count):
+        return pl.BlockSpec((tile, cols), lambda s, a: (jnp.clip(s - low, 0, count - 1), 0))
+
+    blocks = [here, near, fars[0]]
+    arrays = [array for array, _ in (here, near, *fars)]
     return pl.pallas_call(
         kernel,
         out_shape=jax.ShapeDtypeStruct((rows, cols), jnp.float32),
@@ -199,6 +208,7 @@
             num_scalar_prefetch=1,
             grid=(steps,),
             in_specs=[spec(block) for _, block in blocks]
+            + [part_spec(*span) for span in spans[1:]]
             + [pl.BlockSpec(weights.shape, lambda s, a: (0, 0))],
             out_specs=spec(0),
         ),
@@ -207,7 +217,7 @@
             flops=27 * rows * cols, bytes_accessed=16 * rows * cols, transcendentals=0
         ),
         name="move_cols",
-    )(at, *[array for array, _ in blocks], weights)
+    )(at, *arrays, weights)
 
 
 def load(parts, start, size):
@@ -400,9 +410,11 @@
     far_turning = lax.ppermute(covariance, "col", turning)
     near = lax.ppermute(covariance, "col", near_swap)
 
-    def far_part(number, source):
-        block = lax.dynamic_slice_in_dim(source, number * half, half, 0)
+    def far_part(start, size, source):
+        block = lax.dynamic_slice_in_dim(source, start, size, 0)
         return lax.ppermute(block, "col", straight)
+
+    far_begin = far_part(first * half, MAPX, covariance)
 
 
     select, col_weights, down_weights = prepare(
@@ -433,18 +445,19 @@
         return lax.ppermute(block, ("row", "col"), row_swap(odd, kinds))
 
     piece_far = lax.ppermute(total, "col", far_swap)
-    far_first = far_part(first, after(covariance, select))
+    late = after(covariance, select)
+    far_first = far_part(first * half + MAPX, half - MAPX, late)
+
+    early_first = move("first", only="turns")
+    early_second = move("second", only="turns")
     piece_near = lax.ppermute(total, "col", near_swap)
     piece = move_cols(place, (total, 0), (piece_near, 0), [(piece_far, 0)], col_weights, each)
     observed = all_of(piece, Z_BITS)
-    far_second = far_part(second, after(covariance, select))
-
-    early_first = move("first", only="turns")
     halo_first = [swap_rows(early_first, 1, (0, 3))]
-    early_second = move("second", only="turns")
     halo_second = [swap_rows(early_second, 0, (0, 3))]
-
-    moved_first = move("first", far_first)
+    far_second = far_part(second * half, half, late)
+
+    moved_first = move("first", far_begin, far_first)
     halo_first.append(swap_rows(moved_first, 1, (1, 2)))
 
     observed = jnp.concatenate([after(observed[0], moved_first), *observed[1:]])

time: 195 us -> 204 us (1.046)
  the two profiles are of different devices: /device:TPU:37 before, /device:TPU:100 now
where the time goes in v5:
time: 204 us; the launch traced here: 203 us
  starting transfers between devices  91.7 us (45%)
  waiting for transfers between devices  61.6 us (30%)
  Pallas kernels  35.7 us (18%)
  matrix products  6.27 us (3%)
  local copies, waits for them, and re-layouts  5.05 us (2%)
    ppermute x4, waiting for transfers between devices, swap_rows(): return lax.ppermute(block, ('row', 'col'), row_swap(odd, kinds))  27.4 us
    ppermute x6, waiting for transfers between devices, sum_over(): total = total + lax.ppermute(piece, 'row', across(bit))  24.9 us
    ppermute x4, starting transfers between devices, swap_rows(): return lax.ppermute(block, ('row', 'col'), row_swap(odd, kinds))  24.1 us
    ppermute x6, starting transfers between devices, all_of(): return [value] + [lax.ppermute(value, 'row', across(bit)) for bit in bits]  20.1 us
    ppermute x6, starting transfers between devices, sum_over(): total = total + lax.ppermute(piece, 'row', across(bit))  18.5 us
    pallas_call x5, Pallas kernels, move_cols(): pl.pallas_call(kernel, out_shape=jax.ShapeDtypeStruct((rows, cols), jnp.f...  18.2 us
    ppermute x1, starting transfers between devices, local(): piece_near = lax.ppermute(total, 'col', near_swap)  12.1 us
    ppermute x1, starting transfers between devices, local(): far_turning = lax.ppermute(covariance, 'col', turning)  9.47 us
  transfers between devices with their start and end apart: 23, of which 7 were waited for; matrix products, arithmetic and copies ran while one was open for 6% of the time, Pallas kernels for 16%

profile of v5, /device:TPU:100, one launch (start us, length us, event | category | flops | bytes accessed | tf_op | source)
XLA Modules:
  0.0 202.7 jit_solution(11093442881105637635)
XLA Ops:
  0.0 9.5 %collective-permute-start.1 = (f32[1024,512]{1,0:T(8,128)}, f32[1024,512]{1,0:T(8,128)}, u32[]{:S(2)}, u32[]{:S(2)}) collective-permute-start(f32[1024,512]{1,0:T(8,128)} %refs_0_.7), channel_id=1, source_target_pairs={{3,4},{4,3},{7,8},{8,7},{11,12},{12,11},{15,16},{16,15},{19,20},{2... | collective-permute-start | bytes 6291464 | tf_op jit(solution)/shard_map/ppermute | solution.py:410
  12.0 8.7 %prepare.1 = (f32[256,1024]{1,0:T(8,128)}, f32[8,1024]{1,0:T(8,128)}, f32[1536,8]{1,0:T(8,128)}) custom-call(s32[3]{0:T(128)} %pad_add_fusion.1.refs_0_, s32[2,16384]{1,0:T(2,128)} %refs_1_.1, f32[2,16384]{1,0:T(2,128)} %refs_2_.1, s32[256,128]{1,0:T(8,128)} %refs_6_.1, s32[256,128]{1,0:T(8,128)} %refs_6_.1, s32[256,128]{1,0:T(8,128)} %refs_6_.1, ...), custom_call_target="tpu_custom_call" | custom-call | flops 134217728 | bytes 2097152 | tf_op jit(solution)/shard_map/prepare/pallas_call | solution.py:108
  20.6 4.0 %fusion.9 = f32[256,512]{1,0:T(8,128)S(1)} fusion(f32[256,1024]{1,0:T(8,128)} %get-tuple-element.11, f32[1024,512]{1,0:T(8,128)} %refs_0_.7), kind=kOutput, calls=%fused_computation.30 | convolution fusion | flops 1610612736 | bytes 3670016 | tf_op jit(solution)/shard_map/dot_general | solution.py:423
  26.2 3.1 %collective-permute-start.5 = (f32[64,512]{1,0:T(8,128)S(1)}, f32[64,512]{1,0:T(8,128)S(1)}, u32[]{:S(2)}, u32[]{:S(2)}) collective-permute-start(f32[64,512]{1,0:T(8,128)S(1)} %get-tuple-element.17), channel_id=1, source_target_pairs={{0,128},{32,160},{64,192},{96,224},{128,0},{160,32},{192,64},{224,... | collective-permute-start | bytes 393224 | tf_op jit(solution)/shard_map/ppermute | solution.py:430
  31.2 4.8 %collective-permute-start.6 = (f32[64,512]{1,0:T(8,128)}, f32[64,512]{1,0:T(8,128)}, u32[]{:S(2)}, u32[]{:S(2)}) collective-permute-start(f32[64,512]{1,0:T(8,128)} %get-tuple-element.19), channel_id=1, source_target_pairs={{0,256},{32,288},{64,320},{96,352},{128,384},{160,416},{192,448},{... | collective-permute-start | bytes 393224 | tf_op jit(solution)/shard_map/ppermute | solution.py:430
  44.1 4.3 %collective-permute-start.10 = (f32[16,512]{1,0:T(8,128)S(1)}, f32[16,512]{1,0:T(8,128)S(1)}, u32[]{:S(2)}, u32[]{:S(2)}) collective-permute-start(f32[16,512]{1,0:T(8,128)S(1)} %get-tuple-element.21), channel_id=1, source_target_pairs={{0,96},{32,64},{64,32},{96,0},{128,224},{160,192},{192,160},{224,1... | collective-permute-start | bytes 98312 | tf_op jit(solution)/shard_map/ppermute | solution.py:430
  49.2 10.6 %collective-permute-done.8 = f32[16,512]{1,0:T(8,128)S(1)} collective-permute-done((f32[16,512]{1,0:T(8,128)S(1)}, f32[16,512]{1,0:T(8,128)S(1)}, u32[]{:S(2)}, u32[]{:S(2)}) %collective-permute-start.8) | collective-permute-done | bytes 32800 | tf_op jit(solution)/shard_map/ppermute | solution.py:430
  61.3 8.0 %collective-permute-done.10 = f32[16,512]{1,0:T(8,128)S(1)} collective-permute-done((f32[16,512]{1,0:T(8,128)S(1)}, f32[16,512]{1,0:T(8,128)S(1)}, u32[]{:S(2)}, u32[]{:S(2)}) %collective-permute-start.10) | collective-permute-done | bytes 32800 | tf_op jit(solution)/shard_map/ppermute | solution.py:430
  71.2 5.1 %collective-permute-done.9 = f32[16,512]{1,0:T(8,128)S(1)} collective-permute-done((f32[16,512]{1,0:T(8,128)S(1)}, f32[16,512]{1,0:T(8,128)S(1)}, u32[]{:S(2)}, u32[]{:S(2)}) %collective-permute-start.9) | collective-permute-done | bytes 32800 | tf_op jit(solution)/shard_map/ppermute | solution.py:430
  79.3 8.4 %collective-permute-done.12.refs_2_ = f32[16,512]{1,0:T(8,128)S(1)} collective-permute-done((f32[16,512]{1,0:T(8,128)S(1)}, f32[16,512]{1,0:T(8,128)S(1)}, u32[]{:S(2)}, u32[]{:S(2)}) %collective-permute-start.12) | collective-permute-done | bytes 32800 | tf_op jit(solution)/shard_map/ppermute | solution.py:447
  87.7 12.1 %collective-permute-start.11 = (f32[16,512]{1,0:T(8,128)S(1)}, f32[16,512]{1,0:T(8,128)S(1)}, u32[]{:S(2)}, u32[]{:S(2)}) collective-permute-start(f32[16,512]{1,0:T(8,128)S(1)} %fusion.6.refs_0_), channel_id=1, source_target_pairs={{0,1},{1,0},{2,3},{3,2},{4,5},{5,4},{6,7},{7,6},{8,9},{9,8},{10,11... | collective-permute-start | bytes 98312 | tf_op jit(solution)/shard_map/ppermute | solution.py:453
  102.1 4.2 %collective-permute-start.15 = (f32[16,512]{1,0:T(8,128)S(1)}, f32[16,512]{1,0:T(8,128)S(1)}, u32[]{:S(2)}, u32[]{:S(2)}) collective-permute-start(f32[16,512]{1,0:T(8,128)S(1)} %move_cols.6), channel_id=1, source_target_pairs={{0,96},{32,64},{64,32},{96,0},{128,224},{160,192},{192,160},{224,1... | collective-permute-start | bytes 98312 | tf_op jit(solution)/shard_map/ppermute | solution.py:434
  106.3 3.2 %collective-permute-start.14 = (f32[16,512]{1,0:T(8,128)S(1)}, f32[16,512]{1,0:T(8,128)S(1)}, u32[]{:S(2)}, u32[]{:S(2)}) collective-permute-start(f32[16,512]{1,0:T(8,128)S(1)} %move_cols.6), channel_id=1, source_target_pairs={{0,64},{32,96},{64,0},{96,32},{128,192},{160,224},{192,128},{224,1... | collective-permute-start | bytes 98312 | tf_op jit(solution)/shard_map/ppermute | solution.py:434
  112.4 4.5 %move_cols.5.refs_1_ = f32[512,512]{1,0:T(8,128)S(1)} custom-call(s32[4]{0:T(128)S(1)} %pad_add_fusion.at_ref.refs_0_, f32[1024,512]{1,0:T(8,128)S(1)} %copy-done.1, f32[1024,512]{1,0:T(8,128)} %collective-permute-done.refs_1_, f32[1024,512]{1,0:T(8,128)} %collective-permute-done.1.refs_2_, f32[256,512]{1,0:T(8,128)S(1)} %collective-permute-done.2.refs_3_, ...), custom_call_target="tpu_custom_call" | custom-call | flops 7077888 | bytes 4194304 | tf_op jit(solution)/shard_map/move_cols/pallas_call | solution.py:204
  119.5 4.0 %collective-permute-start.16 = (f32[64,512]{1,0:T(8,128)S(1)}, f32[64,512]{1,0:T(8,128)S(1)}, u32[]{:S(2)}, u32[]{:S(2)}) collective-permute-start(f32[64,512]{1,0:T(8,128)S(1)} %get-tuple-element.23), channel_id=1, source_target_pairs={{0,128},{32,160},{64,192},{96,224},{128,0},{160,32},{192,64},{224,... | collective-permute-start | bytes 393224 | tf_op jit(solution)/shard_map/ppermute | solution.py:434
  124.0 3.4 %collective-permute-start.18 = (f32[64,512]{1,0:T(8,128)S(1)}, f32[64,512]{1,0:T(8,128)S(1)}, u32[]{:S(2)}, u32[]{:S(2)}) collective-permute-start(f32[64,512]{1,0:T(8,128)S(1)} %get-tuple-element.23), channel_id=1, source_target_pairs={{0,384},{32,416},{64,448},{96,480},{128,256},{160,288},{192,320},{... | collective-permute-start | bytes 393224 | tf_op jit(solution)/shard_map/ppermute | solution.py:434
  128.1 4.3 %move_cols.9 = f32[512,512]{1,0:T(8,128)S(1)} custom-call(s32[4]{0:T(128)S(1)} %pad_add_fusion.at_ref.refs_0_, f32[1024,512]{1,0:T(8,128)S(1)} %copy-done.1, f32[1024,512]{1,0:T(8,128)} %collective-permute-done.refs_1_, f32[1024,512]{1,0:T(8,128)} %collective-permute-done.1.refs_2_, f32[8,1024]{1,0:T(8,128)S(1)} %copy-done.3), custom_call_target="tpu_custom_call" | custom-call | flops 7077888 | bytes 4194304 | tf_op jit(solution)/shard_map/move_cols/pallas_call | solution.py:204
  132.4 4.3 %move_cols.8 = f32[512,512]{1,0:T(8,128)S(1)} custom-call(s32[4]{0:T(128)S(1)} %pad_add_fusion.at_ref.refs_0_, f32[1024,512]{1,0:T(8,128)S(1)} %copy-done.1, f32[1024,512]{1,0:T(8,128)} %collective-permute-done.refs_1_, f32[1024,512]{1,0:T(8,128)} %collective-permute-done.1.refs_2_, f32[8,1024]{1,0:T(8,128)S(1)} %copy-done.3), custom_call_target="tpu_custom_call" | custom-call | flops 7077888 | bytes 4194304 | tf_op jit(solution)/shard_map/move_cols/pallas_call | solution.py:204
  136.7 18.8 %collective-permute-start.19 = (f32[512,512]{1,0:T(8,128)S(1)}, f32[512,512]{1,0:T(8,128)S(1)}, u32[]{:S(2)}, u32[]{:S(2)}) collective-permute-start(f32[512,512]{1,0:T(8,128)S(1)} %move_cols.8), channel_id=1, source_target_pairs={{32,64},{35,67},{36,68},{39,71},{40,72},{43,75},{44,76},{47,79},{4... | collective-permute-start | bytes 3145736 | tf_op jit(solution)/shard_map/ppermute | solution.py:445
  155.6 3.8 %collective-permute-start.21 = (f32[512,512]{1,0:T(8,128)S(1)}, f32[512,512]{1,0:T(8,128)S(1)}, u32[]{:S(2)}, u32[]{:S(2)}) collective-permute-start(f32[512,512]{1,0:T(8,128)S(1)} %move_cols.9), channel_id=1, source_target_pairs={{0,32},{3,35},{4,36},{7,39},{8,40},{11,43},{12,44},{15,47},{16,48}... | collective-permute-start | bytes 3145736 | tf_op jit(solution)/shard_map/ppermute | solution.py:445
  161.4 4.3 %move_cols.7.refs_2_ = f32[512,512]{1,0:T(8,128)S(1)} custom-call(s32[4]{0:T(128)S(1)} %pad_add_fusion.at_ref.refs_0_, f32[1024,512]{1,0:T(8,128)S(1)} %copy-done.1, f32[1024,512]{1,0:T(8,128)} %collective-permute-done.refs_1_, f32[1024,512]{1,0:T(8,128)} %collective-permute-done.1.refs_2_, f32[512,512]{1,0:T(8,128)S(1)} %collective-permute-done.4.refs_3_, ...), custom_call_target="tpu_custom_call" | custom-call | flops 7077888 | bytes 4194304 | tf_op jit(solution)/shard_map/move_cols/pallas_call | solution.py:204
  166.4 27.4 %collective-permute-done.19.refs_3_ = f32[512,512]{1,0:T(8,128)S(1)} collective-permute-done((f32[512,512]{1,0:T(8,128)S(1)}, f32[512,512]{1,0:T(8,128)S(1)}, u32[]{:S(2)}, u32[]{:S(2)}) %collective-permute-start.19) | collective-permute-done | bytes 1048608 | tf_op jit(solution)/shard_map/ppermute | solution.py:445
  193.8 5.5 %move_rows.1.refs_1_ = f32[1024,512]{1,0:T(8,128)} custom-call(s32[4]{0:T(128)S(1)} %pad_add_fusion.at_ref.refs_0_, f32[512,512]{1,0:T(8,128)S(1)} %move_cols.5.refs_1_, f32[512,512]{1,0:T(8,128)S(1)} %move_cols.7.refs_2_, f32[512,512]{1,0:T(8,128)S(1)} %collective-permute-done.19.refs_3_, f32[512,512]{1,0:T(8,128)S(1)} %collective-permute-done.20.refs_4_, ...), custom_call_target="tpu_custom_call" | custom-call | flops 12582912 | bytes 8388608 | tf_op jit(solution)/shard_map/move_rows/pallas_call | solution.py:302
  199.3 3.4 %add_last.1 = f32[1024,512]{1,0:T(8,128)} custom-call(s32[4]{0:T(128)S(1)} %pad_add_fusion.at_ref.refs_0_, f32[1024,512]{1,0:T(8,128)} %move_rows.1.refs_1_, f32[512,512]{1,0:T(8,128)S(1)} %collective-permute-done.21.refs_2_, f32[512,512]{1,0:T(8,128)S(1)} %collective-permute-done.22.refs_3_, f32[1536,8]{1,0:T(8,128)S(1)} %copy-done.2), custom_call_target="tpu_custom_call", output_to_operand_aliasing={{}: (1, {})} | custom-call | flops 5242880 | bytes 4194304 | tf_op jit(solution)/shard_map/add_last/pallas_call | solution.py:366
  (65 shorter events, 32.5 us)
Async XLA Ops:
  0.0 123.5 %copy-start = (bf16[1024,256]{1,0:T(8,128)(2,1)S(1)}, bf16[1024,256]{1,0:T(8,128)(2,1)}, u32[]{:S(2)}) copy-start(bf16[1024,256]{1,0:T(8,128)(2,1)} %param.11) | copy-start | bytes 1572868
  0.0 109.5 %collective-permute-start.1 = (f32[1024,512]{1,0:T(8,128)}, f32[1024,512]{1,0:T(8,128)}, u32[]{:S(2)}, u32[]{:S(2)}) collective-permute-start(f32[1024,512]{1,0:T(8,128)} %refs_0_.7), channel_id=1, source_target_pairs={{3,4},{4,3},{7,8},{8,7},{11,12},{12,11},{15,16},{16,15},{19,20},{2... | collective-permute-start | bytes 6291464 | tf_op jit(solution)/shard_map/ppermute | solution.py:410
  9.5 103.0 %collective-permute-start = (f32[1024,512]{1,0:T(8,128)}, f32[1024,512]{1,0:T(8,128)}, u32[]{:S(2)}, u32[]{:S(2)}) collective-permute-start(f32[1024,512]{1,0:T(8,128)} %refs_0_.7), channel_id=1, source_target_pairs={{0,1},{1,0},{2,3},{3,2},{4,5},{5,4},{6,7},{7,6},{8,9},{9,8},{10,11... | collective-permute-start | bytes 6291464 | tf_op jit(solution)/shard_map/ppermute | solution.py:411
  26.2 11.8 %collective-permute-start.5 = (f32[64,512]{1,0:T(8,128)S(1)}, f32[64,512]{1,0:T(8,128)S(1)}, u32[]{:S(2)}, u32[]{:S(2)}) collective-permute-start(f32[64,512]{1,0:T(8,128)S(1)} %get-tuple-element.17), channel_id=1, source_target_pairs={{0,128},{32,160},{64,192},{96,224},{128,0},{160,32},{192,64},{224,... | collective-permute-start | bytes 393224 | tf_op jit(solution)/shard_map/ppermute | solution.py:430
  29.3 9.4 %collective-permute-start.7 = (f32[64,512]{1,0:T(8,128)}, f32[64,512]{1,0:T(8,128)S(1)}, u32[]{:S(2)}, u32[]{:S(2)}) collective-permute-start(f32[64,512]{1,0:T(8,128)} %get-tuple-element.18), channel_id=1, source_target_pairs={{0,384},{32,416},{64,448},{96,480},{128,256},{160,288},{192,320},{... | collective-permute-start | bytes 393224 | tf_op jit(solution)/shard_map/ppermute | solution.py:430
  31.2 9.3 %collective-permute-start.6 = (f32[64,512]{1,0:T(8,128)}, f32[64,512]{1,0:T(8,128)}, u32[]{:S(2)}, u32[]{:S(2)}) collective-permute-start(f32[64,512]{1,0:T(8,128)} %get-tuple-element.19), channel_id=1, source_target_pairs={{0,256},{32,288},{64,320},{96,352},{128,384},{160,416},{192,448},{... | collective-permute-start | bytes 393224 | tf_op jit(solution)/shard_map/ppermute | solution.py:430
  37.9 64.2 %collective-permute-start.2 = (f32[256,512]{1,0:T(8,128)}, f32[256,512]{1,0:T(8,128)S(1)}, u32[]{:S(2)}, u32[]{:S(2)}) collective-permute-start(f32[256,512]{1,0:T(8,128)} %constant_dynamic-slice_fusion.2), channel_id=1, source_target_pairs={{1,2},{2,1},{5,6},{6,5},{9,10},{10,9},{13,14},{14,13},{17,18},{18,... | collective-permute-start | bytes 1572872 | tf_op jit(solution)/shard_map/ppermute | solution.py:415
  41.6 18.2 %collective-permute-start.8 = (f32[16,512]{1,0:T(8,128)S(1)}, f32[16,512]{1,0:T(8,128)S(1)}, u32[]{:S(2)}, u32[]{:S(2)}) collective-permute-start(f32[16,512]{1,0:T(8,128)S(1)} %get-tuple-element.20), channel_id=1, source_target_pairs={{0,32},{32,0},{64,96},{96,64},{128,160},{160,128},{192,224},{224,1... | collective-permute-start | bytes 98312 | tf_op jit(solution)/shard_map/ppermute | solution.py:430
  44.1 25.2 %collective-permute-start.10 = (f32[16,512]{1,0:T(8,128)S(1)}, f32[16,512]{1,0:T(8,128)S(1)}, u32[]{:S(2)}, u32[]{:S(2)}) collective-permute-start(f32[16,512]{1,0:T(8,128)S(1)} %get-tuple-element.21), channel_id=1, source_target_pairs={{0,96},{32,64},{64,32},{96,0},{128,224},{160,192},{192,160},{224,1... | collective-permute-start | bytes 98312 | tf_op jit(solution)/shard_map/ppermute | solution.py:430
  59.8 46.5 %collective-permute-start.3 = (f32[256,512]{1,0:T(8,128)}, f32[256,512]{1,0:T(8,128)}, u32[]{:S(2)}, u32[]{:S(2)}) collective-permute-start(f32[256,512]{1,0:T(8,128)} %constant_dynamic-slice_fusion.1), channel_id=1, source_target_pairs={{1,2},{2,1},{5,6},{6,5},{9,10},{10,9},{13,14},{14,13},{17,18},{18,... | collective-permute-start | bytes 1572872 | tf_op jit(solution)/shard_map/ppermute | solution.py:415
  69.3 7.0 %collective-permute-start.9 = (f32[16,512]{1,0:T(8,128)S(1)}, f32[16,512]{1,0:T(8,128)S(1)}, u32[]{:S(2)}, u32[]{:S(2)}) collective-permute-start(f32[16,512]{1,0:T(8,128)S(1)} %get-tuple-element.22), channel_id=1, source_target_pairs={{0,64},{32,96},{64,0},{96,32},{128,192},{160,224},{192,128},{224,1... | collective-permute-start | bytes 98312 | tf_op jit(solution)/shard_map/ppermute | solution.py:430
  76.4 11.3 %collective-permute-start.12 = (f32[16,512]{1,0:T(8,128)S(1)}, f32[16,512]{1,0:T(8,128)S(1)}, u32[]{:S(2)}, u32[]{:S(2)}) collective-permute-start(f32[16,512]{1,0:T(8,128)S(1)} %fusion.6.refs_0_), channel_id=1, source_target_pairs={{1,2},{2,1},{3,4},{4,3},{5,6},{6,5},{7,8},{8,7},{9,10},{10,9},{11,... | collective-permute-start | bytes 98312 | tf_op jit(solution)/shard_map/ppermute | solution.py:447
  87.7 13.0 %collective-permute-start.11 = (f32[16,512]{1,0:T(8,128)S(1)}, f32[16,512]{1,0:T(8,128)S(1)}, u32[]{:S(2)}, u32[]{:S(2)}) collective-permute-start(f32[16,512]{1,0:T(8,128)S(1)} %fusion.6.refs_0_), channel_id=1, source_target_pairs={{0,1},{1,0},{2,3},{3,2},{4,5},{5,4},{6,7},{7,6},{8,9},{9,8},{10,11... | collective-permute-start | bytes 98312 | tf_op jit(solution)/shard_map/ppermute | solution.py:453
  100.6 60.7 %collective-permute-start.4 = (f32[512,512]{1,0:T(8,128)}, f32[512,512]{1,0:T(8,128)S(1)}, u32[]{:S(2)}, u32[]{:S(2)}) collective-permute-start(f32[512,512]{1,0:T(8,128)} %constant_dynamic-slice_fusion), channel_id=1, source_target_pairs={{1,2},{2,1},{5,6},{6,5},{9,10},{10,9},{13,14},{14,13},{17,18},{18,... | collective-permute-start | bytes 3145736 | tf_op jit(solution)/shard_map/ppermute | solution.py:415
  102.1 15.0 %collective-permute-start.15 = (f32[16,512]{1,0:T(8,128)S(1)}, f32[16,512]{1,0:T(8,128)S(1)}, u32[]{:S(2)}, u32[]{:S(2)}) collective-permute-start(f32[16,512]{1,0:T(8,128)S(1)} %move_cols.6), channel_id=1, source_target_pairs={{0,96},{32,64},{64,32},{96,0},{128,224},{160,192},{192,160},{224,1... | collective-permute-start | bytes 98312 | tf_op jit(solution)/shard_map/ppermute | solution.py:434
  106.3 10.7 %collective-permute-start.14 = (f32[16,512]{1,0:T(8,128)S(1)}, f32[16,512]{1,0:T(8,128)S(1)}, u32[]{:S(2)}, u32[]{:S(2)}) collective-permute-start(f32[16,512]{1,0:T(8,128)S(1)} %move_cols.6), channel_id=1, source_target_pairs={{0,64},{32,96},{64,0},{96,32},{128,192},{160,224},{192,128},{224,1... | collective-permute-start | bytes 98312 | tf_op jit(solution)/shard_map/ppermute | solution.py:434
  109.5 7.5 %collective-permute-start.13 = (f32[16,512]{1,0:T(8,128)S(1)}, f32[16,512]{1,0:T(8,128)S(1)}, u32[]{:S(2)}, u32[]{:S(2)}) collective-permute-start(f32[16,512]{1,0:T(8,128)S(1)} %move_cols.6), channel_id=1, source_target_pairs={{0,32},{32,0},{64,96},{96,64},{128,160},{160,128},{192,224},{224,1... | collective-permute-start | bytes 98312 | tf_op jit(solution)/shard_map/ppermute | solution.py:434
  117.1 38.5 %collective-permute-start.17 = (f32[64,512]{1,0:T(8,128)S(1)}, f32[64,512]{1,0:T(8,128)S(1)}, u32[]{:S(2)}, u32[]{:S(2)}) collective-permute-start(f32[64,512]{1,0:T(8,128)S(1)} %get-tuple-element.23), channel_id=1, source_target_pairs={{0,256},{32,288},{64,320},{96,352},{128,384},{160,416},{192,448},{... | collective-permute-start | bytes 393224 | tf_op jit(solution)/shard_map/ppermute | solution.py:434
  119.5 17.2 %collective-permute-start.16 = (f32[64,512]{1,0:T(8,128)S(1)}, f32[64,512]{1,0:T(8,128)S(1)}, u32[]{:S(2)}, u32[]{:S(2)}) collective-permute-start(f32[64,512]{1,0:T(8,128)S(1)} %get-tuple-element.23), channel_id=1, source_target_pairs={{0,128},{32,160},{64,192},{96,224},{128,0},{160,32},{192,64},{224,... | collective-permute-start | bytes 393224 | tf_op jit(solution)/shard_map/ppermute | solution.py:434
  124.0 35.5 %collective-permute-start.18 = (f32[64,512]{1,0:T(8,128)S(1)}, f32[64,512]{1,0:T(8,128)S(1)}, u32[]{:S(2)}, u32[]{:S(2)}) collective-permute-start(f32[64,512]{1,0:T(8,128)S(1)} %get-tuple-element.23), channel_id=1, source_target_pairs={{0,384},{32,416},{64,448},{96,480},{128,256},{160,288},{192,320},{... | collective-permute-start | bytes 393224 | tf_op jit(solution)/shard_map/ppermute | solution.py:434
  127.4 66.4 %collective-permute-start.20 = (f32[512,512]{1,0:T(8,128)S(1)}, f32[512,512]{1,0:T(8,128)S(1)}, u32[]{:S(2)}, u32[]{:S(2)}) collective-permute-start(f32[512,512]{1,0:T(8,128)S(1)} %move_cols.5.refs_1_), channel_id=1, source_target_pairs={{33,65},{34,66},{37,69},{38,70},{41,73},{42,74},{45,77},{46,78},{4... | collective-permute-start | bytes 3145736 | tf_op jit(solution)/shard_map/ppermute | solution.py:445
  136.7 57.1 %collective-permute-start.19 = (f32[512,512]{1,0:T(8,128)S(1)}, f32[512,512]{1,0:T(8,128)S(1)}, u32[]{:S(2)}, u32[]{:S(2)}) collective-permute-start(f32[512,512]{1,0:T(8,128)S(1)} %move_cols.8), channel_id=1, source_target_pairs={{32,64},{35,67},{36,68},{39,71},{40,72},{43,75},{44,76},{47,79},{4... | collective-permute-start | bytes 3145736 | tf_op jit(solution)/shard_map/ppermute | solution.py:445
  155.6 43.7 %collective-permute-start.21 = (f32[512,512]{1,0:T(8,128)S(1)}, f32[512,512]{1,0:T(8,128)S(1)}, u32[]{:S(2)}, u32[]{:S(2)}) collective-permute-start(f32[512,512]{1,0:T(8,128)S(1)} %move_cols.9), channel_id=1, source_target_pairs={{0,32},{3,35},{4,36},{7,39},{8,40},{11,43},{12,44},{15,47},{16,48}... | collective-permute-start | bytes 3145736 | tf_op jit(solution)/shard_map/ppermute | solution.py:445
  165.7 33.6 %collective-permute-start.22 = (f32[512,512]{1,0:T(8,128)S(1)}, f32[512,512]{1,0:T(8,128)S(1)}, u32[]{:S(2)}, u32[]{:S(2)}) collective-permute-start(f32[512,512]{1,0:T(8,128)S(1)} %move_cols.7.refs_2_), channel_id=1, source_target_pairs={{1,33},{2,34},{5,37},{6,38},{9,41},{10,42},{13,45},{14,46},{17,49}... | collective-permute-start | bytes 3145736 | tf_op jit(solution)/shard_map/ppermute | solution.py:445
  (6 other events, 156.7 us)

commit v6 on v5

--- a/solution.py
+++ b/solution.py
@@ -454,13 +454,15 @@
     piece = move_cols(place, (total, 0), (piece_near, 0), [(piece_far, 0)], col_weights, each)
     observed = all_of(piece, Z_BITS)
     halo_first = [swap_rows(early_first, 1, (0, 3))]
-    halo_second = [swap_rows(early_second, 0, (0, 3))]
     far_second = far_part(second * half, half, late)
 
     moved_first = move("first", far_begin, far_first)
     halo_first.append(swap_rows(moved_first, 1, (1, 2)))
 
-    observed = jnp.concatenate([after(observed[0], moved_first), *observed[1:]])
+    moved_second = move("second", far_second)
+    halo_second = [swap_rows(moved_second, 0, (1, 2))]
+
+    observed = jnp.concatenate([after(observed[0], moved_second), *observed[1:]])
     observed = jnp.concatenate(all_of(observed, X_BITS))
     index = jnp.arange(gain.shape[1], dtype=jnp.int32)
     reorder = (index[:, None] ^ (row_at * each)) == index[None, :]
@@ -469,8 +471,7 @@
     ordered_gain = ordered_gain * ordered_scale[None, :]
     update = jnp.dot(ordered_gain, observed, precision=HIGH, preferred_element_type=jnp.float32)
 
-    moved_second = move("second", after(far_second, update))
-    halo_second.append(swap_rows(moved_second, 0, (1, 2)))
+    halo_second.append(swap_rows(early_second, 0, (0, 3)))
 
     result = move_rows(place, moved_first, moved_second, halo_first, update, down_weights)
     return add_last(place, result, halo_second, down_weights)

time: 204 us -> 191 us (0.936)
  the two profiles are of different devices: /device:TPU:100 before, /device:TPU:488 now
where the time goes in v6:
time: 191 us; the launch traced here: 190 us
  starting transfers between devices  81.8 us (43%)
  waiting for transfers between devices  65.5 us (34%)
  Pallas kernels  30.2 us (16%)
  matrix products  6.27 us (3%)
  local copies, waits for them, and re-layouts  3.46 us (2%)
    ppermute x6, waiting for transfers between devices, sum_over(): total = total + lax.ppermute(piece, 'row', across(bit))  33 us
    ppermute x6, waiting for transfers between devices, all_of(): return [value] + [lax.ppermute(value, 'row', across(bit)) for bit in bits]  30.5 us
    ppermute x6, starting transfers between devices, all_of(): return [value] + [lax.ppermute(value, 'row', across(bit)) for bit in bits]  30.1 us
    ppermute x6, starting transfers between devices, sum_over(): total = total + lax.ppermute(piece, 'row', across(bit))  17.7 us
    ppermute x3, starting transfers between devices, far_part(): return lax.ppermute(block, 'col', straight)  17.1 us
    pallas_call x5, Pallas kernels, move_cols(): pl.pallas_call(kernel, out_shape=jax.ShapeDtypeStruct((rows, cols), jnp.f...  12.7 us
    pallas_call x1, Pallas kernels, prepare(): pl.pallas_call(kernel, out_shape=(jax.ShapeDtypeStruct((obs_count, rows),...  8.65 us
    ppermute x4, starting transfers between devices, swap_rows(): return lax.ppermute(block, ('row', 'col'), row_swap(odd, kinds))  5.83 us
  transfers between devices with their start and end apart: 23, of which 7 were waited for; matrix products, arithmetic and copies ran while one was open for 6% of the time, Pallas kernels for 14%

profile of v6, /device:TPU:488, one launch (start us, length us, event | category | flops | bytes accessed | tf_op | source)
XLA Modules:
  0.0 189.6 jit_solution(729561312327949897)
XLA Ops:
  4.6 8.7 %prepare.1 = (f32[256,1024]{1,0:T(8,128)}, f32[8,1024]{1,0:T(8,128)}, f32[1536,8]{1,0:T(8,128)}) custom-call(s32[3]{0:T(128)} %pad_add_fusion.1.refs_0_, s32[2,16384]{1,0:T(2,128)} %refs_1_.1, f32[2,16384]{1,0:T(2,128)} %refs_2_.1, s32[256,128]{1,0:T(8,128)} %refs_6_.1, s32[256,128]{1,0:T(8,128)} %refs_6_.1, s32[256,128]{1,0:T(8,128)} %refs_6_.1, ...), custom_call_target="tpu_custom_call" | custom-call | flops 134217728 | bytes 2097152 | tf_op jit(solution)/shard_map/prepare/pallas_call | solution.py:108
  13.3 4.0 %fusion.9 = f32[256,512]{1,0:T(8,128)S(1)} fusion(f32[256,1024]{1,0:T(8,128)} %get-tuple-element.10, f32[1024,512]{1,0:T(8,128)} %refs_0_.7), kind=kOutput, calls=%fused_computation.30 | convolution fusion | flops 1610612736 | bytes 3670016 | tf_op jit(solution)/shard_map/dot_general | solution.py:423
  18.1 3.4 %collective-permute-start.7 = (f32[64,512]{1,0:T(8,128)}, f32[64,512]{1,0:T(8,128)S(1)}, u32[]{:S(2)}, u32[]{:S(2)}) collective-permute-start(f32[64,512]{1,0:T(8,128)} %get-tuple-element.15), channel_id=1, source_target_pairs={{0,128},{32,160},{64,192},{96,224},{128,0},{160,32},{192,64},{224,... | collective-permute-start | bytes 393224 | tf_op jit(solution)/shard_map/ppermute | solution.py:430
  21.5 4.0 %collective-permute-start.9 = (f32[64,512]{1,0:T(8,128)}, f32[64,512]{1,0:T(8,128)S(1)}, u32[]{:S(2)}, u32[]{:S(2)}) collective-permute-start(f32[64,512]{1,0:T(8,128)} %get-tuple-element.16), channel_id=1, source_target_pairs={{0,384},{32,416},{64,448},{96,480},{128,256},{160,288},{192,320},{... | collective-permute-start | bytes 393224 | tf_op jit(solution)/shard_map/ppermute | solution.py:430
  25.5 2.6 %collective-permute-start.8 = (f32[64,512]{1,0:T(8,128)}, f32[64,512]{1,0:T(8,128)}, u32[]{:S(2)}, u32[]{:S(2)}) collective-permute-start(f32[64,512]{1,0:T(8,128)} %get-tuple-element.17), channel_id=1, source_target_pairs={{0,256},{32,288},{64,320},{96,352},{128,384},{160,416},{192,448},{... | collective-permute-start | bytes 393224 | tf_op jit(solution)/shard_map/ppermute | solution.py:430
  29.1 7.7 %collective-permute-start.4 = (f32[512,512]{1,0:T(8,128)}, f32[512,512]{1,0:T(8,128)}, u32[]{:S(2)}, u32[]{:S(2)}) collective-permute-start(f32[512,512]{1,0:T(8,128)} %constant_dynamic-slice_fusion), channel_id=1, source_target_pairs={{1,2},{2,1},{5,6},{6,5},{9,10},{10,9},{13,14},{14,13},{17,18},{18,... | collective-permute-start | bytes 3145736 | tf_op jit(solution)/shard_map/ppermute | solution.py:415
  38.5 2.5 %collective-permute-start.10 = (f32[16,512]{1,0:T(8,128)S(1)}, f32[16,512]{1,0:T(8,128)S(1)}, u32[]{:S(2)}, u32[]{:S(2)}) collective-permute-start(f32[16,512]{1,0:T(8,128)S(1)} %get-tuple-element.18), channel_id=1, source_target_pairs={{0,32},{32,0},{64,96},{96,64},{128,160},{160,128},{192,224},{224,1... | collective-permute-start | bytes 98312 | tf_op jit(solution)/shard_map/ppermute | solution.py:430
  41.0 3.4 %collective-permute-start.12 = (f32[16,512]{1,0:T(8,128)S(1)}, f32[16,512]{1,0:T(8,128)S(1)}, u32[]{:S(2)}, u32[]{:S(2)}) collective-permute-start(f32[16,512]{1,0:T(8,128)S(1)} %get-tuple-element.19), channel_id=1, source_target_pairs={{0,96},{32,64},{64,32},{96,0},{128,224},{160,192},{192,160},{224,1... | collective-permute-start | bytes 98312 | tf_op jit(solution)/shard_map/ppermute | solution.py:430
  44.3 29.1 %collective-permute-done.10 = f32[16,512]{1,0:T(8,128)S(1)} collective-permute-done((f32[16,512]{1,0:T(8,128)S(1)}, f32[16,512]{1,0:T(8,128)S(1)}, u32[]{:S(2)}, u32[]{:S(2)}) %collective-permute-start.10) | collective-permute-done | bytes 32800 | tf_op jit(solution)/shard_map/ppermute | solution.py:430
  76.2 3.9 %collective-permute-done.11 = f32[16,512]{1,0:T(8,128)S(1)} collective-permute-done((f32[16,512]{1,0:T(8,128)S(1)}, f32[16,512]{1,0:T(8,128)S(1)}, u32[]{:S(2)}, u32[]{:S(2)}) %collective-permute-start.11) | collective-permute-done | bytes 32800 | tf_op jit(solution)/shard_map/ppermute | solution.py:430
  80.1 5.1 %collective-permute-start.14 = (f32[16,512]{1,0:T(8,128)S(1)}, f32[16,512]{1,0:T(8,128)S(1)}, u32[]{:S(2)}, u32[]{:S(2)}) collective-permute-start(f32[16,512]{1,0:T(8,128)S(1)} %fusion.6.refs_0_), channel_id=1, source_target_pairs={{1,2},{2,1},{3,4},{4,3},{5,6},{6,5},{7,8},{8,7},{9,10},{10,9},{11,... | collective-permute-start | bytes 98312 | tf_op jit(solution)/shard_map/ppermute | solution.py:447
  89.3 5.2 %collective-permute-start.2 = (f32[256,512]{1,0:T(8,128)}, f32[256,512]{1,0:T(8,128)S(1)}, u32[]{:S(2)}, u32[]{:S(2)}) collective-permute-start(f32[256,512]{1,0:T(8,128)} %constant_dynamic-slice_fusion.2), channel_id=1, source_target_pairs={{1,2},{2,1},{5,6},{6,5},{9,10},{10,9},{13,14},{14,13},{17,18},{18,... | collective-permute-start | bytes 1572872 | tf_op jit(solution)/shard_map/ppermute | solution.py:415
  94.5 4.2 %collective-permute-start.3 = (f32[256,512]{1,0:T(8,128)S(1)}, f32[256,512]{1,0:T(8,128)S(1)}, u32[]{:S(2)}, u32[]{:S(2)}) collective-permute-start(f32[256,512]{1,0:T(8,128)S(1)} %constant_dynamic-slice_fusion.1), channel_id=1, source_target_pairs={{1,2},{2,1},{5,6},{6,5},{9,10},{10,9},{13,14},{14,13},{17,18},{18,... | collective-permute-start | bytes 1572872 | tf_op jit(solution)/shard_map/ppermute | solution.py:415
  99.6 4.2 %collective-permute-start.17 = (f32[16,512]{1,0:T(8,128)S(1)}, f32[16,512]{1,0:T(8,128)S(1)}, u32[]{:S(2)}, u32[]{:S(2)}) collective-permute-start(f32[16,512]{1,0:T(8,128)S(1)} %move_cols.8), channel_id=1, source_target_pairs={{0,96},{32,64},{64,32},{96,0},{128,224},{160,192},{192,160},{224,1... | collective-permute-start | bytes 98312 | tf_op jit(solution)/shard_map/ppermute | solution.py:434
  103.8 3.5 %collective-permute-start.16 = (f32[16,512]{1,0:T(8,128)S(1)}, f32[16,512]{1,0:T(8,128)S(1)}, u32[]{:S(2)}, u32[]{:S(2)}) collective-permute-start(f32[16,512]{1,0:T(8,128)S(1)} %move_cols.8), channel_id=1, source_target_pairs={{0,64},{32,96},{64,0},{96,32},{128,192},{160,224},{192,128},{224,1... | collective-permute-start | bytes 98312 | tf_op jit(solution)/shard_map/ppermute | solution.py:434
  107.3 2.4 %collective-permute-start.15 = (f32[16,512]{1,0:T(8,128)S(1)}, f32[16,512]{1,0:T(8,128)S(1)}, u32[]{:S(2)}, u32[]{:S(2)}) collective-permute-start(f32[16,512]{1,0:T(8,128)S(1)} %move_cols.8), channel_id=1, source_target_pairs={{0,32},{32,0},{64,96},{96,64},{128,160},{160,128},{192,224},{224,1... | collective-permute-start | bytes 98312 | tf_op jit(solution)/shard_map/ppermute | solution.py:434
  109.7 4.5 %move_cols.6.refs_2_ = f32[512,512]{1,0:T(8,128)S(1)} custom-call(s32[4]{0:T(128)S(1)} %pad_add_fusion.at_ref.refs_0_, f32[1024,512]{1,0:T(8,128)S(1)} %copy-done.1, f32[1024,512]{1,0:T(8,128)} %collective-permute-done.refs_1_, f32[1024,512]{1,0:T(8,128)} %collective-permute-done.1.refs_2_, f32[512,512]{1,0:T(8,128)} %collective-permute-done.4.refs_3_, ...), custom_call_target="tpu_custom_call" | custom-call | flops 7077888 | bytes 4194304 | tf_op jit(solution)/shard_map/move_cols/pallas_call | solution.py:204
  114.3 7.6 %collective-permute-done.15 = f32[16,512]{1,0:T(8,128)S(1)} collective-permute-done((f32[16,512]{1,0:T(8,128)S(1)}, f32[16,512]{1,0:T(8,128)S(1)}, u32[]{:S(2)}, u32[]{:S(2)}) %collective-permute-start.15) | collective-permute-done | bytes 32800 | tf_op jit(solution)/shard_map/ppermute | solution.py:434
  125.3 16.2 %collective-permute-start.19 = (f32[64,512]{1,0:T(8,128)S(1)}, f32[64,512]{1,0:T(8,128)S(1)}, u32[]{:S(2)}, u32[]{:S(2)}) collective-permute-start(f32[64,512]{1,0:T(8,128)S(1)} %get-tuple-element.21), channel_id=1, source_target_pairs={{0,256},{32,288},{64,320},{96,352},{128,384},{160,416},{192,448},{... | collective-permute-start | bytes 393224 | tf_op jit(solution)/shard_map/ppermute | solution.py:434
  146.3 4.3 %move_cols.5.refs_1_ = f32[512,512]{1,0:T(8,128)S(1)} custom-call(s32[4]{0:T(128)S(1)} %pad_add_fusion.at_ref.refs_0_, f32[1024,512]{1,0:T(8,128)S(1)} %copy-done.1, f32[1024,512]{1,0:T(8,128)} %collective-permute-done.refs_1_, f32[1024,512]{1,0:T(8,128)} %collective-permute-done.1.refs_2_, f32[256,512]{1,0:T(8,128)S(1)} %collective-permute-done.2.refs_3_, ...), custom_call_target="tpu_custom_call" | custom-call | flops 7077888 | bytes 4194304 | tf_op jit(solution)/shard_map/move_cols/pallas_call | solution.py:204
  155.1 15.7 %collective-permute-done.18 = f32[64,512]{1,0:T(8,128)S(1)} collective-permute-done((f32[64,512]{1,0:T(8,128)S(1)}, f32[64,512]{1,0:T(8,128)S(1)}, u32[]{:S(2)}, u32[]{:S(2)}) %collective-permute-start.18) | collective-permute-done | bytes 131104 | tf_op jit(solution)/shard_map/ppermute | solution.py:434
  172.8 6.1 %collective-permute-done.20 = f32[64,512]{1,0:T(8,128)S(1)} collective-permute-done((f32[64,512]{1,0:T(8,128)S(1)}, f32[64,512]{1,0:T(8,128)S(1)}, u32[]{:S(2)}, u32[]{:S(2)}) %collective-permute-start.20) | collective-permute-done | bytes 131104 | tf_op jit(solution)/shard_map/ppermute | solution.py:434
  180.8 5.4 %move_rows.1.refs_1_ = f32[1024,512]{1,0:T(8,128)} custom-call(s32[4]{0:T(128)S(1)} %pad_add_fusion.at_ref.refs_0_, f32[512,512]{1,0:T(8,128)S(1)} %move_cols.5.refs_1_, f32[512,512]{1,0:T(8,128)S(1)} %move_cols.6.refs_2_, f32[512,512]{1,0:T(8,128)S(1)} %collective-permute-done.5.refs_3_, f32[512,512]{1,0:T(8,128)S(1)} %collective-permute-done.6.refs_4_, ...), custom_call_target="tpu_custom_call" | custom-call | flops 12582912 | bytes 8388608 | tf_op jit(solution)/shard_map/move_rows/pallas_call | solution.py:302
  186.2 3.4 %add_last.1 = f32[1024,512]{1,0:T(8,128)} custom-call(s32[4]{0:T(128)S(1)} %pad_add_fusion.at_ref.refs_0_, f32[1024,512]{1,0:T(8,128)} %move_rows.1.refs_1_, f32[512,512]{1,0:T(8,128)S(1)} %collective-permute-done.21.refs_2_, f32[512,512]{1,0:T(8,128)S(1)} %collective-permute-done.22.refs_3_, f32[1536,8]{1,0:T(8,128)S(1)} %copy-done.2), custom_call_target="tpu_custom_call", output_to_operand_aliasing={{}: (1, {})} | custom-call | flops 5242880 | bytes 4194304 | tf_op jit(solution)/shard_map/add_last/pallas_call | solution.py:366
  (63 shorter events, 32.1 us)
Async XLA Ops:
  0.0 154.7 %copy-start = (bf16[1024,256]{1,0:T(8,128)(2,1)S(1)}, bf16[1024,256]{1,0:T(8,128)(2,1)}, u32[]{:S(2)}) copy-start(bf16[1024,256]{1,0:T(8,128)(2,1)} %param.11) | copy-start | bytes 1572868
  0.0 103.7 %collective-permute-start.1 = (f32[1024,512]{1,0:T(8,128)}, f32[1024,512]{1,0:T(8,128)}, u32[]{:S(2)}, u32[]{:S(2)}) collective-permute-start(f32[1024,512]{1,0:T(8,128)} %refs_0_.7), channel_id=1, source_target_pairs={{3,4},{4,3},{7,8},{8,7},{11,12},{12,11},{15,16},{16,15},{19,20},{2... | collective-permute-start | bytes 6291464 | tf_op jit(solution)/shard_map/ppermute | solution.py:410
  2.1 105.1 %collective-permute-start = (f32[1024,512]{1,0:T(8,128)}, f32[1024,512]{1,0:T(8,128)}, u32[]{:S(2)}, u32[]{:S(2)}) collective-permute-start(f32[1024,512]{1,0:T(8,128)} %refs_0_.7), channel_id=1, source_target_pairs={{0,1},{1,0},{2,3},{3,2},{4,5},{5,4},{6,7},{7,6},{8,9},{9,8},{10,11... | collective-permute-start | bytes 6291464 | tf_op jit(solution)/shard_map/ppermute | solution.py:411
  18.1 11.0 %collective-permute-start.7 = (f32[64,512]{1,0:T(8,128)}, f32[64,512]{1,0:T(8,128)S(1)}, u32[]{:S(2)}, u32[]{:S(2)}) collective-permute-start(f32[64,512]{1,0:T(8,128)} %get-tuple-element.15), channel_id=1, source_target_pairs={{0,128},{32,160},{64,192},{96,224},{128,0},{160,32},{192,64},{224,... | collective-permute-start | bytes 393224 | tf_op jit(solution)/shard_map/ppermute | solution.py:430
  21.5 15.3 %collective-permute-start.9 = (f32[64,512]{1,0:T(8,128)}, f32[64,512]{1,0:T(8,128)S(1)}, u32[]{:S(2)}, u32[]{:S(2)}) collective-permute-start(f32[64,512]{1,0:T(8,128)} %get-tuple-element.16), channel_id=1, source_target_pairs={{0,384},{32,416},{64,448},{96,480},{128,256},{160,288},{192,320},{... | collective-permute-start | bytes 393224 | tf_op jit(solution)/shard_map/ppermute | solution.py:430
  25.5 12.0 %collective-permute-start.8 = (f32[64,512]{1,0:T(8,128)}, f32[64,512]{1,0:T(8,128)}, u32[]{:S(2)}, u32[]{:S(2)}) collective-permute-start(f32[64,512]{1,0:T(8,128)} %get-tuple-element.17), channel_id=1, source_target_pairs={{0,256},{32,288},{64,320},{96,352},{128,384},{160,416},{192,448},{... | collective-permute-start | bytes 393224 | tf_op jit(solution)/shard_map/ppermute | solution.py:430
  29.1 70.4 %collective-permute-start.4 = (f32[512,512]{1,0:T(8,128)}, f32[512,512]{1,0:T(8,128)}, u32[]{:S(2)}, u32[]{:S(2)}) collective-permute-start(f32[512,512]{1,0:T(8,128)} %constant_dynamic-slice_fusion), channel_id=1, source_target_pairs={{1,2},{2,1},{5,6},{6,5},{9,10},{10,9},{13,14},{14,13},{17,18},{18,... | collective-permute-start | bytes 3145736 | tf_op jit(solution)/shard_map/ppermute | solution.py:415
  38.5 34.9 %collective-permute-start.10 = (f32[16,512]{1,0:T(8,128)S(1)}, f32[16,512]{1,0:T(8,128)S(1)}, u32[]{:S(2)}, u32[]{:S(2)}) collective-permute-start(f32[16,512]{1,0:T(8,128)S(1)} %get-tuple-element.18), channel_id=1, source_target_pairs={{0,32},{32,0},{64,96},{96,64},{128,160},{160,128},{192,224},{224,1... | collective-permute-start | bytes 98312 | tf_op jit(solution)/shard_map/ppermute | solution.py:430
  41.0 35.2 %collective-permute-start.12 = (f32[16,512]{1,0:T(8,128)S(1)}, f32[16,512]{1,0:T(8,128)S(1)}, u32[]{:S(2)}, u32[]{:S(2)}) collective-permute-start(f32[16,512]{1,0:T(8,128)S(1)} %get-tuple-element.19), channel_id=1, source_target_pairs={{0,96},{32,64},{64,32},{96,0},{128,224},{160,192},{192,160},{224,1... | collective-permute-start | bytes 98312 | tf_op jit(solution)/shard_map/ppermute | solution.py:430
  73.4 6.7 %collective-permute-start.11 = (f32[16,512]{1,0:T(8,128)S(1)}, f32[16,512]{1,0:T(8,128)S(1)}, u32[]{:S(2)}, u32[]{:S(2)}) collective-permute-start(f32[16,512]{1,0:T(8,128)S(1)} %get-tuple-element.20), channel_id=1, source_target_pairs={{0,64},{32,96},{64,0},{96,32},{128,192},{160,224},{192,128},{224,1... | collective-permute-start | bytes 98312 | tf_op jit(solution)/shard_map/ppermute | solution.py:430
  80.1 9.1 %collective-permute-start.14 = (f32[16,512]{1,0:T(8,128)S(1)}, f32[16,512]{1,0:T(8,128)S(1)}, u32[]{:S(2)}, u32[]{:S(2)}) collective-permute-start(f32[16,512]{1,0:T(8,128)S(1)} %fusion.6.refs_0_), channel_id=1, source_target_pairs={{1,2},{2,1},{3,4},{4,3},{5,6},{6,5},{7,8},{8,7},{9,10},{10,9},{11,... | collective-permute-start | bytes 98312 | tf_op jit(solution)/shard_map/ppermute | solution.py:447
  85.3 9.2 %collective-permute-start.13 = (f32[16,512]{1,0:T(8,128)S(1)}, f32[16,512]{1,0:T(8,128)S(1)}, u32[]{:S(2)}, u32[]{:S(2)}) collective-permute-start(f32[16,512]{1,0:T(8,128)S(1)} %fusion.6.refs_0_), channel_id=1, source_target_pairs={{0,1},{1,0},{2,3},{3,2},{4,5},{5,4},{6,7},{7,6},{8,9},{9,8},{10,11... | collective-permute-start | bytes 98312 | tf_op jit(solution)/shard_map/ppermute | solution.py:453
  89.3 56.2 %collective-permute-start.2 = (f32[256,512]{1,0:T(8,128)}, f32[256,512]{1,0:T(8,128)S(1)}, u32[]{:S(2)}, u32[]{:S(2)}) collective-permute-start(f32[256,512]{1,0:T(8,128)} %constant_dynamic-slice_fusion.2), channel_id=1, source_target_pairs={{1,2},{2,1},{5,6},{6,5},{9,10},{10,9},{13,14},{14,13},{17,18},{18,... | collective-permute-start | bytes 1572872 | tf_op jit(solution)/shard_map/ppermute | solution.py:415
  94.5 51.8 %collective-permute-start.3 = (f32[256,512]{1,0:T(8,128)S(1)}, f32[256,512]{1,0:T(8,128)S(1)}, u32[]{:S(2)}, u32[]{:S(2)}) collective-permute-start(f32[256,512]{1,0:T(8,128)S(1)} %constant_dynamic-slice_fusion.1), channel_id=1, source_target_pairs={{1,2},{2,1},{5,6},{6,5},{9,10},{10,9},{13,14},{14,13},{17,18},{18,... | collective-permute-start | bytes 1572872 | tf_op jit(solution)/shard_map/ppermute | solution.py:415
  99.6 25.8 %collective-permute-start.17 = (f32[16,512]{1,0:T(8,128)S(1)}, f32[16,512]{1,0:T(8,128)S(1)}, u32[]{:S(2)}, u32[]{:S(2)}) collective-permute-start(f32[16,512]{1,0:T(8,128)S(1)} %move_cols.8), channel_id=1, source_target_pairs={{0,96},{32,64},{64,32},{96,0},{128,224},{160,192},{192,160},{224,1... | collective-permute-start | bytes 98312 | tf_op jit(solution)/shard_map/ppermute | solution.py:434
  103.8 21.6 %collective-permute-start.16 = (f32[16,512]{1,0:T(8,128)S(1)}, f32[16,512]{1,0:T(8,128)S(1)}, u32[]{:S(2)}, u32[]{:S(2)}) collective-permute-start(f32[16,512]{1,0:T(8,128)S(1)} %move_cols.8), channel_id=1, source_target_pairs={{0,64},{32,96},{64,0},{96,32},{128,192},{160,224},{192,128},{224,1... | collective-permute-start | bytes 98312 | tf_op jit(solution)/shard_map/ppermute | solution.py:434
  107.3 14.6 %collective-permute-start.15 = (f32[16,512]{1,0:T(8,128)S(1)}, f32[16,512]{1,0:T(8,128)S(1)}, u32[]{:S(2)}, u32[]{:S(2)}) collective-permute-start(f32[16,512]{1,0:T(8,128)S(1)} %move_cols.8), channel_id=1, source_target_pairs={{0,32},{32,0},{64,96},{96,64},{128,160},{160,128},{192,224},{224,1... | collective-permute-start | bytes 98312 | tf_op jit(solution)/shard_map/ppermute | solution.py:434
  121.8 64.4 %collective-permute-start.21 = (f32[512,512]{1,0:T(8,128)S(1)}, f32[512,512]{1,0:T(8,128)S(1)}, u32[]{:S(2)}, u32[]{:S(2)}) collective-permute-start(f32[512,512]{1,0:T(8,128)S(1)} %move_cols.6.refs_2_), channel_id=1, source_target_pairs={{1,33},{2,34},{5,37},{6,38},{9,41},{10,42},{13,45},{14,46},{17,49}... | collective-permute-start | bytes 3145736 | tf_op jit(solution)/shard_map/ppermute | solution.py:445
  125.3 27.4 %collective-permute-start.19 = (f32[64,512]{1,0:T(8,128)S(1)}, f32[64,512]{1,0:T(8,128)S(1)}, u32[]{:S(2)}, u32[]{:S(2)}) collective-permute-start(f32[64,512]{1,0:T(8,128)S(1)} %get-tuple-element.21), channel_id=1, source_target_pairs={{0,256},{32,288},{64,320},{96,352},{128,384},{160,416},{192,448},{... | collective-permute-start | bytes 393224 | tf_op jit(solution)/shard_map/ppermute | solution.py:434
  143.1 37.7 %collective-permute-start.5 = (f32[512,512]{1,0:T(8,128)S(1)}, f32[512,512]{1,0:T(8,128)S(1)}, u32[]{:S(2)}, u32[]{:S(2)}) collective-permute-start(f32[512,512]{1,0:T(8,128)S(1)} %move_cols.7), channel_id=1, source_target_pairs={{32,64},{35,67},{36,68},{39,71},{40,72},{43,75},{44,76},{47,79},{4... | collective-permute-start | bytes 3145736 | tf_op jit(solution)/shard_map/ppermute | solution.py:445
  145.4 40.8 %collective-permute-start.22 = (f32[512,512]{1,0:T(8,128)S(1)}, f32[512,512]{1,0:T(8,128)S(1)}, u32[]{:S(2)}, u32[]{:S(2)}) collective-permute-start(f32[512,512]{1,0:T(8,128)S(1)} %move_cols.9), channel_id=1, source_target_pairs={{0,32},{3,35},{4,36},{7,39},{8,40},{11,43},{12,44},{15,47},{16,48}... | collective-permute-start | bytes 3145736 | tf_op jit(solution)/shard_map/ppermute | solution.py:445
  150.6 30.2 %collective-permute-start.6 = (f32[512,512]{1,0:T(8,128)S(1)}, f32[512,512]{1,0:T(8,128)S(1)}, u32[]{:S(2)}, u32[]{:S(2)}) collective-permute-start(f32[512,512]{1,0:T(8,128)S(1)} %move_cols.5.refs_1_), channel_id=1, source_target_pairs={{33,65},{34,66},{37,69},{38,70},{41,73},{42,74},{45,77},{46,78},{4... | collective-permute-start | bytes 3145736 | tf_op jit(solution)/shard_map/ppermute | solution.py:445
  152.8 18.1 %collective-permute-start.18 = (f32[64,512]{1,0:T(8,128)S(1)}, f32[64,512]{1,0:T(8,128)S(1)}, u32[]{:S(2)}, u32[]{:S(2)}) collective-permute-start(f32[64,512]{1,0:T(8,128)S(1)} %get-tuple-element.21), channel_id=1, source_target_pairs={{0,128},{32,160},{64,192},{96,224},{128,0},{160,32},{192,64},{224,... | collective-permute-start | bytes 393224 | tf_op jit(solution)/shard_map/ppermute | solution.py:434
  170.8 8.1 %collective-permute-start.20 = (f32[64,512]{1,0:T(8,128)S(1)}, f32[64,512]{1,0:T(8,128)S(1)}, u32[]{:S(2)}, u32[]{:S(2)}) collective-permute-start(f32[64,512]{1,0:T(8,128)S(1)} %get-tuple-element.21), channel_id=1, source_target_pairs={{0,384},{32,416},{64,448},{96,480},{128,256},{160,288},{192,320},{... | collective-permute-start | bytes 393224 | tf_op jit(solution)/shard_map/ppermute | solution.py:434
  (5 other events, 100.3 us)
